TPU v7x, 128 devices: a whole 4x4x4 slice. The times are simulated.
128 devices in a mesh: gx: 8 (over z, core), gy: 16 (over x, y).
Axes of the slice: x: 4, y: 4, z: 4, core: 2. Of those that a mesh axis runs over, the one named last changes fastest.
Arguments:
- partials: float32 [131072, 512], P(('gx', 'gy')), may hold values from -5 to 5
- partial_ids: int32 [128, 1024], replicated, may hold values from 0 to 127
- read_lists: int32 [128, 4096], replicated, may hold values from 0 to 127
- sources: int32 [128, 8192], P(('gx', 'gy')), may hold values from 0 to 4095
- targets: int32 [128, 8192], P(('gx', 'gy')), may hold values from 0 to 127
- kernels: float32 [8, 512, 512], replicated, may hold values from -0.03125 to 0.03125
Outputs:
- local_expansions: float32 [16384, 512], P(('gx', 'gy'))
All inputs are finite; a program needn't handle non-finite values.
Results may differ from a plain program's by a relative error of at most 0.0003.
Values sent between devices are 32-bit elements; how exact they have to be, the bound alone decides.
No kernel may reach another device: no remote copies, remote signals or barrier semaphores. Data moves between devices by JAX's collectives and lax.ppermute only.
A program may use at most 192 MiB of HBM per device.

v0:
```python
import functools

import jax
import jax.numpy as jnp
from jax import lax
from jax.experimental import pallas as pl
from jax.experimental.pallas import tpu as pltpu
from jax.sharding import PartitionSpec as P

AXES = ("gx", "gy")
RING = 4
CORES = 2
OCT = 128
PER = 32
DIRS = 8
WIDTH = 512
PLANE = RING * RING * CORES
BLOCK = CORES * RING * PER
HALF = RING // 2 * OCT
BF16 = jnp.bfloat16
F32 = jnp.float32
ANY = pl.BlockSpec(memory_space=pl.ANY)
SMEM = pl.BlockSpec(memory_space=pltpu.SMEM)
VMEM = pl.BlockSpec(memory_space=pltpu.VMEM)
PARAMS = pltpu.CompilerParams(vmem_limit_bytes=48 << 20)


def device_of(x, y, z, c):
    return ((z % RING) * CORES + c % CORES) * RING * RING + (x % RING) * RING + y % RING


def fetch(value, shift):
    pairs = []
    for z in range(RING):
        for c in range(CORES):
            for x in range(RING):
                for y in range(RING):
                    dx, dy, dz, dc = shift(c)
                    pairs.append((device_of(x + dx, y + dy, z + dz, c + dc), device_of(x, y, z, c)))
    return lax.ppermute(value, AXES, pairs)


def along_f(value, k):
    return fetch(value, lambda core: (k, 0, 0, 0) if core == 0 else (0, k, 0, 0))


def along_s(value, k):
    return fetch(value, lambda core: (0, k, 0, 0) if core == 0 else (k, 0, 0, 0))


def along_z(value, k):
    return fetch(value, lambda core: (0, 0, k, 0))


def across(value):
    return fetch(value, lambda core: (0, 0, 0, 1))


def parts(value):
    high = value.astype(BF16)
    return high, (value - high.astype(F32)).astype(BF16)


def count_kernel(row_ref, col_ref, out_ref, rest_hbm, flag_ref, rest_ref):
    reader = pl.program_id(0)
    inner = row_ref.shape[1]
    rows = lax.broadcasted_iota(jnp.int32, (RING // 2 * OCT, inner), 0)
    cols = lax.broadcasted_iota(jnp.int32, (2 * BLOCK, inner), 0)
    for d in range(DIRS):
        step = reader * DIRS + d
        row_hot = jnp.where(rows == row_ref[pl.ds(step, 1), :], 1.0, 0.0).astype(BF16)
        col_hot = jnp.where(cols == col_ref[pl.ds(step, 1), :], 1.0, 0.0).astype(BF16)
        counts = lax.dot_general(
            row_hot, col_hot, (((1,), (1,)), ((), ())), preferred_element_type=F32
        )
        rounded = counts.astype(BF16)
        for s in range(RING):
            i, j = s // 2 * OCT, s % 2 * BLOCK
            out_ref[s, 0, d * OCT : (d + 1) * OCT, :] = rounded[i : i + OCT, j : j + BLOCK]
        large = jnp.max(counts) > 256.0
        flag_ref[step] = large.astype(jnp.int32)

        @pl.when(large)
        def _():
            rest = (counts - rounded.astype(F32)).astype(BF16)
            for s in range(RING):
                i, j = s // 2 * OCT, s % 2 * BLOCK
                rest_ref[s] = rest[i : i + OCT, j : j + BLOCK]
            pltpu.sync_copy(rest_ref, rest_hbm.at[:, reader, pl.ds(d * OCT, OCT), :])


def count(row_codes, col_codes):
    steps, inner = row_codes.shape
    shape = (RING, RING, DIRS * OCT, BLOCK)
    return pl.pallas_call(
        count_kernel,
        grid=(RING,),
        in_specs=[pl.BlockSpec((steps, inner), lambda k: (0, 0))] * 2,
        out_specs=[pl.BlockSpec((RING, 1, DIRS * OCT, BLOCK), lambda k: (0, k, 0, 0)), ANY, SMEM],
        out_shape=[
            jax.ShapeDtypeStruct(shape, BF16),
            jax.ShapeDtypeStruct(shape, BF16),
            jax.ShapeDtypeStruct((steps,), jnp.int32),
        ],
        scratch_shapes=[pltpu.VMEM((RING, OCT, BLOCK), BF16)],
        compiler_params=PARAMS,
        cost_estimate=pl.CostEstimate(
            flops=2 * steps * OCT * inner * RING * BLOCK, bytes_accessed=8 << 20, transcendentals=0
        ),
        name="count",
    )(row_codes, col_codes)


def gather(ids_ref, block_refs, first, held, rows, sems):
    copies = [
        pltpu.make_async_copy(ref, held.at[i], sems.at[i]) for i, ref in enumerate(block_refs)
    ]
    for copy in copies:
        copy.start()
    octants = lax.broadcasted_iota(jnp.int32, (OCT, RING * PER), 0)
    for i, copy in enumerate(copies):
        copy.wait()
        for j in range(2):
            owner = 2 * i + j
            table = jnp.concatenate(parts(held[i, j * OCT : (j + 1) * OCT, :]), axis=1)
            ids = ids_ref[first(owner) : first(owner) + 1, :]
            hot = jnp.where(octants == ids, 1.0, 0.0).astype(BF16)
            picked = lax.dot_general(
                hot, table, (((0,), (0,)), ((), ())), preferred_element_type=F32
            ).astype(BF16)
            for k in range(RING):
                rows[k, owner * PER : (owner + 1) * PER, :] = picked[k * PER : (k + 1) * PER]


def product(counts, rows):
    both = jnp.dot(counts, rows, preferred_element_type=F32)
    return both[:, :WIDTH] + both[:, WIDTH:]


def add_rest(flag_ref, rest_hbm, blocks, k, rows, rest, add):
    @pl.loop(0, DIRS)
    def _(d):
        @pl.when(flag_ref[k * DIRS + d] != 0)
        def _():
            start = pl.multiple_of(d * OCT, OCT)
            for i, s in enumerate(blocks):
                pltpu.sync_copy(rest_hbm.at[s, k, pl.ds(start, OCT), :], rest)
                add(start, product(rest[...], rows[k, i * BLOCK : (i + 1) * BLOCK, :]))


def part_kernel(blocks, adds, *refs):
    n = len(blocks)
    flag_ref, ids_ref, refs = refs[0], refs[1], refs[2:]
    block_refs, refs = refs[: 4 * n], refs[4 * n :]
    count_refs, rest_hbm, refs = refs[:n], refs[n], refs[n + 1 :]
    if adds:
        old_ref, refs = refs[0], refs[1:]
    out_ref, held, rows, rest, sems = refs
    k = pl.program_id(0)

    @pl.when(k == 0)
    def _():
        owner_row = lambda owner: blocks[owner // 8] * 8 + owner % 8
        gather(ids_ref, block_refs, owner_row, held, rows, sems)

    for m in range(RING):
        here = slice(m * 2 * OCT, (m + 1) * 2 * OCT)
        total = old_ref[0, here, :] if adds else None
        for i in range(n):
            term = product(count_refs[i][0, 0, here, :], rows[k, i * BLOCK : (i + 1) * BLOCK, :])
            total = term if total is None else total + term
        out_ref[0, here, :] = total

    def add(start, term):
        out_ref[0, pl.ds(start, OCT), :] += term

    add_rest(flag_ref, rest_hbm, blocks, k, rows, rest, add)


def part(blocks, flags, ids, arrays, counts, rest, old=None):
    n = len(blocks)
    x_spec = pl.BlockSpec((1, DIRS * OCT, WIDTH), lambda k: (k, 0, 0))
    count_specs = [
        pl.BlockSpec((1, 1, DIRS * OCT, BLOCK), lambda k, s=s: (s, k, 0, 0)) for s in blocks
    ]
    olds = [] if old is None else [old]
    return pl.pallas_call(
        functools.partial(part_kernel, blocks, old is not None),
        grid=(RING,),
        in_specs=[SMEM, pl.BlockSpec((PLANE, RING * PER), lambda k: (0, 0))]
        + [ANY] * (4 * n)
        + count_specs
        + [ANY]
        + [x_spec] * len(olds),
        out_specs=x_spec,
        out_shape=jax.ShapeDtypeStruct((RING, DIRS * OCT, WIDTH), F32),
        scratch_shapes=[
            pltpu.VMEM((4 * n, HALF, WIDTH), F32),
            pltpu.VMEM((RING, n * BLOCK, 2 * WIDTH), BF16),
            pltpu.VMEM((OCT, BLOCK), BF16),
            pltpu.SemaphoreType.DMA((4 * n,)),
        ],
        compiler_params=PARAMS,
        cost_estimate=pl.CostEstimate(
            flops=n * 3_000_000_000, bytes_accessed=(4 * n + 8) << 20, transcendentals=0
        ),
        name="part",
    )(flags, ids, *arrays, *[counts] * n, rest, *olds)


def finish_kernel(
    block, readers, flag_ref, ids_ref, b0, b1, b2, b3, count_hbm, rest_hbm, x_hbm, k_hbm,
    out0, out1,
    held, rows, rest, counts, x, kernels, xh, xl, sems,
):
    n = len(readers)
    early = []
    for i, k in enumerate(readers):
        early.append(pltpu.make_async_copy(count_hbm.at[block, k], counts.at[i], sems.at[4 + i]))
        early.append(pltpu.make_async_copy(x_hbm.at[k], x.at[i], sems.at[4 + n + i]))
    late = [
        pltpu.make_async_copy(k_hbm.at[d], kernels.at[d], sems.at[4 + 2 * n + d])
        for d in range(DIRS)
    ]
    for copy in early + late:
        copy.start()
    owner_row = lambda owner: block * 8 + owner
    gather(ids_ref, (b0, b1, b2, b3), owner_row, held, rows, sems)
    for copy in early:
        copy.wait()
    for i, k in enumerate(readers):
        for m in range(RING):
            here = slice(m * 2 * OCT, (m + 1) * 2 * OCT)
            x[i, here, :] += product(counts[i, here, :], rows[k])

        def add(start, term, i=i):
            x[i, pl.ds(start, OCT), :] += term

        add_rest(flag_ref, rest_hbm, (block,), k, rows, rest, add)
        for d in range(DIRS):
            high, low = parts(x[i, d * OCT : (d + 1) * OCT, :])
            xh[d, i * OCT : (i + 1) * OCT, :] = high
            xl[d, i * OCT : (i + 1) * OCT, :] = low

    def dot(a, b):
        return lax.dot_general(a, b, (((1,), (1,)), ((), ())), preferred_element_type=F32)

    total = None
    for d in range(DIRS):
        late[d].wait()
        high, low = parts(kernels[d])
        term = dot(xh[d], high) + dot(xh[d], low) + dot(xl[d], high)
        total = term if total is None else total + term
    for i, out in enumerate((out0, out1)):
        out[...] = total[i * OCT : (i + 1) * OCT]


def finish(block, readers, flags, ids, arrays, counts, rest, x, kernels):
    n = len(readers)
    shape = jax.ShapeDtypeStruct((OCT, WIDTH), F32)
    return pl.pallas_call(
        functools.partial(finish_kernel, block, readers),
        in_specs=[SMEM, VMEM] + [ANY] * 8,
        out_specs=[VMEM] * 2,
        out_shape=[shape] * 2,
        scratch_shapes=[
            pltpu.VMEM((4, HALF, WIDTH), F32),
            pltpu.VMEM((RING, BLOCK, 2 * WIDTH), BF16),
            pltpu.VMEM((OCT, BLOCK), BF16),
            pltpu.VMEM((n, DIRS * OCT, BLOCK), BF16),
            pltpu.VMEM((n, DIRS * OCT, WIDTH), F32),
            pltpu.VMEM((DIRS, WIDTH, WIDTH), F32),
            pltpu.VMEM((DIRS, n * OCT, WIDTH), BF16),
            pltpu.VMEM((DIRS, n * OCT, WIDTH), BF16),
            pltpu.SemaphoreType.DMA((4 + 2 * n + DIRS,)),
        ],
        compiler_params=PARAMS,
        cost_estimate=pl.CostEstimate(
            flops=6_000_000_000, bytes_accessed=16 << 20, transcendentals=0
        ),
        name="finish",
    )(flags, ids, *arrays, counts, rest, x, kernels)


def body(partials, partial_ids, read_lists, sources, targets, kernels):
    gx, gy = lax.axis_index("gx"), lax.axis_index("gy")
    device = gx * (RING * RING) + gy
    z, c, x, y = gx // CORES, gx % CORES, gy // RING, gy % RING
    owners = lax.axis_size(AXES)
    per_owner = partials.shape[0] // owners

    lists = jnp.concatenate([sources, targets], axis=0)
    ring_lists = [lists] + [along_z(lists, k) for k in range(1, RING)]

    received = lax.all_to_all(partials, AXES, split_axis=0, concat_axis=0, tiled=True)

    stacked = jnp.stack(ring_lists)
    slot, target = stacked[:, 0], stacked[:, 1]
    owner = slot // PER
    core = (owner // (RING * RING)) % CORES
    dx = (owner // RING - x) % RING
    dy = (owner - y) % RING
    s = jnp.where(core == 0, dy, dx)
    f = jnp.where(core == 0, dx, dy)
    column = ((s % 2 * CORES + (core + c) % CORES) * RING + f) * PER + slot % PER
    here = owner // PLANE == z
    row_codes = jnp.where(here, s // 2 * OCT + target, -1)
    per_dir = sources.shape[1] // DIRS
    counts, rest, flags = count(
        row_codes.reshape(RING * DIRS, per_dir), column.reshape(RING * DIRS, per_dir)
    )

    number = jnp.arange(PLANE, dtype=jnp.int32)
    s, w, f = number // (RING * CORES), number // RING % CORES, number % RING
    core = (w + c) % CORES
    there_x = (x + jnp.where(core == 0, f, s)) % RING
    there_y = (y + jnp.where(core == 0, s, f)) % RING
    order = core * (RING * RING) + there_x * RING + there_y
    reads = [
        lax.dynamic_slice(
            read_lists,
            (((z + k) % RING * CORES + c) * (RING * RING) + gy, z * (PLANE * PER)),
            (1, PLANE * PER),
        )
        for k in range(RING)
    ]
    reads = jnp.concatenate(reads, axis=0).reshape(RING, PLANE, PER)
    ids = jnp.take(reads.transpose(1, 0, 2).reshape(PLANE, RING * PER), order, axis=0)

    received, counts, rest, flags, ids = lax.optimization_barrier(
        (received, counts, rest, flags, ids)
    )
    octants = jnp.arange(OCT, dtype=jnp.int32)
    column_ids = lax.dynamic_slice_in_dim(partial_ids, device * per_owner, per_owner, 1).reshape(-1)
    selector = (octants[:, None] == column_ids[None, :]).astype(F32)
    density = jnp.dot(
        selector, received, precision=lax.Precision.HIGHEST, preferred_element_type=F32
    )

    line = [density] + [along_f(density, k) for k in range(1, RING)]
    low, high = jnp.concatenate(line[:2], axis=0), jnp.concatenate(line[2:], axis=0)
    low1, high3 = along_s(low, 1), along_s(high, 3)
    high1, low3 = along_s(high, 1), along_s(low, 3)
    low2, high2 = along_s(low1, 1), along_s(high3, 3)
    block = [[low, high], [low1, high1], [low2, high2], [low3, high3]]
    block = [mine + [across(half) for half in mine] for mine in block]

    total = part((0,), flags, ids, block[0], counts, rest)
    total = part((1, 3), flags, ids, block[1] + block[3], counts, rest, total)
    last = (flags, ids, block[2], counts, rest, total, kernels)
    out2, out1 = finish(2, (2, 1), *last)
    out3, out0 = finish(2, (3, 0), *last)
    return out0 + along_z(out2, -2) + along_z(out1, -1) + along_z(out3, -3)


def solution(mesh):
    return jax.shard_map(
        body,
        mesh=mesh,
        in_specs=(P(AXES, None), P(), P(), P(AXES, None), P(AXES, None), P()),
        out_specs=P(AXES, None),
        check_vma=False,
    )
```

profile of v0, /device:TPU:1, one launch (start us, length us, event | category | flops | bytes accessed | tf_op | source)
XLA Modules:
  0.0 132.0 jit_solution(15292360969060538241)
XLA Ops:
  0.0 0.9 fusion.48
  0.9 4.7 %collective-permute-start = (s32[2,8192]{1,0:T(2,128)S(1)}, s32[2,8192]{1,0:T(2,128)S(1)}, u32[]{:S(2)}, u32[]{:S(2)}) collective-permute-start(s32[2,8192]{1,0:T(2,128)S(1)} %get-tuple-element.38), channel_id=1, source_target_pairs={{32,0},{33,1},{34,2},{35,3},{36,4},{37,5},{38,6},{39,7},{40,8},{41... | collective-permute-start | bytes 196616 | tf_op jit(solution)/shard_map/ppermute | solution.py:40
  5.6 0.7 collective-permute-start.2
  6.3 9.7 %all-to-all-start = ((f32[128,8,512]{2,1,0:T(8,128)}), f32[128,8,512]{2,1,0:T(8,128)S(1)}, u32[]{:S(2)}, u32[]{:S(2)}) async-start(f32[128,8,512]{2,1,0:T(8,128)} %bitcast.14), calls=%async_computation | async-start | bytes 4194304 | tf_op jit(solution)/shard_map/all_to_all | solution.py:295
  16.3 0.9 fusion.49
  17.5 0.6 gather_fusion
  18.4 0.7 slice_reduce_fusion.1
  19.2 0.7 fusion.18
  19.9 20.9 %count.1 = (bf16[4,4,1024,256]{3,2,1,0:T(8,128)(2,1)}, bf16[4,4,1024,256]{3,2,1,0:T(8,128)(2,1)}, s32[32]{0:T(128)S(1)}) custom-call(s32[32,1024]{1,0:T(8,128)S(1)} %get-tuple-element.36.row_ref, s32[32,1024]{1,0:T(8,128)S(1)} %get-tuple-element.35.col_ref), custom_call_target="tpu_custom_call" | custom-call | flops 8589934592 | bytes 8388608 | tf_op jit(solution)/shard_map/count/pallas_call | solution.py:95
  40.8 4.9 %all-to-all-done = f32[128,8,512]{2,1,0:T(8,128)S(1)} async-done(((f32[128,8,512]{2,1,0:T(8,128)}), f32[128,8,512]{2,1,0:T(8,128)S(1)}, u32[]{:S(2)}, u32[]{:S(2)}) %all-to-all-start) | async-done | bytes 2097184 | tf_op jit(solution)/shard_map/all_to_all | solution.py:295
  45.8 0.9 fusion
  46.7 1.6 %collective-permute-start.6 = (f32[128,512]{1,0:T(8,128)S(1)}, f32[128,512]{1,0:T(8,128)S(1)}, u32[]{:S(2)}, u32[]{:S(2)}) collective-permute-start(f32[128,512]{1,0:T(8,128)S(1)} %fusion), channel_id=1, source_target_pairs={{8,0},{9,1},{10,2},{11,3},{12,4},{13,5},{14,6},{15,7},{0,8},{1,9},... | collective-permute-start | bytes 786440 | tf_op jit(solution)/shard_map/ppermute | solution.py:40
  48.3 0.9 collective-permute-start.7
  49.2 4.6 %collective-permute-done.6 = f32[128,512]{1,0:T(8,128)S(1)} collective-permute-done((f32[128,512]{1,0:T(8,128)S(1)}, f32[128,512]{1,0:T(8,128)S(1)}, u32[]{:S(2)}, u32[]{:S(2)}) %collective-permute-start.6) | collective-permute-done | bytes 262176 | tf_op jit(solution)/shard_map/ppermute | solution.py:40
  53.8 2.8 %collective-permute-done.7 = f32[128,512]{1,0:T(8,128)S(1)} collective-permute-done((f32[128,512]{1,0:T(8,128)S(1)}, f32[128,512]{1,0:T(8,128)S(1)}, u32[]{:S(2)}, u32[]{:S(2)}) %collective-permute-start.7) | collective-permute-done | bytes 262176 | tf_op jit(solution)/shard_map/ppermute | solution.py:40
  56.6 1.9 %collective-permute-start.19 = (f32[256,512]{1,0:T(8,128)S(1)}, f32[256,512]{1,0:T(8,128)S(1)}, u32[]{:S(2)}, u32[]{:S(2)}) collective-permute-start(f32[256,512]{1,0:T(8,128)S(1)} %constant_dynamic-update-slice_fusion.refs_3_), channel_id=1, source_target_pairs={{16,0},{17,1},{18,2},{19,3},{20,4},{21,5},{22,6},{23,7},{24,8},{25... | collective-permute-start | bytes 1572872 | tf_op jit(solution)/shard_map/ppermute | solution.py:40
  58.8 1.0 collective-permute-start.3
  59.8 1.1 collective-permute-start.8
  60.9 6.0 %collective-permute-done.3 = f32[128,512]{1,0:T(8,128)S(1)} collective-permute-done((f32[128,512]{1,0:T(8,128)S(1)}, f32[128,512]{1,0:T(8,128)S(1)}, u32[]{:S(2)}, u32[]{:S(2)}) %collective-permute-start.3) | collective-permute-done | bytes 262176 | tf_op jit(solution)/shard_map/ppermute | solution.py:40
  66.9 2.3 %collective-permute-start.18 = (f32[256,512]{1,0:T(8,128)S(1)}, f32[256,512]{1,0:T(8,128)S(1)}, u32[]{:S(2)}, u32[]{:S(2)}) collective-permute-start(f32[256,512]{1,0:T(8,128)S(1)} %pad_maximum_fusion.refs_2_), channel_id=1, source_target_pairs={{16,0},{17,1},{18,2},{19,3},{20,4},{21,5},{22,6},{23,7},{24,8},{25... | collective-permute-start | bytes 1572872 | tf_op jit(solution)/shard_map/ppermute | solution.py:40
  69.2 1.5 %collective-permute-start.4 = (f32[256,512]{1,0:T(8,128)S(1)}, f32[256,512]{1,0:T(8,128)S(1)}, u32[]{:S(2)}, u32[]{:S(2)}) collective-permute-start(f32[256,512]{1,0:T(8,128)S(1)} %pad_maximum_fusion.refs_2_), channel_id=1, source_target_pairs={{1,0},{2,1},{3,2},{0,3},{5,4},{6,5},{7,6},{4,7},{9,8},{10,9},{11,1... | collective-permute-start | bytes 1572872 | tf_op jit(solution)/shard_map/ppermute | solution.py:40
  72.0 5.5 %collective-permute-done.4.refs_2_ = f32[256,512]{1,0:T(8,128)S(1)} collective-permute-done((f32[256,512]{1,0:T(8,128)S(1)}, f32[256,512]{1,0:T(8,128)S(1)}, u32[]{:S(2)}, u32[]{:S(2)}) %collective-permute-start.4) | collective-permute-done | bytes 524320 | tf_op jit(solution)/shard_map/ppermute | solution.py:40
  77.5 2.7 %collective-permute-start.5 = (f32[256,512]{1,0:T(8,128)S(1)}, f32[256,512]{1,0:T(8,128)S(1)}, u32[]{:S(2)}, u32[]{:S(2)}) collective-permute-start(f32[256,512]{1,0:T(8,128)S(1)} %collective-permute-done.4.refs_2_), channel_id=1, source_target_pairs={{1,0},{2,1},{3,2},{0,3},{5,4},{6,5},{7,6},{4,7},{9,8},{10,9},{11,1... | collective-permute-start | bytes 1572872 | tf_op jit(solution)/shard_map/ppermute | solution.py:40
  80.8 8.2 %part.2.refs_13_ = f32[4,1024,512]{2,1,0:T(8,128)} custom-call(s32[32]{0:T(128)S(1)} %get-tuple-element.20.refs_0_.flag_ref, s32[32,128]{1,0:T(8,128)S(1)} %broadcast_select_fusion.refs_1_.ids_ref, f32[256,512]{1,0:T(8,128)S(1)} %pad_maximum_fusion.refs_2_, f32[256,512]{1,0:T(8,128)S(1)} %constant_dynamic-update-slice_fusion.refs_3_, ...), custom_call_target="tpu_custom_call" | custom-call | flops 3000000000 | bytes 12582912 | tf_op jit(solution)/shard_map/part/pallas_call | solution.py:187
  89.6 14.0 %part.3.x_hbm = f32[4,1024,512]{2,1,0:T(8,128)} custom-call(s32[32]{0:T(128)S(1)} %get-tuple-element.20.refs_0_.flag_ref, s32[32,128]{1,0:T(8,128)S(1)} %broadcast_select_fusion.refs_1_.ids_ref, f32[256,512]{1,0:T(8,128)S(1)} %collective-permute-done.4.refs_2_, f32[256,512]{1,0:T(8,128)S(1)} %collective-permute-done.12.refs_3_, ...), custom_call_target="tpu_custom_call" | custom-call | flops 6000000000 | bytes 16777216 | tf_op jit(solution)/shard_map/part/pallas_call | solution.py:187
  103.6 9.6 %finish.3 = (f32[128,512]{1,0:T(8,128)S(1)}, f32[128,512]{1,0:T(8,128)S(1)}) custom-call(s32[32]{0:T(128)S(1)} %get-tuple-element.20.refs_0_.flag_ref, s32[32,128]{1,0:T(8,128)S(1)} %broadcast_select_fusion.refs_1_.ids_ref, f32[256,512]{1,0:T(8,128)S(1)} %collective-permute-done.5.b0, f32[256,512]{1,0:T(8,128)S(1)} %collective-permute-done.9.b1, ...), custom_call_target="tpu_custom_call" | custom-call | flops 6000000000 | bytes 16777216 | tf_op jit(solution)/shard_map/finish/pallas_call | solution.py:261
  113.8 0.6 collective-permute-start.21
  114.4 9.6 %finish.2 = (f32[128,512]{1,0:T(8,128)S(1)}, f32[128,512]{1,0:T(8,128)S(1)}) custom-call(s32[32]{0:T(128)S(1)} %get-tuple-element.20.refs_0_.flag_ref, s32[32,128]{1,0:T(8,128)S(1)} %broadcast_select_fusion.refs_1_.ids_ref, f32[256,512]{1,0:T(8,128)S(1)} %collective-permute-done.5.b0, f32[256,512]{1,0:T(8,128)S(1)} %collective-permute-done.9.b1, ...), custom_call_target="tpu_custom_call" | custom-call | flops 6000000000 | bytes 16777216 | tf_op jit(solution)/shard_map/finish/pallas_call | solution.py:261
  124.0 2.1 %collective-permute-start.22 = (f32[128,512]{1,0:T(8,128)S(1)}, f32[128,512]{1,0:T(8,128)S(1)}, u32[]{:S(2)}, u32[]{:S(2)}) collective-permute-start(f32[128,512]{1,0:T(8,128)S(1)} %get-tuple-element.28), channel_id=1, source_target_pairs={{32,0},{33,1},{34,2},{35,3},{36,4},{37,5},{38,6},{39,7},{40,8},{41... | collective-permute-start | bytes 786440 | tf_op jit(solution)/shard_map/ppermute | solution.py:40
  126.2 2.5 %collective-permute-done.21 = f32[128,512]{1,0:T(8,128)S(1)} collective-permute-done((f32[128,512]{1,0:T(8,128)S(1)}, f32[128,512]{1,0:T(8,128)S(1)}, u32[]{:S(2)}, u32[]{:S(2)}) %collective-permute-start.21) | collective-permute-done | bytes 262176 | tf_op jit(solution)/shard_map/ppermute | solution.py:40
  128.7 2.6 %collective-permute-done.22 = f32[128,512]{1,0:T(8,128)S(1)} collective-permute-done((f32[128,512]{1,0:T(8,128)S(1)}, f32[128,512]{1,0:T(8,128)S(1)}, u32[]{:S(2)}, u32[]{:S(2)}) %collective-permute-start.22) | collective-permute-done | bytes 262176 | tf_op jit(solution)/shard_map/ppermute | solution.py:40
  131.2 0.8 add_add_fusion
  (46 shorter events, 4.0 us)
Async XLA Ops:
  0.0 18.1 %copy-start = (s32[128,1024]{1,0:T(8,128)S(1)}, s32[128,1024]{1,0:T(8,128)}, u32[]{:S(2)}) copy-start(s32[128,1024]{1,0:T(8,128)} %param.7) | copy-start | bytes 1572868
  0.9 17.4 %collective-permute-start = (s32[2,8192]{1,0:T(2,128)S(1)}, s32[2,8192]{1,0:T(2,128)S(1)}, u32[]{:S(2)}, u32[]{:S(2)}) collective-permute-start(s32[2,8192]{1,0:T(2,128)S(1)} %get-tuple-element.38), channel_id=1, source_target_pairs={{32,0},{33,1},{34,2},{35,3},{36,4},{37,5},{38,6},{39,7},{40,8},{41... | collective-permute-start | bytes 196616 | tf_op jit(solution)/shard_map/ppermute | solution.py:40
  5.6 12.7 %collective-permute-start.1 = (s32[2,8192]{1,0:T(2,128)S(1)}, s32[2,8192]{1,0:T(2,128)S(1)}, u32[]{:S(2)}, u32[]{:S(2)}) collective-permute-start(s32[2,8192]{1,0:T(2,128)S(1)} %get-tuple-element.38), channel_id=1, source_target_pairs={{64,0},{65,1},{66,2},{67,3},{68,4},{69,5},{70,6},{71,7},{72,8},{73... | collective-permute-start | bytes 196616 | tf_op jit(solution)/shard_map/ppermute | solution.py:40
  5.6 12.8 %collective-permute-start.2 = (s32[2,8192]{1,0:T(2,128)S(1)}, s32[2,8192]{1,0:T(2,128)S(1)}, u32[]{:S(2)}, u32[]{:S(2)}) collective-permute-start(s32[2,8192]{1,0:T(2,128)S(1)} %get-tuple-element.38), channel_id=1, source_target_pairs={{96,0},{97,1},{98,2},{99,3},{100,4},{101,5},{102,6},{103,7},{104,8... | collective-permute-start | bytes 196616 | tf_op jit(solution)/shard_map/ppermute | solution.py:40
  6.3 39.5 %all-to-all-start = ((f32[128,8,512]{2,1,0:T(8,128)}), f32[128,8,512]{2,1,0:T(8,128)S(1)}, u32[]{:S(2)}, u32[]{:S(2)}) async-start(f32[128,8,512]{2,1,0:T(8,128)} %bitcast.14), calls=%async_computation | async-start | bytes 4194304 | tf_op jit(solution)/shard_map/all_to_all | solution.py:295
  46.7 7.1 %collective-permute-start.6 = (f32[128,512]{1,0:T(8,128)S(1)}, f32[128,512]{1,0:T(8,128)S(1)}, u32[]{:S(2)}, u32[]{:S(2)}) collective-permute-start(f32[128,512]{1,0:T(8,128)S(1)} %fusion), channel_id=1, source_target_pairs={{8,0},{9,1},{10,2},{11,3},{12,4},{13,5},{14,6},{15,7},{0,8},{1,9},... | collective-permute-start | bytes 786440 | tf_op jit(solution)/shard_map/ppermute | solution.py:40
  48.3 8.3 %collective-permute-start.7 = (f32[128,512]{1,0:T(8,128)S(1)}, f32[128,512]{1,0:T(8,128)S(1)}, u32[]{:S(2)}, u32[]{:S(2)}) collective-permute-start(f32[128,512]{1,0:T(8,128)S(1)} %fusion), channel_id=1, source_target_pairs={{12,0},{13,1},{14,2},{15,3},{0,4},{1,5},{2,6},{3,7},{4,8},{5,9},{6... | collective-permute-start | bytes 786440 | tf_op jit(solution)/shard_map/ppermute | solution.py:40
  56.6 14.1 %collective-permute-start.19 = (f32[256,512]{1,0:T(8,128)S(1)}, f32[256,512]{1,0:T(8,128)S(1)}, u32[]{:S(2)}, u32[]{:S(2)}) collective-permute-start(f32[256,512]{1,0:T(8,128)S(1)} %constant_dynamic-update-slice_fusion.refs_3_), channel_id=1, source_target_pairs={{16,0},{17,1},{18,2},{19,3},{20,4},{21,5},{22,6},{23,7},{24,8},{25... | collective-permute-start | bytes 1572872 | tf_op jit(solution)/shard_map/ppermute | solution.py:40
  58.6 12.2 %collective-permute-start.12 = (f32[256,512]{1,0:T(8,128)S(1)}, f32[256,512]{1,0:T(8,128)S(1)}, u32[]{:S(2)}, u32[]{:S(2)}) collective-permute-start(f32[256,512]{1,0:T(8,128)S(1)} %constant_dynamic-update-slice_fusion.refs_3_), channel_id=1, source_target_pairs={{1,0},{2,1},{3,2},{0,3},{5,4},{6,5},{7,6},{4,7},{9,8},{10,9},{11,1... | collective-permute-start | bytes 1572872 | tf_op jit(solution)/shard_map/ppermute | solution.py:40
  58.8 8.1 %collective-permute-start.3 = (f32[128,512]{1,0:T(8,128)S(1)}, f32[128,512]{1,0:T(8,128)S(1)}, u32[]{:S(2)}, u32[]{:S(2)}) collective-permute-start(f32[128,512]{1,0:T(8,128)S(1)} %fusion), channel_id=1, source_target_pairs={{4,0},{5,1},{6,2},{7,3},{8,4},{9,5},{10,6},{11,7},{12,8},{13,9},{1... | collective-permute-start | bytes 786440 | tf_op jit(solution)/shard_map/ppermute | solution.py:40
  59.8 11.5 %collective-permute-start.8 = (f32[256,512]{1,0:T(8,128)S(1)}, f32[256,512]{1,0:T(8,128)S(1)}, u32[]{:S(2)}, u32[]{:S(2)}) collective-permute-start(f32[256,512]{1,0:T(8,128)S(1)} %constant_dynamic-update-slice_fusion.refs_3_), channel_id=1, source_target_pairs={{3,0},{0,1},{1,2},{2,3},{7,4},{4,5},{5,6},{6,7},{11,8},{8,9},{9,10... | collective-permute-start | bytes 1572872 | tf_op jit(solution)/shard_map/ppermute | solution.py:40
  66.9 4.7 %collective-permute-start.18 = (f32[256,512]{1,0:T(8,128)S(1)}, f32[256,512]{1,0:T(8,128)S(1)}, u32[]{:S(2)}, u32[]{:S(2)}) collective-permute-start(f32[256,512]{1,0:T(8,128)S(1)} %pad_maximum_fusion.refs_2_), channel_id=1, source_target_pairs={{16,0},{17,1},{18,2},{19,3},{20,4},{21,5},{22,6},{23,7},{24,8},{25... | collective-permute-start | bytes 1572872 | tf_op jit(solution)/shard_map/ppermute | solution.py:40
  69.2 8.3 %collective-permute-start.4 = (f32[256,512]{1,0:T(8,128)S(1)}, f32[256,512]{1,0:T(8,128)S(1)}, u32[]{:S(2)}, u32[]{:S(2)}) collective-permute-start(f32[256,512]{1,0:T(8,128)S(1)} %pad_maximum_fusion.refs_2_), channel_id=1, source_target_pairs={{1,0},{2,1},{3,2},{0,3},{5,4},{6,5},{7,6},{4,7},{9,8},{10,9},{11,1... | collective-permute-start | bytes 1572872 | tf_op jit(solution)/shard_map/ppermute | solution.py:40
  70.7 9.5 %collective-permute-start.15 = (f32[256,512]{1,0:T(8,128)S(1)}, f32[256,512]{1,0:T(8,128)S(1)}, u32[]{:S(2)}, u32[]{:S(2)}) collective-permute-start(f32[256,512]{1,0:T(8,128)S(1)} %pad_maximum_fusion.refs_2_), channel_id=1, source_target_pairs={{3,0},{0,1},{1,2},{2,3},{7,4},{4,5},{5,6},{6,7},{11,8},{8,9},{9,10... | collective-permute-start | bytes 1572872 | tf_op jit(solution)/shard_map/ppermute | solution.py:40
  70.7 9.7 %collective-permute-start.14 = (f32[256,512]{1,0:T(8,128)S(1)}, f32[256,512]{1,0:T(8,128)S(1)}, u32[]{:S(2)}, u32[]{:S(2)}) collective-permute-start(f32[256,512]{1,0:T(8,128)S(1)} %collective-permute-done.12.refs_3_), channel_id=1, source_target_pairs={{16,0},{17,1},{18,2},{19,3},{20,4},{21,5},{22,6},{23,7},{24,8},{25... | collective-permute-start | bytes 1572872 | tf_op jit(solution)/shard_map/ppermute | solution.py:40
  71.3 18.3 %collective-permute-start.17 = (f32[256,512]{1,0:T(8,128)S(1)}, f32[256,512]{1,0:T(8,128)S(1)}, u32[]{:S(2)}, u32[]{:S(2)}) collective-permute-start(f32[256,512]{1,0:T(8,128)S(1)} %collective-permute-done.8.refs_7_), channel_id=1, source_target_pairs={{16,0},{17,1},{18,2},{19,3},{20,4},{21,5},{22,6},{23,7},{24,8},{25... | collective-permute-start | bytes 1572872 | tf_op jit(solution)/shard_map/ppermute | solution.py:40
  71.6 17.4 %collective-permute-start.9 = (f32[256,512]{1,0:T(8,128)S(1)}, f32[256,512]{1,0:T(8,128)S(1)}, u32[]{:S(2)}, u32[]{:S(2)}) collective-permute-start(f32[256,512]{1,0:T(8,128)S(1)} %collective-permute-done.8.refs_7_), channel_id=1, source_target_pairs={{3,0},{0,1},{1,2},{2,3},{7,4},{4,5},{5,6},{6,7},{11,8},{8,9},{9,10... | collective-permute-start | bytes 1572872 | tf_op jit(solution)/shard_map/ppermute | solution.py:40
  77.5 11.7 %collective-permute-start.5 = (f32[256,512]{1,0:T(8,128)S(1)}, f32[256,512]{1,0:T(8,128)S(1)}, u32[]{:S(2)}, u32[]{:S(2)}) collective-permute-start(f32[256,512]{1,0:T(8,128)S(1)} %collective-permute-done.4.refs_2_), channel_id=1, source_target_pairs={{1,0},{2,1},{3,2},{0,3},{5,4},{6,5},{7,6},{4,7},{9,8},{10,9},{11,1... | collective-permute-start | bytes 1572872 | tf_op jit(solution)/shard_map/ppermute | solution.py:40
  80.3 9.4 %collective-permute-start.13 = (f32[256,512]{1,0:T(8,128)S(1)}, f32[256,512]{1,0:T(8,128)S(1)}, u32[]{:S(2)}, u32[]{:S(2)}) collective-permute-start(f32[256,512]{1,0:T(8,128)S(1)} %collective-permute-done.4.refs_2_), channel_id=1, source_target_pairs={{16,0},{17,1},{18,2},{19,3},{20,4},{21,5},{22,6},{23,7},{24,8},{25... | collective-permute-start | bytes 1572872 | tf_op jit(solution)/shard_map/ppermute | solution.py:40
  80.4 9.2 %collective-permute-start.16 = (f32[256,512]{1,0:T(8,128)S(1)}, f32[256,512]{1,0:T(8,128)S(1)}, u32[]{:S(2)}, u32[]{:S(2)}) collective-permute-start(f32[256,512]{1,0:T(8,128)S(1)} %collective-permute-done.15.refs_6_), channel_id=1, source_target_pairs={{16,0},{17,1},{18,2},{19,3},{20,4},{21,5},{22,6},{23,7},{24,8},{25... | collective-permute-start | bytes 1572872 | tf_op jit(solution)/shard_map/ppermute | solution.py:40
  89.0 14.6 %collective-permute-start.11 = (f32[256,512]{1,0:T(8,128)S(1)}, f32[256,512]{1,0:T(8,128)S(1)}, u32[]{:S(2)}, u32[]{:S(2)}) collective-permute-start(f32[256,512]{1,0:T(8,128)S(1)} %collective-permute-done.9.b1), channel_id=1, source_target_pairs={{16,0},{17,1},{18,2},{19,3},{20,4},{21,5},{22,6},{23,7},{24,8},{25... | collective-permute-start | bytes 1572872 | tf_op jit(solution)/shard_map/ppermute | solution.py:40
  89.3 14.4 %collective-permute-start.10 = (f32[256,512]{1,0:T(8,128)S(1)}, f32[256,512]{1,0:T(8,128)S(1)}, u32[]{:S(2)}, u32[]{:S(2)}) collective-permute-start(f32[256,512]{1,0:T(8,128)S(1)} %collective-permute-done.5.b0), channel_id=1, source_target_pairs={{16,0},{17,1},{18,2},{19,3},{20,4},{21,5},{22,6},{23,7},{24,8},{25... | collective-permute-start | bytes 1572872 | tf_op jit(solution)/shard_map/ppermute | solution.py:40
  113.3 12.9 %collective-permute-start.20 = (f32[128,512]{1,0:T(8,128)S(1)}, f32[128,512]{1,0:T(8,128)S(1)}, u32[]{:S(2)}, u32[]{:S(2)}) collective-permute-start(f32[128,512]{1,0:T(8,128)S(1)} %get-tuple-element.26), channel_id=1, source_target_pairs={{64,0},{65,1},{66,2},{67,3},{68,4},{69,5},{70,6},{71,7},{72,8},{73... | collective-permute-start | bytes 786440 | tf_op jit(solution)/shard_map/ppermute | solution.py:40
  113.8 14.9 %collective-permute-start.21 = (f32[128,512]{1,0:T(8,128)S(1)}, f32[128,512]{1,0:T(8,128)S(1)}, u32[]{:S(2)}, u32[]{:S(2)}) collective-permute-start(f32[128,512]{1,0:T(8,128)S(1)} %get-tuple-element.27), channel_id=1, source_target_pairs={{96,0},{97,1},{98,2},{99,3},{100,4},{101,5},{102,6},{103,7},{104,8... | collective-permute-start | bytes 786440 | tf_op jit(solution)/shard_map/ppermute | solution.py:40
  124.0 7.2 %collective-permute-start.22 = (f32[128,512]{1,0:T(8,128)S(1)}, f32[128,512]{1,0:T(8,128)S(1)}, u32[]{:S(2)}, u32[]{:S(2)}) collective-permute-start(f32[128,512]{1,0:T(8,128)S(1)} %get-tuple-element.28), channel_id=1, source_target_pairs={{32,0},{33,1},{34,2},{35,3},{36,4},{37,5},{38,6},{39,7},{40,8},{41... | collective-permute-start | bytes 786440 | tf_op jit(solution)/shard_map/ppermute | solution.py:40
where the time goes:
time: 133 us; the launch traced here: 132 us
  Pallas kernels  62.3 us (47%)
  starting transfers between devices  34.1 us (26%)
  waiting for transfers between devices  28.9 us (22%)
  local copies, waits for them, and re-layouts  2.8 us (2%)
  other arithmetic  2.59 us (2%)
    ppermute x23, starting transfers between devices, fetch(): return lax.ppermute(value, AXES, pairs)  24.4 us
    ppermute x23, waiting for transfers between devices, fetch(): return lax.ppermute(value, AXES, pairs)  24 us
    pallas_call x2, Pallas kernels, part(): pl.pallas_call(functools.partial(part_kernel, blocks, old is not None), g...  22.2 us
    pallas_call x1, Pallas kernels, count(): pl.pallas_call(count_kernel, grid=(RING,), in_specs=[pl.BlockSpec((steps,...  20.9 us
    pallas_call x2, Pallas kernels, finish(): pl.pallas_call(functools.partial(finish_kernel, block, readers), in_specs...  19.2 us
    all_to_all x1, starting transfers between devices, body(): lax.all_to_all(partials, AXES, split_axis=0, concat_axis=0, tiled=True)  9.74 us
    all_to_all x1, waiting for transfers between devices, body(): lax.all_to_all(partials, AXES, split_axis=0, concat_axis=0, tiled=True)  4.94 us
  transfers between devices with their start and end apart: 24, of which 7 were waited for; matrix products, arithmetic and copies ran while one was open for 3% of the time, Pallas kernels for 40%

commit v1 on v0

v1 whole, which is shorter than its diff:
```python
import functools

import jax
import jax.numpy as jnp
from jax import lax
from jax.experimental import pallas as pl
from jax.experimental.pallas import tpu as pltpu
from jax.sharding import PartitionSpec as P

AXES = ("gx", "gy")
RING = 4
CORES = 2
OCT = 128
PER = 32
DIRS = 8
WIDTH = 512
PLANE = RING * RING * CORES
BLOCK = CORES * RING * PER
HALF = RING // 2 * OCT
BF16 = jnp.bfloat16
F32 = jnp.float32
HBM = pl.BlockSpec(memory_space=pltpu.HBM)
SMEM = pl.BlockSpec(memory_space=pltpu.SMEM)
VMEM = pl.BlockSpec(memory_space=pltpu.VMEM)
LIMIT = 24


def device_of(x, y, z, c):
    return ((z % RING) * CORES + c % CORES) * RING * RING + (x % RING) * RING + y % RING


def fetch(value, shift):
    pairs = []
    for z in range(RING):
        for c in range(CORES):
            for x in range(RING):
                for y in range(RING):
                    dx, dy, dz, dc = shift(c)
                    pairs.append((device_of(x + dx, y + dy, z + dz, c + dc), device_of(x, y, z, c)))
    return lax.ppermute(value, AXES, pairs)


def along_f(value, k):
    return fetch(value, lambda core: (k, 0, 0, 0) if core == 0 else (0, k, 0, 0))


def along_s(value, k):
    return fetch(value, lambda core: (0, k, 0, 0) if core == 0 else (k, 0, 0, 0))


def along_z(value, k):
    return fetch(value, lambda core: (0, 0, k, 0))


def across(value):
    return fetch(value, lambda core: (0, 0, 0, 1))


def parts(value):
    high = value.astype(BF16)
    return high, (value - high.astype(F32)).astype(BF16)


def count_kernel(row_ref, col_ref, out_ref, rest_hbm, flag_ref, rest_ref):
    reader = pl.program_id(0)
    inner = row_ref.shape[1]

    def counts_of(d):
        rows = lax.broadcasted_iota(jnp.int32, (RING // 2 * OCT, inner), 0)
        cols = lax.broadcasted_iota(jnp.int32, (2 * BLOCK, inner), 0)
        step = reader * DIRS + d
        row_hot = jnp.where(rows == row_ref[pl.ds(step, 1), :], 1.0, 0.0).astype(BF16)
        col_hot = jnp.where(cols == col_ref[pl.ds(step, 1), :], 1.0, 0.0).astype(BF16)
        return lax.dot_general(
            row_hot, col_hot, (((1,), (1,)), ((), ())), preferred_element_type=F32
        )

    tops = []
    for d in range(DIRS):
        counts = counts_of(d)
        rounded = counts.astype(BF16)
        for s in range(RING):
            i, j = s // 2 * OCT, s % 2 * BLOCK
            out_ref[s, 0, d * OCT : (d + 1) * OCT, :] = rounded[i : i + OCT, j : j + BLOCK]
        tops.append(jnp.max(counts, axis=0, keepdims=True))
    large = jnp.max(functools.reduce(jnp.maximum, tops)) > 256.0
    flag_ref[reader] = large.astype(jnp.int32)

    @pl.when(large)
    def _():
        @pl.loop(0, DIRS)
        def _(d):
            counts = counts_of(d)
            rest = (counts - counts.astype(BF16).astype(F32)).astype(BF16)
            for s in range(RING):
                i, j = s // 2 * OCT, s % 2 * BLOCK
                rest_ref[s] = rest[i : i + OCT, j : j + BLOCK]
            start = pl.multiple_of(d * OCT, OCT)
            pltpu.sync_copy(rest_ref, rest_hbm.at[:, reader, pl.ds(start, OCT), :])


def count(row_codes, col_codes):
    steps, inner = row_codes.shape
    shape = (RING, RING, DIRS * OCT, BLOCK)
    return pl.pallas_call(
        count_kernel,
        grid=(RING,),
        in_specs=[pl.BlockSpec((steps, inner), lambda k: (0, 0))] * 2,
        out_specs=[pl.BlockSpec((RING, 1, DIRS * OCT, BLOCK), lambda k: (0, k, 0, 0)), HBM, SMEM],
        out_shape=[
            jax.ShapeDtypeStruct(shape, BF16),
            jax.ShapeDtypeStruct(shape, BF16),
            jax.ShapeDtypeStruct((RING,), jnp.int32),
        ],
        scratch_shapes=[pltpu.VMEM((RING, OCT, BLOCK), BF16)],
        compiler_params=pltpu.CompilerParams(vmem_limit_bytes=20 << 20),
        cost_estimate=pl.CostEstimate(
            flops=100_000_000, bytes_accessed=1 << 20, transcendentals=0
        ),
        name="count",
    )(row_codes, col_codes)


def pick(ids_ref, first, refs, store):
    octants = lax.broadcasted_iota(jnp.int32, (OCT, RING * PER), 0)
    for i, ref in enumerate(refs):
        for j in range(2):
            owner = 2 * i + j
            table = jnp.concatenate(parts(ref[j * OCT : (j + 1) * OCT, :]), axis=1)
            hot = jnp.where(octants == ids_ref[first + owner : first + owner + 1, :], 1.0, 0.0)
            picked = lax.dot_general(
                hot.astype(BF16), table, (((0,), (0,)), ((), ())), preferred_element_type=F32
            ).astype(BF16)
            for k in range(RING):
                store(owner, k, picked[k * PER : (k + 1) * PER])


def gather_kernel(blocks, ids_ref, *refs):
    n = len(blocks)
    for i, s in enumerate(blocks):
        rows = refs[4 * n + i]

        def store(owner, k, values, rows=rows):
            rows[k, owner * PER : (owner + 1) * PER, :] = values

        pick(ids_ref, s * 2 * RING, refs[4 * i : 4 * i + 4], store)


def gather(blocks, ids, arrays):
    n = len(blocks)
    return pl.pallas_call(
        functools.partial(gather_kernel, blocks),
        in_specs=[VMEM] * (1 + 4 * n),
        out_specs=[VMEM] * n,
        out_shape=[jax.ShapeDtypeStruct((RING, BLOCK, 2 * WIDTH), BF16)] * n,
        compiler_params=pltpu.CompilerParams(vmem_limit_bytes=16 << 20),
        cost_estimate=pl.CostEstimate(
            flops=n * 1_500_000_000, bytes_accessed=n << 20, transcendentals=0
        ),
        name="gather",
    )(ids, *arrays)


def finish_kernel(
    readers, flag_ref, ids_ref, b0, b1, b2, b3, rows0, rows1, rows3, count_ref, k_ref, rest_hbm,
    out0, out1,
    rows2, xh, xl, rest,
):
    def store(owner, k, values):
        rows2[k, owner * PER : (owner + 1) * PER, :] = values

    pick(ids_ref, 2 * 2 * RING, (b0, b1, b2, b3), store)

    def product(counts, k):
        rows = jnp.concatenate([ref[k] for ref in (rows0, rows1, rows2, rows3)], axis=0)
        both = jnp.dot(jnp.concatenate(counts, axis=1), rows, preferred_element_type=F32)
        return both[:, :WIDTH] + both[:, WIDTH:]

    for i, k in enumerate(readers):
        there = slice(i * OCT, (i + 1) * OCT)
        for m in range(0, DIRS, 2):
            here = slice(m * OCT, (m + 2) * OCT)
            high, low = parts(product([count_ref[s, k, here, :] for s in range(RING)], k))
            for j in range(2):
                xh[m + j, there, :] = high[j * OCT : (j + 1) * OCT]
                xl[m + j, there, :] = low[j * OCT : (j + 1) * OCT]

        @pl.when(flag_ref[k] != 0)
        def _():
            @pl.loop(0, DIRS)
            def _(d):
                start = pl.multiple_of(d * OCT, OCT)
                pltpu.sync_copy(rest_hbm.at[:, k, pl.ds(start, OCT), :], rest)
                total = product([rest[s] for s in range(RING)], k)
                total += xh[d, there, :].astype(F32) + xl[d, there, :].astype(F32)
                high, low = parts(total)
                xh[d, there, :] = high
                xl[d, there, :] = low

    def dot(a, b):
        return lax.dot_general(a, b, (((1,), (1,)), ((), ())), preferred_element_type=F32)

    total = None
    for d in range(DIRS):
        high, low = parts(k_ref[d])
        term = dot(xh[d], high) + dot(xh[d], low) + dot(xl[d], high)
        total = term if total is None else total + term
    for i, out in enumerate((out0, out1)):
        out[...] = total[i * OCT : (i + 1) * OCT]


def finish(readers, flags, ids, arrays, rows, counts, kernels, rest):
    n = len(readers)
    return pl.pallas_call(
        functools.partial(finish_kernel, readers),
        in_specs=[SMEM] + [VMEM] * 10 + [HBM],
        out_specs=[VMEM] * 2,
        out_shape=[jax.ShapeDtypeStruct((OCT, WIDTH), F32)] * 2,
        scratch_shapes=[
            pltpu.VMEM((RING, BLOCK, 2 * WIDTH), BF16),
            pltpu.VMEM((DIRS, n * OCT, WIDTH), BF16),
            pltpu.VMEM((DIRS, n * OCT, WIDTH), BF16),
            pltpu.VMEM((RING, OCT, BLOCK), BF16),
        ],
        compiler_params=pltpu.CompilerParams(vmem_limit_bytes=LIMIT << 20),
        cost_estimate=pl.CostEstimate(
            flops=9_000_000_000, bytes_accessed=2 << 20, transcendentals=0
        ),
        name="finish",
    )(flags, ids, *arrays, *rows, counts, kernels, rest)


def body(partials, partial_ids, read_lists, sources, targets, kernels):
    gx, gy = lax.axis_index("gx"), lax.axis_index("gy")
    device = gx * (RING * RING) + gy
    z, c, x, y = gx // CORES, gx % CORES, gy // RING, gy % RING
    owners = lax.axis_size(AXES)
    per_owner = partials.shape[0] // owners

    received = lax.all_to_all(partials, AXES, split_axis=0, concat_axis=0, tiled=True)

    number = jnp.arange(PLANE, dtype=jnp.int32)
    s, w, f = number // (RING * CORES), number // RING % CORES, number % RING
    core = (w + c) % CORES
    there_x = (x + jnp.where(core == 0, f, s)) % RING
    there_y = (y + jnp.where(core == 0, s, f)) % RING
    order = core * (RING * RING) + there_x * RING + there_y
    reads = [
        lax.dynamic_slice(
            read_lists,
            (((z + k) % RING * CORES + c) * (RING * RING) + gy, z * (PLANE * PER)),
            (1, PLANE * PER),
        )
        for k in range(RING)
    ]
    reads = jnp.concatenate(reads, axis=0).reshape(RING, PLANE, PER)
    ids = jnp.take(reads.transpose(1, 0, 2).reshape(PLANE, RING * PER), order, axis=0)

    lists = jnp.concatenate([sources, targets], axis=0)
    ring_lists = [lists] + [along_z(lists, k) for k in range(1, RING)]

    stacked = jnp.stack(ring_lists)
    slot, target = stacked[:, 0], stacked[:, 1]
    owner = slot // PER
    core = (owner // (RING * RING)) % CORES
    dx = (owner // RING - x) % RING
    dy = (owner - y) % RING
    s = jnp.where(core == 0, dy, dx)
    f = jnp.where(core == 0, dx, dy)
    column = ((s % 2 * CORES + (core + c) % CORES) * RING + f) * PER + slot % PER
    here = owner // PLANE == z
    row_codes = jnp.where(here, s // 2 * OCT + target, -1)
    per_dir = sources.shape[1] // DIRS
    counts, rest, flags = count(
        row_codes.reshape(RING * DIRS, per_dir), column.reshape(RING * DIRS, per_dir)
    )

    received, counts, rest, flags, ids = lax.optimization_barrier(
        (received, counts, rest, flags, ids)
    )
    octants = jnp.arange(OCT, dtype=jnp.int32)
    column_ids = lax.dynamic_slice_in_dim(partial_ids, device * per_owner, per_owner, 1).reshape(-1)
    selector = (octants[:, None] == column_ids[None, :]).astype(F32)
    density = jnp.dot(
        selector, received, precision=lax.Precision.HIGHEST, preferred_element_type=F32
    )

    line = lax.optimization_barrier([density] + [along_f(density, k) for k in range(1, RING)])
    low, high = jnp.concatenate(line[:2], axis=0), jnp.concatenate(line[2:], axis=0)
    low1, high3, high1, low3 = along_s(low, 1), along_s(high, 3), along_s(high, 1), along_s(low, 3)
    rows = {}
    (rows[0],) = gather((0,), ids, [low, high, across(low), across(high)])
    low1, high3, rows[0] = lax.optimization_barrier((low1, high3, rows[0]))
    low2, high2 = along_s(low1, 1), along_s(high3, 3)
    near = [low1, high1, across(low1), across(high1), low3, high3, across(low3), across(high3)]
    rows[1], rows[3] = gather((1, 3), ids, near)
    low2, high2, rows[1], rows[3] = lax.optimization_barrier((low2, high2, rows[1], rows[3]))
    far = [low2, high2, across(low2), across(high2)]
    last = (flags, ids, far, (rows[0], rows[1], rows[3]), counts, kernels, rest)
    out2, out1 = finish((2, 1), *last)
    out3, out0 = finish((3, 0), *last)
    return out0 + along_z(out2, -2) + along_z(out1, -1) + along_z(out3, -3)


def solution(mesh):
    return jax.shard_map(
        body,
        mesh=mesh,
        in_specs=(P(AXES, None), P(), P(), P(AXES, None), P(AXES, None), P()),
        out_specs=P(AXES, None),
        check_vma=False,
    )
```

time: 133 us -> 121 us (0.910)
  Pallas kernels: 62.3 us -> 32 us
  waiting for transfers between devices: 28.9 us -> 40.5 us
  local copies, waits for them, and re-layouts: 2.8 us -> 9.36 us
    pallas_call x4, Pallas kernels: 41.4 us -> 20.5 us  [the longest x2 18.5 us: finish(): pl.pallas_call(functools.partial(finish_kernel, readers), in_specs=[SMEM]...]
    pallas_call x1, Pallas kernels: 20.9 us -> 11.5 us  [count(): pl.pallas_call(count_kernel, grid=(RING,), in_specs=[pl.BlockSpec((steps,...]
    ppermute x23, waiting for transfers between devices: 24 us -> 32.6 us  [fetch(): return lax.ppermute(value, AXES, pairs)]
    unnamed x3 -> x14, local copies, waits for them, and re-layouts: 0.02 us -> 6.56 us
    all_to_all x1, waiting for transfers between devices: 4.94 us -> 7.89 us  [body(): lax.all_to_all(partials, AXES, split_axis=0, concat_axis=0, tiled=True)]
  transfers between devices with their start and end apart: 24 -> 24, of which waited for: 7 -> 13; matrix products, arithmetic and copies ran while one was open for 3% -> 3% of each run, Pallas kernels for 40% -> 19%
where the time goes in v1:
time: 121 us; the launch traced here: 120 us
  waiting for transfers between devices  40.5 us (33%)
  starting transfers between devices  34.4 us (28%)
  Pallas kernels  32 us (26%)
  local copies, waits for them, and re-layouts  9.36 us (8%)
  other arithmetic  2.56 us (2%)
    ppermute x23, waiting for transfers between devices, fetch(): return lax.ppermute(value, AXES, pairs)  32.6 us
    ppermute x23, starting transfers between devices, fetch(): return lax.ppermute(value, AXES, pairs)  24.6 us
    pallas_call x2, Pallas kernels, finish(): pl.pallas_call(functools.partial(finish_kernel, readers), in_specs=[SMEM]...  18.5 us
    pallas_call x1, Pallas kernels, count(): pl.pallas_call(count_kernel, grid=(RING,), in_specs=[pl.BlockSpec((steps,...  11.5 us
    all_to_all x1, starting transfers between devices, body(): lax.all_to_all(partials, AXES, split_axis=0, concat_axis=0, tiled=True)  9.74 us
    all_to_all x1, waiting for transfers between devices, body(): lax.all_to_all(partials, AXES, split_axis=0, concat_axis=0, tiled=True)  7.89 us
    unnamed x14, local copies, waits for them, and re-layouts  6.56 us
  transfers between devices with their start and end apart: 24, of which 13 were waited for; matrix products, arithmetic and copies ran while one was open for 3% of the time, Pallas kernels for 19%

profile of v1, /device:TPU:1, one launch (start us, length us, event | category | flops | bytes accessed | tf_op | source)
XLA Modules:
  0.0 120.1 jit_solution(6788844962547942104)
XLA Ops:
  0.0 0.9 fusion.48
  0.9 4.7 %collective-permute-start = (s32[2,8192]{1,0:T(2,128)S(1)}, s32[2,8192]{1,0:T(2,128)S(1)}, u32[]{:S(2)}, u32[]{:S(2)}) collective-permute-start(s32[2,8192]{1,0:T(2,128)S(1)} %get-tuple-element.64), channel_id=1, source_target_pairs={{32,0},{33,1},{34,2},{35,3},{36,4},{37,5},{38,6},{39,7},{40,8},{41... | collective-permute-start | bytes 196616 | tf_op jit(solution)/shard_map/ppermute | solution.py:40
  6.3 9.7 %all-to-all-start = ((f32[128,8,512]{2,1,0:T(8,128)}), f32[128,8,512]{2,1,0:T(8,128)S(1)}, u32[]{:S(2)}, u32[]{:S(2)}) async-start(f32[128,8,512]{2,1,0:T(8,128)} %bitcast.16), calls=%async_computation | async-start | bytes 4194304 | tf_op jit(solution)/shard_map/all_to_all | solution.py:240
  16.2 0.9 fusion.49
  19.9 11.5 %count.1 = (bf16[4,4,1024,256]{3,2,1,0:T(8,128)(2,1)S(1)}, bf16[4,4,1024,256]{3,2,1,0:T(8,128)(2,1)S(1)}, s32[4]{0:T(128)S(1)}) custom-call(s32[32,1024]{1,0:T(8,128)S(1)} %get-tuple-element.62.row_ref, s32[32,1024]{1,0:T(8,128)S(1)} %get-tuple-element.61.col_ref), custom_call_target="tpu_custom_call" | custom-call | flops 100000000 | bytes 1048576 | tf_op jit(solution)/shard_map/count/pallas_call | solution.py:105
  31.4 3.3 %copy-done.1 = bf16[4,4,1024,256]{3,2,1,0:T(8,128)(2,1)} copy-done((bf16[4,4,1024,256]{3,2,1,0:T(8,128)(2,1)}, bf16[4,4,1024,256]{3,2,1,0:T(8,128)(2,1)S(1)}, u32[]{:S(2)}) %copy-start.1) | copy-done | bytes 8388632
  34.6 3.2 %copy-done.3 = bf16[4,4,1024,256]{3,2,1,0:T(8,128)(2,1)} copy-done((bf16[4,4,1024,256]{3,2,1,0:T(8,128)(2,1)}, bf16[4,4,1024,256]{3,2,1,0:T(8,128)(2,1)S(1)}, u32[]{:S(2)}) %copy-start.3) | copy-done | bytes 8388632
  37.9 7.9 %all-to-all-done = f32[128,8,512]{2,1,0:T(8,128)S(1)} async-done(((f32[128,8,512]{2,1,0:T(8,128)}), f32[128,8,512]{2,1,0:T(8,128)S(1)}, u32[]{:S(2)}, u32[]{:S(2)}) %all-to-all-start) | async-done | bytes 2097184 | tf_op jit(solution)/shard_map/all_to_all | solution.py:240
  45.8 0.9 fusion
  46.7 1.9 %collective-permute-start.3 = (f32[128,512]{1,0:T(8,128)S(1)}, f32[128,512]{1,0:T(8,128)S(1)}, u32[]{:S(2)}, u32[]{:S(2)}) collective-permute-start(f32[128,512]{1,0:T(8,128)S(1)} %fusion), channel_id=1, source_target_pairs={{4,0},{5,1},{6,2},{7,3},{8,4},{9,5},{10,6},{11,7},{12,8},{13,9},{1... | collective-permute-start | bytes 786440 | tf_op jit(solution)/shard_map/ppermute | solution.py:40
  49.3 5.5 %collective-permute-done.3 = f32[128,512]{1,0:T(8,128)S(1)} collective-permute-done((f32[128,512]{1,0:T(8,128)S(1)}, f32[128,512]{1,0:T(8,128)S(1)}, u32[]{:S(2)}, u32[]{:S(2)}) %collective-permute-start.3) | collective-permute-done | bytes 262176 | tf_op jit(solution)/shard_map/ppermute | solution.py:40
  54.7 0.9 collective-permute-done.4
  55.7 2.8 %collective-permute-done.5 = f32[128,512]{1,0:T(8,128)S(1)} collective-permute-done((f32[128,512]{1,0:T(8,128)S(1)}, f32[128,512]{1,0:T(8,128)S(1)}, u32[]{:S(2)}, u32[]{:S(2)}) %collective-permute-start.5) | collective-permute-done | bytes 262176 | tf_op jit(solution)/shard_map/ppermute | solution.py:40
  59.7 2.2 %collective-permute-start.6 = (f32[256,512]{1,0:T(8,128)S(1)}, f32[256,512]{1,0:T(8,128)S(1)}, u32[]{:S(2)}, u32[]{:S(2)}) collective-permute-start(f32[256,512]{1,0:T(8,128)S(1)} %constant_dynamic-update-slice_fusion.refs_0_), channel_id=1, source_target_pairs={{1,0},{2,1},{3,2},{0,3},{5,4},{6,5},{7,6},{4,7},{9,8},{10,9},{11,1... | collective-permute-start | bytes 1572872 | tf_op jit(solution)/shard_map/ppermute | solution.py:40
  61.9 1.4 %collective-permute-start.15 = (f32[256,512]{1,0:T(8,128)S(1)}, f32[256,512]{1,0:T(8,128)S(1)}, u32[]{:S(2)}, u32[]{:S(2)}) collective-permute-start(f32[256,512]{1,0:T(8,128)S(1)} %constant_dynamic-update-slice_fusion.refs_0_), channel_id=1, source_target_pairs={{3,0},{0,1},{1,2},{2,3},{7,4},{4,5},{5,6},{6,7},{11,8},{8,9},{9,10... | collective-permute-start | bytes 1572872 | tf_op jit(solution)/shard_map/ppermute | solution.py:40
  64.2 4.6 %collective-permute-done.7.refs_5_ = f32[256,512]{1,0:T(8,128)S(1)} collective-permute-done((f32[256,512]{1,0:T(8,128)S(1)}, f32[256,512]{1,0:T(8,128)S(1)}, u32[]{:S(2)}, u32[]{:S(2)}) %collective-permute-start.7) | collective-permute-done | bytes 524320 | tf_op jit(solution)/shard_map/ppermute | solution.py:40
  68.8 1.3 %collective-permute-start.13 = (f32[256,512]{1,0:T(8,128)S(1)}, f32[256,512]{1,0:T(8,128)S(1)}, u32[]{:S(2)}, u32[]{:S(2)}) collective-permute-start(f32[256,512]{1,0:T(8,128)S(1)} %collective-permute-done.6.refs_0_), channel_id=1, source_target_pairs={{16,0},{17,1},{18,2},{19,3},{20,4},{21,5},{22,6},{23,7},{24,8},{25... | collective-permute-start | bytes 1572872 | tf_op jit(solution)/shard_map/ppermute | solution.py:40
  70.1 3.6 %collective-permute-done.12.refs_1_ = f32[256,512]{1,0:T(8,128)S(1)} collective-permute-done((f32[256,512]{1,0:T(8,128)S(1)}, f32[256,512]{1,0:T(8,128)S(1)}, u32[]{:S(2)}, u32[]{:S(2)}) %collective-permute-start.12) | collective-permute-done | bytes 524320 | tf_op jit(solution)/shard_map/ppermute | solution.py:40
  73.7 1.7 %collective-permute-start.14 = (f32[256,512]{1,0:T(8,128)S(1)}, f32[256,512]{1,0:T(8,128)S(1)}, u32[]{:S(2)}, u32[]{:S(2)}) collective-permute-start(f32[256,512]{1,0:T(8,128)S(1)} %collective-permute-done.12.refs_1_), channel_id=1, source_target_pairs={{16,0},{17,1},{18,2},{19,3},{20,4},{21,5},{22,6},{23,7},{24,8},{25... | collective-permute-start | bytes 1572872 | tf_op jit(solution)/shard_map/ppermute | solution.py:40
  75.7 1.6 %collective-permute-start.10 = (f32[256,512]{1,0:T(8,128)S(1)}, f32[256,512]{1,0:T(8,128)S(1)}, u32[]{:S(2)}, u32[]{:S(2)}) collective-permute-start(f32[256,512]{1,0:T(8,128)S(1)} %collective-permute-done.6.refs_0_), channel_id=1, source_target_pairs={{1,0},{2,1},{3,2},{0,3},{5,4},{6,5},{7,6},{4,7},{9,8},{10,9},{11,1... | collective-permute-start | bytes 1572872 | tf_op jit(solution)/shard_map/ppermute | solution.py:40
  77.7 1.3 %gather.10 = (bf16[4,256,1024]{2,1,0:T(8,128)(2,1)S(1)}, bf16[4,256,1024]{2,1,0:T(8,128)(2,1)S(1)}) custom-call(s32[32,128]{1,0:T(8,128)S(1)} %broadcast_select_fusion.ids_ref, f32[256,512]{1,0:T(8,128)S(1)} %collective-permute-done.6.refs_0_, f32[256,512]{1,0:T(8,128)S(1)} %collective-permute-done.12.refs_1_, ...), custom_call_target="tpu_custom_call" | custom-call | flops 3000000000 | bytes 2097152 | tf_op jit(solution)/shard_map/gather/pallas_call | solution.py:151
  79.0 5.0 %collective-permute-done.10.b0 = f32[256,512]{1,0:T(8,128)S(1)} collective-permute-done((f32[256,512]{1,0:T(8,128)S(1)}, f32[256,512]{1,0:T(8,128)S(1)}, u32[]{:S(2)}, u32[]{:S(2)}) %collective-permute-start.10) | collective-permute-done | bytes 524320 | tf_op jit(solution)/shard_map/ppermute | solution.py:40
  84.0 2.8 %collective-permute-done.11.b1 = f32[256,512]{1,0:T(8,128)S(1)} collective-permute-done((f32[256,512]{1,0:T(8,128)S(1)}, f32[256,512]{1,0:T(8,128)S(1)}, u32[]{:S(2)}, u32[]{:S(2)}) %collective-permute-start.11) | collective-permute-done | bytes 524320 | tf_op jit(solution)/shard_map/ppermute | solution.py:40
  86.8 3.0 %collective-permute-start.18 = (f32[256,512]{1,0:T(8,128)S(1)}, f32[256,512]{1,0:T(8,128)S(1)}, u32[]{:S(2)}, u32[]{:S(2)}) collective-permute-start(f32[256,512]{1,0:T(8,128)S(1)} %collective-permute-done.10.b0), channel_id=1, source_target_pairs={{16,0},{17,1},{18,2},{19,3},{20,4},{21,5},{22,6},{23,7},{24,8},{25... | collective-permute-start | bytes 1572872 | tf_op jit(solution)/shard_map/ppermute | solution.py:40
  89.8 1.5 %collective-permute-done.18.b2 = f32[256,512]{1,0:T(8,128)S(1)} collective-permute-done((f32[256,512]{1,0:T(8,128)S(1)}, f32[256,512]{1,0:T(8,128)S(1)}, u32[]{:S(2)}, u32[]{:S(2)}) %collective-permute-start.18) | collective-permute-done | bytes 524320 | tf_op jit(solution)/shard_map/ppermute | solution.py:40
  92.1 9.2 %finish.3 = (f32[128,512]{1,0:T(8,128)S(1)}, f32[128,512]{1,0:T(8,128)S(1)}) custom-call(s32[4]{0:T(128)S(1)} %get-tuple-element.33.flag_ref, s32[32,128]{1,0:T(8,128)S(1)} %broadcast_select_fusion.ids_ref, f32[256,512]{1,0:T(8,128)S(1)} %collective-permute-done.10.b0, f32[256,512]{1,0:T(8,128)S(1)} %collective-permute-done.11.b1, ...), custom_call_target="tpu_custom_call" | custom-call | flops 8999999488 | bytes 2097152 | tf_op jit(solution)/shard_map/finish/pallas_call | solution.py:214
  101.4 1.2 collective-permute-start.20
  103.1 9.2 %finish.2 = (f32[128,512]{1,0:T(8,128)S(1)}, f32[128,512]{1,0:T(8,128)S(1)}) custom-call(s32[4]{0:T(128)S(1)} %get-tuple-element.33.flag_ref, s32[32,128]{1,0:T(8,128)S(1)} %broadcast_select_fusion.ids_ref, f32[256,512]{1,0:T(8,128)S(1)} %collective-permute-done.10.b0, f32[256,512]{1,0:T(8,128)S(1)} %collective-permute-done.11.b1, ...), custom_call_target="tpu_custom_call" | custom-call | flops 8999999488 | bytes 2097152 | tf_op jit(solution)/shard_map/finish/pallas_call | solution.py:214
  112.4 2.2 %collective-permute-start.22 = (f32[128,512]{1,0:T(8,128)S(1)}, f32[128,512]{1,0:T(8,128)S(1)}, u32[]{:S(2)}, u32[]{:S(2)}) collective-permute-start(f32[128,512]{1,0:T(8,128)S(1)} %get-tuple-element.54), channel_id=1, source_target_pairs={{32,0},{33,1},{34,2},{35,3},{36,4},{37,5},{38,6},{39,7},{40,8},{41... | collective-permute-start | bytes 786440 | tf_op jit(solution)/shard_map/ppermute | solution.py:40
  114.6 2.2 %collective-permute-done.21 = f32[128,512]{1,0:T(8,128)S(1)} collective-permute-done((f32[128,512]{1,0:T(8,128)S(1)}, f32[128,512]{1,0:T(8,128)S(1)}, u32[]{:S(2)}, u32[]{:S(2)}) %collective-permute-start.21) | collective-permute-done | bytes 262176 | tf_op jit(solution)/shard_map/ppermute | solution.py:40
  116.8 2.5 %collective-permute-done.22 = f32[128,512]{1,0:T(8,128)S(1)} collective-permute-done((f32[128,512]{1,0:T(8,128)S(1)}, f32[128,512]{1,0:T(8,128)S(1)}, u32[]{:S(2)}, u32[]{:S(2)}) %collective-permute-start.22) | collective-permute-done | bytes 262176 | tf_op jit(solution)/shard_map/ppermute | solution.py:40
  119.3 0.8 add_add_fusion
  (58 shorter events, 8.1 us)
Async XLA Ops:
  0.0 18.1 %copy-start = (s32[128,1024]{1,0:T(8,128)S(1)}, s32[128,1024]{1,0:T(8,128)}, u32[]{:S(2)}) copy-start(s32[128,1024]{1,0:T(8,128)} %param.7) | copy-start | bytes 1572868
  0.9 17.4 %collective-permute-start = (s32[2,8192]{1,0:T(2,128)S(1)}, s32[2,8192]{1,0:T(2,128)S(1)}, u32[]{:S(2)}, u32[]{:S(2)}) collective-permute-start(s32[2,8192]{1,0:T(2,128)S(1)} %get-tuple-element.64), channel_id=1, source_target_pairs={{32,0},{33,1},{34,2},{35,3},{36,4},{37,5},{38,6},{39,7},{40,8},{41... | collective-permute-start | bytes 196616 | tf_op jit(solution)/shard_map/ppermute | solution.py:40
  5.6 12.7 %collective-permute-start.1 = (s32[2,8192]{1,0:T(2,128)S(1)}, s32[2,8192]{1,0:T(2,128)S(1)}, u32[]{:S(2)}, u32[]{:S(2)}) collective-permute-start(s32[2,8192]{1,0:T(2,128)S(1)} %get-tuple-element.64), channel_id=1, source_target_pairs={{64,0},{65,1},{66,2},{67,3},{68,4},{69,5},{70,6},{71,7},{72,8},{73... | collective-permute-start | bytes 196616 | tf_op jit(solution)/shard_map/ppermute | solution.py:40
  5.6 12.7 %collective-permute-start.2 = (s32[2,8192]{1,0:T(2,128)S(1)}, s32[2,8192]{1,0:T(2,128)S(1)}, u32[]{:S(2)}, u32[]{:S(2)}) collective-permute-start(s32[2,8192]{1,0:T(2,128)S(1)} %get-tuple-element.64), channel_id=1, source_target_pairs={{96,0},{97,1},{98,2},{99,3},{100,4},{101,5},{102,6},{103,7},{104,8... | collective-permute-start | bytes 196616 | tf_op jit(solution)/shard_map/ppermute | solution.py:40
  6.3 39.5 %all-to-all-start = ((f32[128,8,512]{2,1,0:T(8,128)}), f32[128,8,512]{2,1,0:T(8,128)S(1)}, u32[]{:S(2)}, u32[]{:S(2)}) async-start(f32[128,8,512]{2,1,0:T(8,128)} %bitcast.16), calls=%async_computation | async-start | bytes 4194304 | tf_op jit(solution)/shard_map/all_to_all | solution.py:240
  31.4 3.3 %copy-start.1 = (bf16[4,4,1024,256]{3,2,1,0:T(8,128)(2,1)}, bf16[4,4,1024,256]{3,2,1,0:T(8,128)(2,1)S(1)}, u32[]{:S(2)}) copy-start(bf16[4,4,1024,256]{3,2,1,0:T(8,128)(2,1)S(1)} %get-tuple-element.49.count_ref) | copy-start | bytes 25165828
  34.6 3.2 %copy-start.3 = (bf16[4,4,1024,256]{3,2,1,0:T(8,128)(2,1)}, bf16[4,4,1024,256]{3,2,1,0:T(8,128)(2,1)S(1)}, u32[]{:S(2)}) copy-start(bf16[4,4,1024,256]{3,2,1,0:T(8,128)(2,1)S(1)} %get-tuple-element.50.rest_hbm) | copy-start | bytes 25165828
  46.7 8.1 %collective-permute-start.3 = (f32[128,512]{1,0:T(8,128)S(1)}, f32[128,512]{1,0:T(8,128)S(1)}, u32[]{:S(2)}, u32[]{:S(2)}) collective-permute-start(f32[128,512]{1,0:T(8,128)S(1)} %fusion), channel_id=1, source_target_pairs={{4,0},{5,1},{6,2},{7,3},{8,4},{9,5},{10,6},{11,7},{12,8},{13,9},{1... | collective-permute-start | bytes 786440 | tf_op jit(solution)/shard_map/ppermute | solution.py:40
  48.6 7.1 %collective-permute-start.4 = (f32[128,512]{1,0:T(8,128)S(1)}, f32[128,512]{1,0:T(8,128)S(1)}, u32[]{:S(2)}, u32[]{:S(2)}) collective-permute-start(f32[128,512]{1,0:T(8,128)S(1)} %fusion), channel_id=1, source_target_pairs={{8,0},{9,1},{10,2},{11,3},{12,4},{13,5},{14,6},{15,7},{0,8},{1,9},... | collective-permute-start | bytes 786440 | tf_op jit(solution)/shard_map/ppermute | solution.py:40
  49.1 9.4 %collective-permute-start.5 = (f32[128,512]{1,0:T(8,128)S(1)}, f32[128,512]{1,0:T(8,128)S(1)}, u32[]{:S(2)}, u32[]{:S(2)}) collective-permute-start(f32[128,512]{1,0:T(8,128)S(1)} %fusion), channel_id=1, source_target_pairs={{12,0},{13,1},{14,2},{15,3},{0,4},{1,5},{2,6},{3,7},{4,8},{5,9},{6... | collective-permute-start | bytes 786440 | tf_op jit(solution)/shard_map/ppermute | solution.py:40
  58.5 3.5 %collective-permute-start.9 = (f32[256,512]{1,0:T(8,128)S(1)}, f32[256,512]{1,0:T(8,128)S(1)}, u32[]{:S(2)}, u32[]{:S(2)}) collective-permute-start(f32[256,512]{1,0:T(8,128)S(1)} %constant_dynamic-update-slice_fusion.2.refs_1_), channel_id=1, source_target_pairs={{16,0},{17,1},{18,2},{19,3},{20,4},{21,5},{22,6},{23,7},{24,8},{25... | collective-permute-start | bytes 1572872 | tf_op jit(solution)/shard_map/ppermute | solution.py:40
  59.0 33.1 %copy-start.2 = (bf16[4,4,1024,256]{3,2,1,0:T(8,128)(2,1)S(1)}, bf16[4,4,1024,256]{3,2,1,0:T(8,128)(2,1)}, u32[]{:S(2)}) copy-start(bf16[4,4,1024,256]{3,2,1,0:T(8,128)(2,1)} %copy-done.1) | copy-start | bytes 25165828
  59.1 4.3 %collective-permute-start.8 = (f32[256,512]{1,0:T(8,128)S(1)}, f32[256,512]{1,0:T(8,128)S(1)}, u32[]{:S(2)}, u32[]{:S(2)}) collective-permute-start(f32[256,512]{1,0:T(8,128)S(1)} %constant_dynamic-update-slice_fusion.refs_0_), channel_id=1, source_target_pairs={{16,0},{17,1},{18,2},{19,3},{20,4},{21,5},{22,6},{23,7},{24,8},{25... | collective-permute-start | bytes 1572872 | tf_op jit(solution)/shard_map/ppermute | solution.py:40
  59.2 9.5 %collective-permute-start.7 = (f32[256,512]{1,0:T(8,128)S(1)}, f32[256,512]{1,0:T(8,128)S(1)}, u32[]{:S(2)}, u32[]{:S(2)}) collective-permute-start(f32[256,512]{1,0:T(8,128)S(1)} %constant_dynamic-update-slice_fusion.2.refs_1_), channel_id=1, source_target_pairs={{3,0},{0,1},{1,2},{2,3},{7,4},{4,5},{5,6},{6,7},{11,8},{8,9},{9,10... | collective-permute-start | bytes 1572872 | tf_op jit(solution)/shard_map/ppermute | solution.py:40
  59.7 9.1 %collective-permute-start.6 = (f32[256,512]{1,0:T(8,128)S(1)}, f32[256,512]{1,0:T(8,128)S(1)}, u32[]{:S(2)}, u32[]{:S(2)}) collective-permute-start(f32[256,512]{1,0:T(8,128)S(1)} %constant_dynamic-update-slice_fusion.refs_0_), channel_id=1, source_target_pairs={{1,0},{2,1},{3,2},{0,3},{5,4},{6,5},{7,6},{4,7},{9,8},{10,9},{11,1... | collective-permute-start | bytes 1572872 | tf_op jit(solution)/shard_map/ppermute | solution.py:40
  61.9 11.7 %collective-permute-start.12 = (f32[256,512]{1,0:T(8,128)S(1)}, f32[256,512]{1,0:T(8,128)S(1)}, u32[]{:S(2)}, u32[]{:S(2)}) collective-permute-start(f32[256,512]{1,0:T(8,128)S(1)} %constant_dynamic-update-slice_fusion.2.refs_1_), channel_id=1, source_target_pairs={{1,0},{2,1},{3,2},{0,3},{5,4},{6,5},{7,6},{4,7},{9,8},{10,9},{11,1... | collective-permute-start | bytes 1572872 | tf_op jit(solution)/shard_map/ppermute | solution.py:40
  61.9 13.4 %collective-permute-start.15 = (f32[256,512]{1,0:T(8,128)S(1)}, f32[256,512]{1,0:T(8,128)S(1)}, u32[]{:S(2)}, u32[]{:S(2)}) collective-permute-start(f32[256,512]{1,0:T(8,128)S(1)} %constant_dynamic-update-slice_fusion.refs_0_), channel_id=1, source_target_pairs={{3,0},{0,1},{1,2},{2,3},{7,4},{4,5},{5,6},{6,7},{11,8},{8,9},{9,10... | collective-permute-start | bytes 1572872 | tf_op jit(solution)/shard_map/ppermute | solution.py:40
  63.4 28.7 %slice-start = ((s8[8388608]{0:T(1024)(128)(4,1)}), s8[4194304]{0:T(1024)(128)(4,1)S(1)}, s32[]{:S(2)}) async-start(s8[8388608]{0:T(1024)(128)(4,1)} %bitcast.13), calls=%async_computation.1 | async-start | bytes 8388608
  64.1 28.0 %slice-start.1 = ((s8[8388608]{0:T(1024)(128)(4,1)}), s8[4194304]{0:T(1024)(128)(4,1)S(1)}, s32[]{:S(2)}) async-start(s8[8388608]{0:T(1024)(128)(4,1)} %bitcast.13), calls=%async_computation.2 | async-start | bytes 8388608
  68.8 8.5 %collective-permute-start.13 = (f32[256,512]{1,0:T(8,128)S(1)}, f32[256,512]{1,0:T(8,128)S(1)}, u32[]{:S(2)}, u32[]{:S(2)}) collective-permute-start(f32[256,512]{1,0:T(8,128)S(1)} %collective-permute-done.6.refs_0_), channel_id=1, source_target_pairs={{16,0},{17,1},{18,2},{19,3},{20,4},{21,5},{22,6},{23,7},{24,8},{25... | collective-permute-start | bytes 1572872 | tf_op jit(solution)/shard_map/ppermute | solution.py:40
  70.1 7.2 %collective-permute-start.17 = (f32[256,512]{1,0:T(8,128)S(1)}, f32[256,512]{1,0:T(8,128)S(1)}, u32[]{:S(2)}, u32[]{:S(2)}) collective-permute-start(f32[256,512]{1,0:T(8,128)S(1)} %collective-permute-done.7.refs_5_), channel_id=1, source_target_pairs={{16,0},{17,1},{18,2},{19,3},{20,4},{21,5},{22,6},{23,7},{24,8},{25... | collective-permute-start | bytes 1572872 | tf_op jit(solution)/shard_map/ppermute | solution.py:40
  73.7 3.6 %collective-permute-start.14 = (f32[256,512]{1,0:T(8,128)S(1)}, f32[256,512]{1,0:T(8,128)S(1)}, u32[]{:S(2)}, u32[]{:S(2)}) collective-permute-start(f32[256,512]{1,0:T(8,128)S(1)} %collective-permute-done.12.refs_1_), channel_id=1, source_target_pairs={{16,0},{17,1},{18,2},{19,3},{20,4},{21,5},{22,6},{23,7},{24,8},{25... | collective-permute-start | bytes 1572872 | tf_op jit(solution)/shard_map/ppermute | solution.py:40
  75.4 2.3 %collective-permute-start.16 = (f32[256,512]{1,0:T(8,128)S(1)}, f32[256,512]{1,0:T(8,128)S(1)}, u32[]{:S(2)}, u32[]{:S(2)}) collective-permute-start(f32[256,512]{1,0:T(8,128)S(1)} %collective-permute-done.15.refs_4_), channel_id=1, source_target_pairs={{16,0},{17,1},{18,2},{19,3},{20,4},{21,5},{22,6},{23,7},{24,8},{25... | collective-permute-start | bytes 1572872 | tf_op jit(solution)/shard_map/ppermute | solution.py:40
  75.7 8.3 %collective-permute-start.10 = (f32[256,512]{1,0:T(8,128)S(1)}, f32[256,512]{1,0:T(8,128)S(1)}, u32[]{:S(2)}, u32[]{:S(2)}) collective-permute-start(f32[256,512]{1,0:T(8,128)S(1)} %collective-permute-done.6.refs_0_), channel_id=1, source_target_pairs={{1,0},{2,1},{3,2},{0,3},{5,4},{6,5},{7,6},{4,7},{9,8},{10,9},{11,1... | collective-permute-start | bytes 1572872 | tf_op jit(solution)/shard_map/ppermute | solution.py:40
  77.3 9.5 %collective-permute-start.11 = (f32[256,512]{1,0:T(8,128)S(1)}, f32[256,512]{1,0:T(8,128)S(1)}, u32[]{:S(2)}, u32[]{:S(2)}) collective-permute-start(f32[256,512]{1,0:T(8,128)S(1)} %collective-permute-done.7.refs_5_), channel_id=1, source_target_pairs={{3,0},{0,1},{1,2},{2,3},{7,4},{4,5},{5,6},{6,7},{11,8},{8,9},{9,10... | collective-permute-start | bytes 1572872 | tf_op jit(solution)/shard_map/ppermute | solution.py:40
  86.8 4.5 %collective-permute-start.18 = (f32[256,512]{1,0:T(8,128)S(1)}, f32[256,512]{1,0:T(8,128)S(1)}, u32[]{:S(2)}, u32[]{:S(2)}) collective-permute-start(f32[256,512]{1,0:T(8,128)S(1)} %collective-permute-done.10.b0), channel_id=1, source_target_pairs={{16,0},{17,1},{18,2},{19,3},{20,4},{21,5},{22,6},{23,7},{24,8},{25... | collective-permute-start | bytes 1572872 | tf_op jit(solution)/shard_map/ppermute | solution.py:40
  89.8 2.3 %collective-permute-start.19 = (f32[256,512]{1,0:T(8,128)S(1)}, f32[256,512]{1,0:T(8,128)S(1)}, u32[]{:S(2)}, u32[]{:S(2)}) collective-permute-start(f32[256,512]{1,0:T(8,128)S(1)} %collective-permute-done.11.b1), channel_id=1, source_target_pairs={{16,0},{17,1},{18,2},{19,3},{20,4},{21,5},{22,6},{23,7},{24,8},{25... | collective-permute-start | bytes 1572872 | tf_op jit(solution)/shard_map/ppermute | solution.py:40
  101.4 13.2 %collective-permute-start.20 = (f32[128,512]{1,0:T(8,128)S(1)}, f32[128,512]{1,0:T(8,128)S(1)}, u32[]{:S(2)}, u32[]{:S(2)}) collective-permute-start(f32[128,512]{1,0:T(8,128)S(1)} %get-tuple-element.52), channel_id=1, source_target_pairs={{64,0},{65,1},{66,2},{67,3},{68,4},{69,5},{70,6},{71,7},{72,8},{73... | collective-permute-start | bytes 786440 | tf_op jit(solution)/shard_map/ppermute | solution.py:40
  102.5 14.3 %collective-permute-start.21 = (f32[128,512]{1,0:T(8,128)S(1)}, f32[128,512]{1,0:T(8,128)S(1)}, u32[]{:S(2)}, u32[]{:S(2)}) collective-permute-start(f32[128,512]{1,0:T(8,128)S(1)} %get-tuple-element.53), channel_id=1, source_target_pairs={{96,0},{97,1},{98,2},{99,3},{100,4},{101,5},{102,6},{103,7},{104,8... | collective-permute-start | bytes 786440 | tf_op jit(solution)/shard_map/ppermute | solution.py:40
  112.4 6.9 %collective-permute-start.22 = (f32[128,512]{1,0:T(8,128)S(1)}, f32[128,512]{1,0:T(8,128)S(1)}, u32[]{:S(2)}, u32[]{:S(2)}) collective-permute-start(f32[128,512]{1,0:T(8,128)S(1)} %get-tuple-element.54), channel_id=1, source_target_pairs={{32,0},{33,1},{34,2},{35,3},{36,4},{37,5},{38,6},{39,7},{40,8},{41... | collective-permute-start | bytes 786440 | tf_op jit(solution)/shard_map/ppermute | solution.py:40

commit v2 on v1

--- a/solution.py
+++ b/solution.py
@@ -16,13 +16,12 @@
 WIDTH = 512
 PLANE = RING * RING * CORES
 BLOCK = CORES * RING * PER
-HALF = RING // 2 * OCT
 BF16 = jnp.bfloat16
 F32 = jnp.float32
 HBM = pl.BlockSpec(memory_space=pltpu.HBM)
 SMEM = pl.BlockSpec(memory_space=pltpu.SMEM)
 VMEM = pl.BlockSpec(memory_space=pltpu.VMEM)
-LIMIT = 24
+LIMIT = 16
 
 
 def device_of(x, y, z, c):
@@ -113,7 +112,7 @@
             jax.ShapeDtypeStruct((RING,), jnp.int32),
         ],
         scratch_shapes=[pltpu.VMEM((RING, OCT, BLOCK), BF16)],
-        compiler_params=pltpu.CompilerParams(vmem_limit_bytes=20 << 20),
+        compiler_params=pltpu.CompilerParams(vmem_limit_bytes=60 << 20),
         cost_estimate=pl.CostEstimate(
             flops=100_000_000, bytes_accessed=1 << 20, transcendentals=0
         ),
@@ -124,8 +123,8 @@
 def pick(ids_ref, first, refs, store):
     octants = lax.broadcasted_iota(jnp.int32, (OCT, RING * PER), 0)
     for i, ref in enumerate(refs):
-        for j in range(2):
-            owner = 2 * i + j
+        for j in range(RING):
+            owner = RING * i + j
             table = jnp.concatenate(parts(ref[j * OCT : (j + 1) * OCT, :]), axis=1)
             hot = jnp.where(octants == ids_ref[first + owner : first + owner + 1, :], 1.0, 0.0)
             picked = lax.dot_general(
@@ -138,19 +137,19 @@
 def gather_kernel(blocks, ids_ref, *refs):
     n = len(blocks)
     for i, s in enumerate(blocks):
-        rows = refs[4 * n + i]
+        rows = refs[2 * n + i]
 
         def store(owner, k, values, rows=rows):
             rows[k, owner * PER : (owner + 1) * PER, :] = values
 
-        pick(ids_ref, s * 2 * RING, refs[4 * i : 4 * i + 4], store)
+        pick(ids_ref, s * 2 * RING, refs[2 * i : 2 * i + 2], store)
 
 
 def gather(blocks, ids, arrays):
     n = len(blocks)
     return pl.pallas_call(
         functools.partial(gather_kernel, blocks),
-        in_specs=[VMEM] * (1 + 4 * n),
+        in_specs=[VMEM] * (1 + 2 * n),
         out_specs=[VMEM] * n,
         out_shape=[jax.ShapeDtypeStruct((RING, BLOCK, 2 * WIDTH), BF16)] * n,
         compiler_params=pltpu.CompilerParams(vmem_limit_bytes=16 << 20),
@@ -161,26 +160,57 @@
     )(ids, *arrays)
 
 
+def product(counts, rows):
+    both = jnp.dot(
+        jnp.concatenate(counts, axis=1),
+        jnp.concatenate(rows, axis=0),
+        preferred_element_type=F32,
+    )
+    return both[:, :WIDTH] + both[:, WIDTH:]
+
+
+def collect_kernel(blocks, count_ref, *refs):
+    rows, out_ref = refs[:-1], refs[-1]
+
+    @pl.loop(0, RING)
+    def _(k):
+        for m in range(0, DIRS, 2):
+            here = slice(m * OCT, (m + 2) * OCT)
+            out_ref[k, here, :] = product(
+                [count_ref[s, k, here, :] for s in blocks], [ref[k] for ref in rows]
+            )
+
+
+def collect(blocks, counts, rows):
+    n = len(blocks)
+    return pl.pallas_call(
+        functools.partial(collect_kernel, blocks),
+        in_specs=[VMEM] * (1 + n),
+        out_specs=VMEM,
+        out_shape=jax.ShapeDtypeStruct((RING, DIRS * OCT, WIDTH), F32),
+        compiler_params=pltpu.CompilerParams(vmem_limit_bytes=8 << 20),
+        cost_estimate=pl.CostEstimate(
+            flops=n * 2_200_000_000, bytes_accessed=n << 20, transcendentals=0
+        ),
+        name="collect",
+    )(counts, *rows)
+
+
 def finish_kernel(
-    readers, flag_ref, ids_ref, b0, b1, b2, b3, rows0, rows1, rows3, count_ref, k_ref, rest_hbm,
+    readers, flag_ref, ids_ref, b0, b1, x_ref, rows0, rows1, rows3, count_ref, k_ref, rest_hbm,
     out0, out1,
     rows2, xh, xl, rest,
 ):
     def store(owner, k, values):
         rows2[k, owner * PER : (owner + 1) * PER, :] = values
 
-    pick(ids_ref, 2 * 2 * RING, (b0, b1, b2, b3), store)
-
-    def product(counts, k):
-        rows = jnp.concatenate([ref[k] for ref in (rows0, rows1, rows2, rows3)], axis=0)
-        both = jnp.dot(jnp.concatenate(counts, axis=1), rows, preferred_element_type=F32)
-        return both[:, :WIDTH] + both[:, WIDTH:]
-
+    pick(ids_ref, 2 * 2 * RING, (b0, b1), store)
     for i, k in enumerate(readers):
         there = slice(i * OCT, (i + 1) * OCT)
         for m in range(0, DIRS, 2):
             here = slice(m * OCT, (m + 2) * OCT)
-            high, low = parts(product([count_ref[s, k, here, :] for s in range(RING)], k))
+            total = x_ref[k, here, :] + product([count_ref[2, k, here, :]], [rows2[k]])
+            high, low = parts(total)
             for j in range(2):
                 xh[m + j, there, :] = high[j * OCT : (j + 1) * OCT]
                 xl[m + j, there, :] = low[j * OCT : (j + 1) * OCT]
@@ -191,7 +221,8 @@
             def _(d):
                 start = pl.multiple_of(d * OCT, OCT)
                 pltpu.sync_copy(rest_hbm.at[:, k, pl.ds(start, OCT), :], rest)
-                total = product([rest[s] for s in range(RING)], k)
+                rows = [ref[k] for ref in (rows0, rows1, rows2, rows3)]
+                total = product([rest[s] for s in range(RING)], rows)
                 total += xh[d, there, :].astype(F32) + xl[d, there, :].astype(F32)
                 high, low = parts(total)
                 xh[d, there, :] = high
@@ -209,11 +240,11 @@
         out[...] = total[i * OCT : (i + 1) * OCT]
 
 
-def finish(readers, flags, ids, arrays, rows, counts, kernels, rest):
+def finish(readers, flags, ids, arrays, x, rows, counts, kernels, rest):
     n = len(readers)
     return pl.pallas_call(
         functools.partial(finish_kernel, readers),
-        in_specs=[SMEM] + [VMEM] * 10 + [HBM],
+        in_specs=[SMEM] + [VMEM] * 9 + [HBM],
         out_specs=[VMEM] * 2,
         out_shape=[jax.ShapeDtypeStruct((OCT, WIDTH), F32)] * 2,
         scratch_shapes=[
@@ -224,10 +255,10 @@
         ],
         compiler_params=pltpu.CompilerParams(vmem_limit_bytes=LIMIT << 20),
         cost_estimate=pl.CostEstimate(
-            flops=9_000_000_000, bytes_accessed=2 << 20, transcendentals=0
+            flops=6_000_000_000, bytes_accessed=2 << 20, transcendentals=0
         ),
         name="finish",
-    )(flags, ids, *arrays, *rows, counts, kernels, rest)
+    )(flags, ids, *arrays, x, *rows, counts, kernels, rest)
 
 
 def body(partials, partial_ids, read_lists, sources, targets, kernels):
@@ -275,9 +306,6 @@
         row_codes.reshape(RING * DIRS, per_dir), column.reshape(RING * DIRS, per_dir)
     )
 
-    received, counts, rest, flags, ids = lax.optimization_barrier(
-        (received, counts, rest, flags, ids)
-    )
     octants = jnp.arange(OCT, dtype=jnp.int32)
     column_ids = lax.dynamic_slice_in_dim(partial_ids, device * per_owner, per_owner, 1).reshape(-1)
     selector = (octants[:, None] == column_ids[None, :]).astype(F32)
@@ -285,18 +313,21 @@
         selector, received, precision=lax.Precision.HIGHEST, preferred_element_type=F32
     )
 
-    line = lax.optimization_barrier([density] + [along_f(density, k) for k in range(1, RING)])
-    low, high = jnp.concatenate(line[:2], axis=0), jnp.concatenate(line[2:], axis=0)
-    low1, high3, high1, low3 = along_s(low, 1), along_s(high, 3), along_s(high, 1), along_s(low, 3)
+    line = [density] + [along_f(density, k) for k in range(1, RING)]
+    line, counts, rest, flags, ids = lax.optimization_barrier((line, counts, rest, flags, ids))
+    line = jnp.concatenate(line, axis=0)
+    block = {1: along_s(line, 1), 3: along_s(line, 3)}
     rows = {}
-    (rows[0],) = gather((0,), ids, [low, high, across(low), across(high)])
-    low1, high3, rows[0] = lax.optimization_barrier((low1, high3, rows[0]))
-    low2, high2 = along_s(low1, 1), along_s(high3, 3)
-    near = [low1, high1, across(low1), across(high1), low3, high3, across(low3), across(high3)]
+    (rows[0],) = gather((0,), ids, [line, across(line)])
+    line, rows[0] = lax.optimization_barrier((line, rows[0]))
+    block[2] = along_s(line, 2)
+    near = [block[1], across(block[1]), block[3], across(block[3])]
     rows[1], rows[3] = gather((1, 3), ids, near)
-    low2, high2, rows[1], rows[3] = lax.optimization_barrier((low2, high2, rows[1], rows[3]))
-    far = [low2, high2, across(low2), across(high2)]
-    last = (flags, ids, far, (rows[0], rows[1], rows[3]), counts, kernels, rest)
+    rows = (rows[0], rows[1], rows[3])
+    x = collect((0, 1, 3), counts, rows)
+    block[2], x = lax.optimization_barrier((block[2], x))
+    far = [block[2], across(block[2])]
+    last = (flags, ids, far, x, rows, counts, kernels, rest)
     out2, out1 = finish((2, 1), *last)
     out3, out0 = finish((3, 0), *last)
     return out0 + along_z(out2, -2) + along_z(out1, -1) + along_z(out3, -3)

time: 121 us -> 120 us (level)
  local copies, waits for them, and re-layouts: 9.36 us -> 2.86 us
  waiting for transfers between devices: 40.5 us -> 46.6 us
  Pallas kernels: 32 us -> 34.4 us
  starting transfers between devices: 34.4 us -> 32.6 us
    ppermute x23 -> x16, waiting for transfers between devices: 32.6 us -> 46.5 us  [fetch(): return lax.ppermute(value, AXES, pairs)]
    all_to_all x1, waiting for transfers between devices: 7.89 us -> 0.09 us  [body(): lax.all_to_all(partials, AXES, split_axis=0, concat_axis=0, tiled=True)]
    pallas_call x0 -> x1, Pallas kernels: none -> 7.16 us  [collect(): pl.pallas_call(functools.partial(collect_kernel, blocks), in_specs=[VMEM]...]
    unnamed x14 -> x19, local copies, waits for them, and re-layouts: 6.56 us -> 0.1 us
    pallas_call x2, Pallas kernels: 18.5 us -> 12.5 us  [finish(): pl.pallas_call(functools.partial(finish_kernel, readers), in_specs=[SMEM]...]
    ppermute x23 -> x16, starting transfers between devices: 24.6 us -> 21.1 us  [fetch(): return lax.ppermute(value, AXES, pairs)]
    all_to_all x1, starting transfers between devices: 9.74 us -> 11.5 us  [body(): lax.all_to_all(partials, AXES, split_axis=0, concat_axis=0, tiled=True)]
    pallas_call x1, Pallas kernels: 11.5 us -> 12.7 us  [count(): pl.pallas_call(count_kernel, grid=(RING,), in_specs=[pl.BlockSpec((steps,...]
  transfers between devices with their start and end apart: 24 -> 17, of which waited for: 13 -> 8; matrix products, arithmetic and copies ran while one was open for 3% -> 4% of each run, Pallas kernels for 19% -> 24%
where the time goes in v2:
time: 120 us
  waiting for transfers between devices  46.6 us (39%)
  Pallas kernels  34.4 us (29%)
  starting transfers between devices  32.6 us (27%)
  local copies, waits for them, and re-layouts  2.86 us (2%)
  other arithmetic  2.41 us (2%)
    ppermute x16, waiting for transfers between devices, fetch(): return lax.ppermute(value, AXES, pairs)  46.5 us
    ppermute x16, starting transfers between devices, fetch(): return lax.ppermute(value, AXES, pairs)  21.1 us
    pallas_call x1, Pallas kernels, count(): pl.pallas_call(count_kernel, grid=(RING,), in_specs=[pl.BlockSpec((steps,...  12.7 us
    pallas_call x2, Pallas kernels, finish(): pl.pallas_call(functools.partial(finish_kernel, readers), in_specs=[SMEM]...  12.5 us
    all_to_all x1, starting transfers between devices, body(): lax.all_to_all(partials, AXES, split_axis=0, concat_axis=0, tiled=True)  11.5 us
    pallas_call x1, Pallas kernels, collect(): pl.pallas_call(functools.partial(collect_kernel, blocks), in_specs=[VMEM]...  7.16 us
  transfers between devices with their start and end apart: 17, of which 8 were waited for; matrix products, arithmetic and copies ran while one was open for 4% of the time, Pallas kernels for 24%

profile of v2, /device:TPU:1, one launch (start us, length us, event | category | flops | bytes accessed | tf_op | source)
XLA Modules:
  0.0 120.0 jit_solution(12133311355491943485)
XLA Ops:
  0.0 11.5 %all-to-all-start = ((f32[128,8,512]{2,1,0:T(8,128)}), f32[128,8,512]{2,1,0:T(8,128)S(1)}, u32[]{:S(2)}, u32[]{:S(2)}) async-start(f32[128,8,512]{2,1,0:T(8,128)} %bitcast.18), calls=%async_computation | async-start | bytes 4194304 | tf_op jit(solution)/shard_map/all_to_all | solution.py:271
  11.6 3.3 %collective-permute-start.3 = (s32[2,8192]{1,0:T(2,128)S(1)}, s32[2,8192]{1,0:T(2,128)S(1)}, u32[]{:S(2)}, u32[]{:S(2)}) collective-permute-start(s32[2,8192]{1,0:T(2,128)S(1)} %get-tuple-element.56), channel_id=1, source_target_pairs={{32,0},{33,1},{34,2},{35,3},{36,4},{37,5},{38,6},{39,7},{40,8},{41... | collective-permute-start | bytes 196616 | tf_op jit(solution)/shard_map/ppermute | solution.py:39
  15.1 0.8 collective-permute-start.5
  15.8 0.9 fusion.50
  17.9 11.8 %collective-permute-done.3 = s32[2,8192]{1,0:T(2,128)S(1)} collective-permute-done((s32[2,8192]{1,0:T(2,128)S(1)}, s32[2,8192]{1,0:T(2,128)S(1)}, u32[]{:S(2)}, u32[]{:S(2)}) %collective-permute-start.3) | collective-permute-done | bytes 65568 | tf_op jit(solution)/shard_map/ppermute | solution.py:39
  29.7 8.4 %collective-permute-done.4 = s32[2,8192]{1,0:T(2,128)S(1)} collective-permute-done((s32[2,8192]{1,0:T(2,128)S(1)}, s32[2,8192]{1,0:T(2,128)S(1)}, u32[]{:S(2)}, u32[]{:S(2)}) %collective-permute-start.4) | collective-permute-done | bytes 65568 | tf_op jit(solution)/shard_map/ppermute | solution.py:39
  38.1 3.0 %collective-permute-done.5 = s32[2,8192]{1,0:T(2,128)S(1)} collective-permute-done((s32[2,8192]{1,0:T(2,128)S(1)}, s32[2,8192]{1,0:T(2,128)S(1)}, u32[]{:S(2)}, u32[]{:S(2)}) %collective-permute-start.5) | collective-permute-done | bytes 65568 | tf_op jit(solution)/shard_map/ppermute | solution.py:39
  41.3 0.9 fusion
  42.2 1.9 %collective-permute-start = (f32[128,512]{1,0:T(8,128)S(1)}, f32[128,512]{1,0:T(8,128)S(1)}, u32[]{:S(2)}, u32[]{:S(2)}) collective-permute-start(f32[128,512]{1,0:T(8,128)S(1)} %fusion), channel_id=1, source_target_pairs={{4,0},{5,1},{6,2},{7,3},{8,4},{9,5},{10,6},{11,7},{12,8},{13,9},{1... | collective-permute-start | bytes 786440 | tf_op jit(solution)/shard_map/ppermute | solution.py:39
  44.6 0.7 collective-permute-start.2
  45.3 0.7 slice_reduce_fusion.1
  46.2 1.4 %fusion.19 = (s32[32,1024]{1,0:T(8,128)}, s32[32,1024]{1,0:T(8,128)}) fusion(s32[32,1024]{1,0:T(8,128)S(1)} %squeeze.6, s32[]{:T(128)S(6)} %select_n.306, s32[]{:T(128)S(6)} %select_n.297, s32[]{:T(128)S(6)} %select_n.300, s32[32,1024]{1,0:T(8,128)S(1)} %squeeze.7, s32[]{:T(128)S(6)} %select_n.294), kind=kLoop, calls=%fused_computation.55 | loop fusion | flops 4358144 | bytes 524304 | tf_op jit(solution)/shard_map/add | solution.py:301
  47.5 12.7 %count.1 = (bf16[4,4,1024,256]{3,2,1,0:T(8,128)(2,1)}, bf16[4,4,1024,256]{3,2,1,0:T(8,128)(2,1)}, s32[4]{0:T(128)}) custom-call(s32[32,1024]{1,0:T(8,128)} %get-tuple-element.54.row_ref, s32[32,1024]{1,0:T(8,128)} %get-tuple-element.53.col_ref), custom_call_target="tpu_custom_call" | custom-call | flops 100000000 | bytes 1048576 | tf_op jit(solution)/shard_map/count/pallas_call | solution.py:104
  60.4 1.2 collective-permute-start.10
  61.5 1.6 %collective-permute-start.8 = (f32[512,512]{1,0:T(8,128)S(1)}, f32[512,512]{1,0:T(8,128)S(1)}, u32[]{:S(2)}, u32[]{:S(2)}) collective-permute-start(f32[512,512]{1,0:T(8,128)S(1)} %constant_dynamic-update-slice_fusion.refs_0_), channel_id=1, source_target_pairs={{1,0},{2,1},{3,2},{0,3},{5,4},{6,5},{7,6},{4,7},{9,8},{10,9},{11,1... | collective-permute-start | bytes 3145736 | tf_op jit(solution)/shard_map/ppermute | solution.py:39
  63.1 1.6 %collective-permute-start.6 = (f32[512,512]{1,0:T(8,128)S(1)}, f32[512,512]{1,0:T(8,128)S(1)}, u32[]{:S(2)}, u32[]{:S(2)}) collective-permute-start(f32[512,512]{1,0:T(8,128)S(1)} %constant_dynamic-update-slice_fusion.refs_0_), channel_id=1, source_target_pairs={{16,0},{17,1},{18,2},{19,3},{20,4},{21,5},{22,6},{23,7},{24,8},{25... | collective-permute-start | bytes 3145736 | tf_op jit(solution)/shard_map/ppermute | solution.py:39
  64.8 10.9 %collective-permute-done.10.refs_2_ = f32[512,512]{1,0:T(8,128)S(1)} collective-permute-done((f32[512,512]{1,0:T(8,128)S(1)}, f32[512,512]{1,0:T(8,128)S(1)}, u32[]{:S(2)}, u32[]{:S(2)}) %collective-permute-start.10) | collective-permute-done | bytes 1048608 | tf_op jit(solution)/shard_map/ppermute | solution.py:39
  75.6 1.9 %collective-permute-start.11 = (f32[512,512]{1,0:T(8,128)S(1)}, f32[512,512]{1,0:T(8,128)S(1)}, u32[]{:S(2)}, u32[]{:S(2)}) collective-permute-start(f32[512,512]{1,0:T(8,128)S(1)} %collective-permute-done.10.refs_2_), channel_id=1, source_target_pairs={{16,0},{17,1},{18,2},{19,3},{20,4},{21,5},{22,6},{23,7},{24,8},{25... | collective-permute-start | bytes 3145736 | tf_op jit(solution)/shard_map/ppermute | solution.py:39
  77.9 0.7 gather.9.refs_0_.rows0
  78.7 2.7 %collective-permute-start.7 = (f32[512,512]{1,0:T(8,128)S(1)}, f32[512,512]{1,0:T(8,128)S(1)}, u32[]{:S(2)}, u32[]{:S(2)}) collective-permute-start(f32[512,512]{1,0:T(8,128)S(1)} %constant_dynamic-update-slice_fusion.refs_0_), channel_id=1, source_target_pairs={{2,0},{3,1},{0,2},{1,3},{6,4},{7,5},{4,6},{5,7},{10,8},{11,9},{8,1... | collective-permute-start | bytes 3145736 | tf_op jit(solution)/shard_map/ppermute | solution.py:39
  81.4 1.3 %gather.10 = (bf16[4,256,1024]{2,1,0:T(8,128)(2,1)S(1)}, bf16[4,256,1024]{2,1,0:T(8,128)(2,1)S(1)}) custom-call(s32[32,128]{1,0:T(8,128)S(1)} %broadcast_select_fusion.ids_ref, f32[512,512]{1,0:T(8,128)S(1)} %collective-permute-done.8.refs_0_, f32[512,512]{1,0:T(8,128)S(1)} %collective-permute-done.9.refs_1_, ...), custom_call_target="tpu_custom_call" | custom-call | flops 3000000000 | bytes 2097152 | tf_op jit(solution)/shard_map/gather/pallas_call | solution.py:150
  82.8 7.2 %collect.1.x_ref = f32[4,1024,512]{2,1,0:T(8,128)S(1)} custom-call(bf16[4,4,1024,256]{3,2,1,0:T(8,128)(2,1)S(1)} %bitcast.17, bf16[4,256,1024]{2,1,0:T(8,128)(2,1)S(1)} %gather.9.refs_0_.rows0, bf16[4,256,1024]{2,1,0:T(8,128)(2,1)S(1)} %get-tuple-element.38.refs_1_.rows1, bf16[4,256,1024]{2,1,0:T(8,128)(2,1)S(1)} %get-tuple-element.39.refs_2_.rows3), custom_call_target="tpu_custom_call" | custom-call | flops 6600000000 | bytes 3145728 | tf_op jit(solution)/shard_map/collect/pallas_call | solution.py:186
  89.9 4.5 %collective-permute-done.7.b0 = f32[512,512]{1,0:T(8,128)S(1)} collective-permute-done((f32[512,512]{1,0:T(8,128)S(1)}, f32[512,512]{1,0:T(8,128)S(1)}, u32[]{:S(2)}, u32[]{:S(2)}) %collective-permute-start.7) | collective-permute-done | bytes 1048608 | tf_op jit(solution)/shard_map/ppermute | solution.py:39
  94.4 1.0 collective-permute-start.12
  95.4 2.3 %collective-permute-done.12.b1 = f32[512,512]{1,0:T(8,128)S(1)} collective-permute-done((f32[512,512]{1,0:T(8,128)S(1)}, f32[512,512]{1,0:T(8,128)S(1)}, u32[]{:S(2)}, u32[]{:S(2)}) %collective-permute-start.12) | collective-permute-done | bytes 1048608 | tf_op jit(solution)/shard_map/ppermute | solution.py:39
  97.7 6.1 %finish.3 = (f32[128,512]{1,0:T(8,128)S(1)}, f32[128,512]{1,0:T(8,128)S(1)}) custom-call(s32[4]{0:T(128)S(1)} %copy-done.1, s32[32,128]{1,0:T(8,128)S(1)} %broadcast_select_fusion.ids_ref, f32[512,512]{1,0:T(8,128)S(1)} %collective-permute-done.7.b0, f32[512,512]{1,0:T(8,128)S(1)} %collective-permute-done.12.b1, f32[4,1024,512]{2,1,0:T(8,128)S(1)} %collect.1.x_ref, ...), custom_call_target="tpu_custom_call" | custom-call | flops 6000000000 | bytes 2097152 | tf_op jit(solution)/shard_map/finish/pallas_call | solution.py:245
  103.8 0.7 collective-permute-start.13
  104.5 0.8 collective-permute-start.14
  105.4 6.4 %finish.2 = (f32[128,512]{1,0:T(8,128)S(1)}, f32[128,512]{1,0:T(8,128)S(1)}) custom-call(s32[4]{0:T(128)S(1)} %copy-done.1, s32[32,128]{1,0:T(8,128)S(1)} %broadcast_select_fusion.ids_ref, f32[512,512]{1,0:T(8,128)S(1)} %collective-permute-done.7.b0, f32[512,512]{1,0:T(8,128)S(1)} %collective-permute-done.12.b1, f32[4,1024,512]{2,1,0:T(8,128)S(1)} %collect.1.x_ref, ...), custom_call_target="tpu_custom_call" | custom-call | flops 6000000000 | bytes 2097152 | tf_op jit(solution)/shard_map/finish/pallas_call | solution.py:245
  111.7 1.9 %collective-permute-start.15 = (f32[128,512]{1,0:T(8,128)S(1)}, f32[128,512]{1,0:T(8,128)S(1)}, u32[]{:S(2)}, u32[]{:S(2)}) collective-permute-start(f32[128,512]{1,0:T(8,128)S(1)} %get-tuple-element.46), channel_id=1, source_target_pairs={{32,0},{33,1},{34,2},{35,3},{36,4},{37,5},{38,6},{39,7},{40,8},{41... | collective-permute-start | bytes 786440 | tf_op jit(solution)/shard_map/ppermute | solution.py:39
  113.6 5.6 %collective-permute-done.14 = f32[128,512]{1,0:T(8,128)S(1)} collective-permute-done((f32[128,512]{1,0:T(8,128)S(1)}, f32[128,512]{1,0:T(8,128)S(1)}, u32[]{:S(2)}, u32[]{:S(2)}) %collective-permute-start.14) | collective-permute-done | bytes 262176 | tf_op jit(solution)/shard_map/ppermute | solution.py:39
  119.3 0.8 add_add_fusion
  (50 shorter events, 2.6 us)
Async XLA Ops:
  0.0 17.8 %copy-start = (s32[128,1024]{1,0:T(8,128)S(1)}, s32[128,1024]{1,0:T(8,128)}, u32[]{:S(2)}) copy-start(s32[128,1024]{1,0:T(8,128)} %param.7) | copy-start | bytes 1572868
  0.0 11.5 %copy-start.2 = (s32[1,8192]{1,0:T(1,128)S(1)}, s32[1,8192]{1,0:T(1,128)}, u32[]{:S(2)}) copy-start(s32[1,8192]{1,0:T(1,128)} %param.10) | copy-start | bytes 98308
  0.0 11.5 %copy-start.3 = (s32[1,8192]{1,0:T(1,128)S(1)}, s32[1,8192]{1,0:T(1,128)}, u32[]{:S(2)}) copy-start(s32[1,8192]{1,0:T(1,128)} %param.9) | copy-start | bytes 98308
  0.0 41.3 %all-to-all-start = ((f32[128,8,512]{2,1,0:T(8,128)}), f32[128,8,512]{2,1,0:T(8,128)S(1)}, u32[]{:S(2)}, u32[]{:S(2)}) async-start(f32[128,8,512]{2,1,0:T(8,128)} %bitcast.18), calls=%async_computation | async-start | bytes 4194304 | tf_op jit(solution)/shard_map/all_to_all | solution.py:271
  11.6 18.1 %collective-permute-start.3 = (s32[2,8192]{1,0:T(2,128)S(1)}, s32[2,8192]{1,0:T(2,128)S(1)}, u32[]{:S(2)}, u32[]{:S(2)}) collective-permute-start(s32[2,8192]{1,0:T(2,128)S(1)} %get-tuple-element.56), channel_id=1, source_target_pairs={{32,0},{33,1},{34,2},{35,3},{36,4},{37,5},{38,6},{39,7},{40,8},{41... | collective-permute-start | bytes 196616 | tf_op jit(solution)/shard_map/ppermute | solution.py:39
  14.9 23.2 %collective-permute-start.4 = (s32[2,8192]{1,0:T(2,128)S(1)}, s32[2,8192]{1,0:T(2,128)S(1)}, u32[]{:S(2)}, u32[]{:S(2)}) collective-permute-start(s32[2,8192]{1,0:T(2,128)S(1)} %get-tuple-element.56), channel_id=1, source_target_pairs={{64,0},{65,1},{66,2},{67,3},{68,4},{69,5},{70,6},{71,7},{72,8},{73... | collective-permute-start | bytes 196616 | tf_op jit(solution)/shard_map/ppermute | solution.py:39
  15.1 26.1 %collective-permute-start.5 = (s32[2,8192]{1,0:T(2,128)S(1)}, s32[2,8192]{1,0:T(2,128)S(1)}, u32[]{:S(2)}, u32[]{:S(2)}) collective-permute-start(s32[2,8192]{1,0:T(2,128)S(1)} %get-tuple-element.56), channel_id=1, source_target_pairs={{96,0},{97,1},{98,2},{99,3},{100,4},{101,5},{102,6},{103,7},{104,8... | collective-permute-start | bytes 196616 | tf_op jit(solution)/shard_map/ppermute | solution.py:39
  42.2 18.1 %collective-permute-start = (f32[128,512]{1,0:T(8,128)S(1)}, f32[128,512]{1,0:T(8,128)S(1)}, u32[]{:S(2)}, u32[]{:S(2)}) collective-permute-start(f32[128,512]{1,0:T(8,128)S(1)} %fusion), channel_id=1, source_target_pairs={{4,0},{5,1},{6,2},{7,3},{8,4},{9,5},{10,6},{11,7},{12,8},{13,9},{1... | collective-permute-start | bytes 786440 | tf_op jit(solution)/shard_map/ppermute | solution.py:39
  44.1 16.1 %collective-permute-start.1 = (f32[128,512]{1,0:T(8,128)S(1)}, f32[128,512]{1,0:T(8,128)S(1)}, u32[]{:S(2)}, u32[]{:S(2)}) collective-permute-start(f32[128,512]{1,0:T(8,128)S(1)} %fusion), channel_id=1, source_target_pairs={{8,0},{9,1},{10,2},{11,3},{12,4},{13,5},{14,6},{15,7},{0,8},{1,9},... | collective-permute-start | bytes 786440 | tf_op jit(solution)/shard_map/ppermute | solution.py:39
  44.6 15.7 %collective-permute-start.2 = (f32[128,512]{1,0:T(8,128)S(1)}, f32[128,512]{1,0:T(8,128)S(1)}, u32[]{:S(2)}, u32[]{:S(2)}) collective-permute-start(f32[128,512]{1,0:T(8,128)S(1)} %fusion), channel_id=1, source_target_pairs={{12,0},{13,1},{14,2},{15,3},{0,4},{1,5},{2,6},{3,7},{4,8},{5,9},{6... | collective-permute-start | bytes 786440 | tf_op jit(solution)/shard_map/ppermute | solution.py:39
  60.4 15.2 %collective-permute-start.10 = (f32[512,512]{1,0:T(8,128)S(1)}, f32[512,512]{1,0:T(8,128)S(1)}, u32[]{:S(2)}, u32[]{:S(2)}) collective-permute-start(f32[512,512]{1,0:T(8,128)S(1)} %constant_dynamic-update-slice_fusion.refs_0_), channel_id=1, source_target_pairs={{3,0},{0,1},{1,2},{2,3},{7,4},{4,5},{5,6},{6,7},{11,8},{8,9},{9,10... | collective-permute-start | bytes 3145736 | tf_op jit(solution)/shard_map/ppermute | solution.py:39
  61.5 16.0 %collective-permute-start.8 = (f32[512,512]{1,0:T(8,128)S(1)}, f32[512,512]{1,0:T(8,128)S(1)}, u32[]{:S(2)}, u32[]{:S(2)}) collective-permute-start(f32[512,512]{1,0:T(8,128)S(1)} %constant_dynamic-update-slice_fusion.refs_0_), channel_id=1, source_target_pairs={{1,0},{2,1},{3,2},{0,3},{5,4},{6,5},{7,6},{4,7},{9,8},{10,9},{11,1... | collective-permute-start | bytes 3145736 | tf_op jit(solution)/shard_map/ppermute | solution.py:39
  63.1 14.8 %collective-permute-start.6 = (f32[512,512]{1,0:T(8,128)S(1)}, f32[512,512]{1,0:T(8,128)S(1)}, u32[]{:S(2)}, u32[]{:S(2)}) collective-permute-start(f32[512,512]{1,0:T(8,128)S(1)} %constant_dynamic-update-slice_fusion.refs_0_), channel_id=1, source_target_pairs={{16,0},{17,1},{18,2},{19,3},{20,4},{21,5},{22,6},{23,7},{24,8},{25... | collective-permute-start | bytes 3145736 | tf_op jit(solution)/shard_map/ppermute | solution.py:39
  75.6 5.8 %collective-permute-start.11 = (f32[512,512]{1,0:T(8,128)S(1)}, f32[512,512]{1,0:T(8,128)S(1)}, u32[]{:S(2)}, u32[]{:S(2)}) collective-permute-start(f32[512,512]{1,0:T(8,128)S(1)} %collective-permute-done.10.refs_2_), channel_id=1, source_target_pairs={{16,0},{17,1},{18,2},{19,3},{20,4},{21,5},{22,6},{23,7},{24,8},{25... | collective-permute-start | bytes 3145736 | tf_op jit(solution)/shard_map/ppermute | solution.py:39
  77.5 3.9 %collective-permute-start.9 = (f32[512,512]{1,0:T(8,128)S(1)}, f32[512,512]{1,0:T(8,128)S(1)}, u32[]{:S(2)}, u32[]{:S(2)}) collective-permute-start(f32[512,512]{1,0:T(8,128)S(1)} %collective-permute-done.8.refs_0_), channel_id=1, source_target_pairs={{16,0},{17,1},{18,2},{19,3},{20,4},{21,5},{22,6},{23,7},{24,8},{25... | collective-permute-start | bytes 3145736 | tf_op jit(solution)/shard_map/ppermute | solution.py:39
  77.9 4.8 %slice-start.2 = ((s8[8388608]{0:T(1024)(128)(4,1)}), s8[4194304]{0:T(1024)(128)(4,1)S(1)}, s32[]{:S(2)}) async-start(s8[8388608]{0:T(1024)(128)(4,1)} %bitcast.16), calls=%async_computation.3 | async-start | bytes 8388608
  78.7 4.1 %slice-start.3 = ((s8[8388608]{0:T(1024)(128)(4,1)}), s8[4194304]{0:T(1024)(128)(4,1)S(1)}, s32[]{:S(2)}) async-start(s8[8388608]{0:T(1024)(128)(4,1)} %bitcast.16), calls=%async_computation.4 | async-start | bytes 8388608
  78.7 15.7 %collective-permute-start.7 = (f32[512,512]{1,0:T(8,128)S(1)}, f32[512,512]{1,0:T(8,128)S(1)}, u32[]{:S(2)}, u32[]{:S(2)}) collective-permute-start(f32[512,512]{1,0:T(8,128)S(1)} %constant_dynamic-update-slice_fusion.refs_0_), channel_id=1, source_target_pairs={{2,0},{3,1},{0,2},{1,3},{6,4},{7,5},{4,6},{5,7},{10,8},{11,9},{8,1... | collective-permute-start | bytes 3145736 | tf_op jit(solution)/shard_map/ppermute | solution.py:39
  82.7 14.9 %slice-start = ((s8[8388608]{0:T(1024)(128)(4,1)}), s8[4194304]{0:T(1024)(128)(4,1)S(1)}, s32[]{:S(2)}) async-start(s8[8388608]{0:T(1024)(128)(4,1)} %bitcast.14), calls=%async_computation.1 | async-start | bytes 8388608
  82.8 14.9 %slice-start.1 = ((s8[8388608]{0:T(1024)(128)(4,1)}), s8[4194304]{0:T(1024)(128)(4,1)S(1)}, s32[]{:S(2)}) async-start(s8[8388608]{0:T(1024)(128)(4,1)} %bitcast.14), calls=%async_computation.2 | async-start | bytes 8388608
  82.8 14.9 %copy-start.1 = (s32[4]{0:T(128)S(1)}, s32[4]{0:T(128)}, u32[]{:S(2)}) copy-start(s32[4]{0:T(128)} %get-tuple-element.29.flag_ref) | copy-start | bytes 52
  94.4 3.3 %collective-permute-start.12 = (f32[512,512]{1,0:T(8,128)S(1)}, f32[512,512]{1,0:T(8,128)S(1)}, u32[]{:S(2)}, u32[]{:S(2)}) collective-permute-start(f32[512,512]{1,0:T(8,128)S(1)} %collective-permute-done.7.b0), channel_id=1, source_target_pairs={{16,0},{17,1},{18,2},{19,3},{20,4},{21,5},{22,6},{23,7},{24,8},{25... | collective-permute-start | bytes 3145736 | tf_op jit(solution)/shard_map/ppermute | solution.py:39
  103.8 9.8 %collective-permute-start.13 = (f32[128,512]{1,0:T(8,128)S(1)}, f32[128,512]{1,0:T(8,128)S(1)}, u32[]{:S(2)}, u32[]{:S(2)}) collective-permute-start(f32[128,512]{1,0:T(8,128)S(1)} %get-tuple-element.44), channel_id=1, source_target_pairs={{64,0},{65,1},{66,2},{67,3},{68,4},{69,5},{70,6},{71,7},{72,8},{73... | collective-permute-start | bytes 786440 | tf_op jit(solution)/shard_map/ppermute | solution.py:39
  104.5 14.7 %collective-permute-start.14 = (f32[128,512]{1,0:T(8,128)S(1)}, f32[128,512]{1,0:T(8,128)S(1)}, u32[]{:S(2)}, u32[]{:S(2)}) collective-permute-start(f32[128,512]{1,0:T(8,128)S(1)} %get-tuple-element.45), channel_id=1, source_target_pairs={{96,0},{97,1},{98,2},{99,3},{100,4},{101,5},{102,6},{103,7},{104,8... | collective-permute-start | bytes 786440 | tf_op jit(solution)/shard_map/ppermute | solution.py:39
  111.7 7.5 %collective-permute-start.15 = (f32[128,512]{1,0:T(8,128)S(1)}, f32[128,512]{1,0:T(8,128)S(1)}, u32[]{:S(2)}, u32[]{:S(2)}) collective-permute-start(f32[128,512]{1,0:T(8,128)S(1)} %get-tuple-element.46), channel_id=1, source_target_pairs={{32,0},{33,1},{34,2},{35,3},{36,4},{37,5},{38,6},{39,7},{40,8},{41... | collective-permute-start | bytes 786440 | tf_op jit(solution)/shard_map/ppermute | solution.py:39

commit v3 on v2

--- a/solution.py
+++ b/solution.py
@@ -122,9 +122,10 @@
 
 def pick(ids_ref, first, refs, store):
     octants = lax.broadcasted_iota(jnp.int32, (OCT, RING * PER), 0)
+    many = CORES * RING // len(refs)
     for i, ref in enumerate(refs):
-        for j in range(RING):
-            owner = RING * i + j
+        for j in range(many):
+            owner = many * i + j
             table = jnp.concatenate(parts(ref[j * OCT : (j + 1) * OCT, :]), axis=1)
             hot = jnp.where(octants == ids_ref[first + owner : first + owner + 1, :], 1.0, 0.0)
             picked = lax.dot_general(
@@ -197,14 +198,14 @@
 
 
 def finish_kernel(
-    readers, flag_ref, ids_ref, b0, b1, x_ref, rows0, rows1, rows3, count_ref, k_ref, rest_hbm,
+    readers, flag_ref, ids_ref, b0, b1, b2, b3, x_ref, rows0, rows1, rows3, count_ref, k_ref, rest_hbm,
     out0, out1,
     rows2, xh, xl, rest,
 ):
     def store(owner, k, values):
         rows2[k, owner * PER : (owner + 1) * PER, :] = values
 
-    pick(ids_ref, 2 * 2 * RING, (b0, b1), store)
+    pick(ids_ref, 2 * 2 * RING, (b0, b1, b2, b3), store)
     for i, k in enumerate(readers):
         there = slice(i * OCT, (i + 1) * OCT)
         for m in range(0, DIRS, 2):
@@ -244,7 +245,7 @@
     n = len(readers)
     return pl.pallas_call(
         functools.partial(finish_kernel, readers),
-        in_specs=[SMEM] + [VMEM] * 9 + [HBM],
+        in_specs=[SMEM] + [VMEM] * 11 + [HBM],
         out_specs=[VMEM] * 2,
         out_shape=[jax.ShapeDtypeStruct((OCT, WIDTH), F32)] * 2,
         scratch_shapes=[
@@ -302,9 +303,7 @@
     here = owner // PLANE == z
     row_codes = jnp.where(here, s // 2 * OCT + target, -1)
     per_dir = sources.shape[1] // DIRS
-    counts, rest, flags = count(
-        row_codes.reshape(RING * DIRS, per_dir), column.reshape(RING * DIRS, per_dir)
-    )
+    codes = [code.reshape(RING * DIRS, per_dir) for code in (row_codes, column)]
 
     octants = jnp.arange(OCT, dtype=jnp.int32)
     column_ids = lax.dynamic_slice_in_dim(partial_ids, device * per_owner, per_owner, 1).reshape(-1)
@@ -314,20 +313,20 @@
     )
 
     line = [density] + [along_f(density, k) for k in range(1, RING)]
-    line, counts, rest, flags, ids = lax.optimization_barrier((line, counts, rest, flags, ids))
+    line, codes, ids = lax.optimization_barrier((line, codes, ids))
     line = jnp.concatenate(line, axis=0)
-    block = {1: along_s(line, 1), 3: along_s(line, 3)}
-    rows = {}
-    (rows[0],) = gather((0,), ids, [line, across(line)])
-    line, rows[0] = lax.optimization_barrier((line, rows[0]))
-    block[2] = along_s(line, 2)
-    near = [block[1], across(block[1]), block[3], across(block[3])]
-    rows[1], rows[3] = gather((1, 3), ids, near)
-    rows = (rows[0], rows[1], rows[3])
+    near1, near3 = along_s(line, 1), along_s(line, 3)
+    counts, rest, flags = count(*codes)
+    near1, near3, counts, rest, flags = lax.optimization_barrier(
+        (near1, near3, counts, rest, flags)
+    )
+    low, high = along_s(near1[: 2 * OCT], 1), along_s(near3[2 * OCT :], 3)
+    (rows0,) = gather((0,), ids, [line, across(line)])
+    rows1, rows3 = gather((1, 3), ids, [near1, across(near1), near3, across(near3)])
+    rows = (rows0, rows1, rows3)
     x = collect((0, 1, 3), counts, rows)
-    block[2], x = lax.optimization_barrier((block[2], x))
-    far = [block[2], across(block[2])]
-    last = (flags, ids, far, x, rows, counts, kernels, rest)
+    low, high, x = lax.optimization_barrier((low, high, x))
+    last = (flags, ids, [low, high, across(low), across(high)], x, rows, counts, kernels, rest)
     out2, out1 = finish((2, 1), *last)
     out3, out0 = finish((3, 0), *last)
     return out0 + along_z(out2, -2) + along_z(out1, -1) + along_z(out3, -3)

time: 120 us -> 117 us (0.975)
  waiting for transfers between devices: 46.6 us -> 38 us
  local copies, waits for them, and re-layouts: 2.86 us -> 6.65 us
  Pallas kernels: 34.4 us -> 36.4 us
    ppermute x16 -> x18, waiting for transfers between devices: 46.5 us -> 37.9 us  [fetch(): return lax.ppermute(value, AXES, pairs)]
    unnamed x19, local copies, waits for them, and re-layouts: 0.1 us -> 3.11 us
    pallas_call x2, Pallas kernels: 2.05 us -> 3.74 us  [gather(): pl.pallas_call(functools.partial(gather_kernel, blocks), in_specs=[VMEM]...]
    ppermute x16 -> x18, starting transfers between devices: 21.1 us -> 20.7 us  [fetch(): return lax.ppermute(value, AXES, pairs)]
  transfers between devices with their start and end apart: 17 -> 19, of which waited for: 8 -> 11; matrix products, arithmetic and copies ran while one was open for 4% -> 4% of each run, Pallas kernels for 24% -> 26%
where the time goes in v3:
time: 117 us
  waiting for transfers between devices  38 us (32%)
  Pallas kernels  36.4 us (31%)
  starting transfers between devices  32.2 us (28%)
  local copies, waits for them, and re-layouts  6.65 us (6%)
  other arithmetic  2.41 us (2%)
    ppermute x18, waiting for transfers between devices, fetch(): return lax.ppermute(value, AXES, pairs)  37.9 us
    ppermute x18, starting transfers between devices, fetch(): return lax.ppermute(value, AXES, pairs)  20.7 us
    pallas_call x1, Pallas kernels, count(): pl.pallas_call(count_kernel, grid=(RING,), in_specs=[pl.BlockSpec((steps,...  12.7 us
    pallas_call x2, Pallas kernels, finish(): pl.pallas_call(functools.partial(finish_kernel, readers), in_specs=[SMEM]...  12.7 us
    all_to_all x1, starting transfers between devices, body(): lax.all_to_all(partials, AXES, split_axis=0, concat_axis=0, tiled=True)  11.5 us
    pallas_call x1, Pallas kernels, collect(): pl.pallas_call(functools.partial(collect_kernel, blocks), in_specs=[VMEM]...  7.15 us
    pallas_call x2, Pallas kernels, gather(): pl.pallas_call(functools.partial(gather_kernel, blocks), in_specs=[VMEM]...  3.74 us
    unnamed x19, local copies, waits for them, and re-layouts  3.11 us
  transfers between devices with their start and end apart: 19, of which 11 were waited for; matrix products, arithmetic and copies ran while one was open for 4% of the time, Pallas kernels for 26%

profile of v3, /device:TPU:1, one launch (start us, length us, event | category | flops | bytes accessed | tf_op | source)
XLA Modules:
  0.0 116.8 jit_solution(2053989650177029873)
XLA Ops:
  0.0 11.5 %all-to-all-start = ((f32[128,8,512]{2,1,0:T(8,128)}), f32[128,8,512]{2,1,0:T(8,128)S(1)}, u32[]{:S(2)}, u32[]{:S(2)}) async-start(f32[128,8,512]{2,1,0:T(8,128)} %bitcast.18), calls=%async_computation | async-start | bytes 4194304 | tf_op jit(solution)/shard_map/all_to_all | solution.py:272
  11.6 3.3 %collective-permute-start.3 = (s32[2,8192]{1,0:T(2,128)S(1)}, s32[2,8192]{1,0:T(2,128)S(1)}, u32[]{:S(2)}, u32[]{:S(2)}) collective-permute-start(s32[2,8192]{1,0:T(2,128)S(1)} %get-tuple-element.62), channel_id=1, source_target_pairs={{32,0},{33,1},{34,2},{35,3},{36,4},{37,5},{38,6},{39,7},{40,8},{41... | collective-permute-start | bytes 196616 | tf_op jit(solution)/shard_map/ppermute | solution.py:39
  15.1 0.8 collective-permute-start.5
  15.8 0.9 fusion.50
  17.9 11.8 %collective-permute-done.3 = s32[2,8192]{1,0:T(2,128)S(1)} collective-permute-done((s32[2,8192]{1,0:T(2,128)S(1)}, s32[2,8192]{1,0:T(2,128)S(1)}, u32[]{:S(2)}, u32[]{:S(2)}) %collective-permute-start.3) | collective-permute-done | bytes 65568 | tf_op jit(solution)/shard_map/ppermute | solution.py:39
  29.7 8.4 %collective-permute-done.4 = s32[2,8192]{1,0:T(2,128)S(1)} collective-permute-done((s32[2,8192]{1,0:T(2,128)S(1)}, s32[2,8192]{1,0:T(2,128)S(1)}, u32[]{:S(2)}, u32[]{:S(2)}) %collective-permute-start.4) | collective-permute-done | bytes 65568 | tf_op jit(solution)/shard_map/ppermute | solution.py:39
  38.1 3.0 %collective-permute-done.5 = s32[2,8192]{1,0:T(2,128)S(1)} collective-permute-done((s32[2,8192]{1,0:T(2,128)S(1)}, s32[2,8192]{1,0:T(2,128)S(1)}, u32[]{:S(2)}, u32[]{:S(2)}) %collective-permute-start.5) | collective-permute-done | bytes 65568 | tf_op jit(solution)/shard_map/ppermute | solution.py:39
  41.3 0.9 fusion
  42.2 1.9 %collective-permute-start = (f32[128,512]{1,0:T(8,128)S(1)}, f32[128,512]{1,0:T(8,128)S(1)}, u32[]{:S(2)}, u32[]{:S(2)}) collective-permute-start(f32[128,512]{1,0:T(8,128)S(1)} %fusion), channel_id=1, source_target_pairs={{4,0},{5,1},{6,2},{7,3},{8,4},{9,5},{10,6},{11,7},{12,8},{13,9},{1... | collective-permute-start | bytes 786440 | tf_op jit(solution)/shard_map/ppermute | solution.py:39
  46.2 1.4 %fusion.19 = (s32[32,1024]{1,0:T(8,128)}, s32[32,1024]{1,0:T(8,128)}) fusion(s32[32,1024]{1,0:T(8,128)S(1)} %squeeze.6, s32[]{:T(128)S(6)} %select_n.306, s32[]{:T(128)S(6)} %select_n.297, s32[]{:T(128)S(6)} %select_n.300, s32[32,1024]{1,0:T(8,128)S(1)} %squeeze.7, s32[]{:T(128)S(6)} %select_n.294), kind=kLoop, calls=%fused_computation.55 | loop fusion | flops 4358144 | bytes 524304 | tf_op jit(solution)/shard_map/add | solution.py:302
  47.5 2.7 %collective-permute-done = f32[128,512]{1,0:T(8,128)S(1)} collective-permute-done((f32[128,512]{1,0:T(8,128)S(1)}, f32[128,512]{1,0:T(8,128)S(1)}, u32[]{:S(2)}, u32[]{:S(2)}) %collective-permute-start) | collective-permute-done | bytes 262176 | tf_op jit(solution)/shard_map/ppermute | solution.py:39
  50.2 0.9 collective-permute-done.1
  51.2 2.8 %collective-permute-done.2 = f32[128,512]{1,0:T(8,128)S(1)} collective-permute-done((f32[128,512]{1,0:T(8,128)S(1)}, f32[128,512]{1,0:T(8,128)S(1)}, u32[]{:S(2)}, u32[]{:S(2)}) %collective-permute-start.2) | collective-permute-done | bytes 262176 | tf_op jit(solution)/shard_map/ppermute | solution.py:39
  55.4 0.7 constant_dynamic-update-slice_fusion.1
  56.8 2.0 %collective-permute-start.6 = (f32[512,512]{1,0:T(8,128)}, f32[512,512]{1,0:T(8,128)S(1)}, u32[]{:S(2)}, u32[]{:S(2)}) collective-permute-start(f32[512,512]{1,0:T(8,128)} %constant_dynamic-update-slice_fusion.refs_0_), channel_id=1, source_target_pairs={{1,0},{2,1},{3,2},{0,3},{5,4},{6,5},{7,6},{4,7},{9,8},{10,9},{11,1... | collective-permute-start | bytes 3145736 | tf_op jit(solution)/shard_map/ppermute | solution.py:39
  58.8 2.3 %collective-permute-start.10 = (f32[512,512]{1,0:T(8,128)}, f32[512,512]{1,0:T(8,128)}, u32[]{:S(2)}, u32[]{:S(2)}) collective-permute-start(f32[512,512]{1,0:T(8,128)} %constant_dynamic-update-slice_fusion.refs_0_), channel_id=1, source_target_pairs={{16,0},{17,1},{18,2},{19,3},{20,4},{21,5},{22,6},{23,7},{24,8},{25... | collective-permute-start | bytes 3145736 | tf_op jit(solution)/shard_map/ppermute | solution.py:39
  61.1 12.7 %count.1 = (bf16[4,4,1024,256]{3,2,1,0:T(8,128)(2,1)}, bf16[4,4,1024,256]{3,2,1,0:T(8,128)(2,1)}, s32[4]{0:T(128)}) custom-call(s32[32,1024]{1,0:T(8,128)} %get-tuple-element.33.row_ref, s32[32,1024]{1,0:T(8,128)} %get-tuple-element.34.col_ref), custom_call_target="tpu_custom_call" | custom-call | flops 100000000 | bytes 1048576 | tf_op jit(solution)/shard_map/count/pallas_call | solution.py:104
  74.2 3.1 %collective-permute-start.11 = (f32[512,512]{1,0:T(8,128)S(1)}, f32[512,512]{1,0:T(8,128)S(1)}, u32[]{:S(2)}, u32[]{:S(2)}) collective-permute-start(f32[512,512]{1,0:T(8,128)S(1)} %collective-permute-done.6.refs_0_), channel_id=1, source_target_pairs={{16,0},{17,1},{18,2},{19,3},{20,4},{21,5},{22,6},{23,7},{24,8},{25... | collective-permute-start | bytes 3145736 | tf_op jit(solution)/shard_map/ppermute | solution.py:39
  77.8 1.1 collective-permute-start.9
  78.9 2.4 %gather.9.refs_0_.rows0 = bf16[4,256,1024]{2,1,0:T(8,128)(2,1)S(1)} custom-call(s32[32,128]{1,0:T(8,128)S(1)} %broadcast_select_fusion.ids_ref, f32[512,512]{1,0:T(8,128)} %constant_dynamic-update-slice_fusion.refs_0_, f32[512,512]{1,0:T(8,128)} %collective-permute-done.10.refs_1_), custom_call_target="tpu_custom_call" | custom-call | flops 1500000000 | bytes 1048576 | tf_op jit(solution)/shard_map/gather/pallas_call | solution.py:151
  81.4 1.3 %gather.10 = (bf16[4,256,1024]{2,1,0:T(8,128)(2,1)S(1)}, bf16[4,256,1024]{2,1,0:T(8,128)(2,1)S(1)}) custom-call(s32[32,128]{1,0:T(8,128)S(1)} %broadcast_select_fusion.ids_ref, f32[512,512]{1,0:T(8,128)S(1)} %collective-permute-done.6.refs_0_, f32[512,512]{1,0:T(8,128)S(1)} %collective-permute-done.11.refs_1_, ...), custom_call_target="tpu_custom_call" | custom-call | flops 3000000000 | bytes 2097152 | tf_op jit(solution)/shard_map/gather/pallas_call | solution.py:151
  82.8 0.9 slice-done.3
  83.7 7.2 %collect.1.x_ref = f32[4,1024,512]{2,1,0:T(8,128)S(1)} custom-call(bf16[4,4,1024,256]{3,2,1,0:T(8,128)(2,1)S(1)} %bitcast.17, bf16[4,256,1024]{2,1,0:T(8,128)(2,1)S(1)} %gather.9.refs_0_.rows0, bf16[4,256,1024]{2,1,0:T(8,128)(2,1)S(1)} %get-tuple-element.43.refs_1_.rows1, bf16[4,256,1024]{2,1,0:T(8,128)(2,1)S(1)} %get-tuple-element.44.refs_2_.rows3), custom_call_target="tpu_custom_call" | custom-call | flops 6600000000 | bytes 3145728 | tf_op jit(solution)/shard_map/collect/pallas_call | solution.py:187
  90.9 1.1 collective-permute-start.13
  92.1 1.4 %collective-permute-done.13.b2 = f32[256,512]{1,0:T(8,128)S(1)} collective-permute-done((f32[256,512]{1,0:T(8,128)S(1)}, f32[256,512]{1,0:T(8,128)S(1)}, u32[]{:S(2)}, u32[]{:S(2)}) %collective-permute-start.13) | collective-permute-done | bytes 524320 | tf_op jit(solution)/shard_map/ppermute | solution.py:39
  93.5 0.7 collective-permute-done.14.b3
  94.3 6.3 %finish.3 = (f32[128,512]{1,0:T(8,128)S(1)}, f32[128,512]{1,0:T(8,128)S(1)}) custom-call(s32[4]{0:T(128)S(1)} %copy-done.1, s32[32,128]{1,0:T(8,128)S(1)} %broadcast_select_fusion.ids_ref, f32[256,512]{1,0:T(8,128)S(1)} %collective-permute-done.8.b0, f32[256,512]{1,0:T(8,128)S(1)} %collective-permute-done.9.b1, f32[256,512]{1,0:T(8,128)S(1)} %collective-permute-done.13.b2, ...), custom_call_target="tpu_custom_call" | custom-call | flops 6000000000 | bytes 2097152 | tf_op jit(solution)/shard_map/finish/pallas_call | solution.py:246
  100.7 1.3 %collective-permute-start.16 = (f32[128,512]{1,0:T(8,128)S(1)}, f32[128,512]{1,0:T(8,128)S(1)}, u32[]{:S(2)}, u32[]{:S(2)}) collective-permute-start(f32[128,512]{1,0:T(8,128)S(1)} %get-tuple-element.51), channel_id=1, source_target_pairs={{96,0},{97,1},{98,2},{99,3},{100,4},{101,5},{102,6},{103,7},{104,8... | collective-permute-start | bytes 786440 | tf_op jit(solution)/shard_map/ppermute | solution.py:39
  102.0 6.5 %finish.2 = (f32[128,512]{1,0:T(8,128)S(1)}, f32[128,512]{1,0:T(8,128)S(1)}) custom-call(s32[4]{0:T(128)S(1)} %copy-done.1, s32[32,128]{1,0:T(8,128)S(1)} %broadcast_select_fusion.ids_ref, f32[256,512]{1,0:T(8,128)S(1)} %collective-permute-done.8.b0, f32[256,512]{1,0:T(8,128)S(1)} %collective-permute-done.9.b1, f32[256,512]{1,0:T(8,128)S(1)} %collective-permute-done.13.b2, ...), custom_call_target="tpu_custom_call" | custom-call | flops 6000000000 | bytes 2097152 | tf_op jit(solution)/shard_map/finish/pallas_call | solution.py:246
  108.5 1.8 %collective-permute-start.17 = (f32[128,512]{1,0:T(8,128)S(1)}, f32[128,512]{1,0:T(8,128)S(1)}, u32[]{:S(2)}, u32[]{:S(2)}) collective-permute-start(f32[128,512]{1,0:T(8,128)S(1)} %get-tuple-element.52), channel_id=1, source_target_pairs={{32,0},{33,1},{34,2},{35,3},{36,4},{37,5},{38,6},{39,7},{40,8},{41... | collective-permute-start | bytes 786440 | tf_op jit(solution)/shard_map/ppermute | solution.py:39
  110.3 5.7 %collective-permute-done.16 = f32[128,512]{1,0:T(8,128)S(1)} collective-permute-done((f32[128,512]{1,0:T(8,128)S(1)}, f32[128,512]{1,0:T(8,128)S(1)}, u32[]{:S(2)}, u32[]{:S(2)}) %collective-permute-start.16) | collective-permute-done | bytes 262176 | tf_op jit(solution)/shard_map/ppermute | solution.py:39
  116.0 0.8 add_add_fusion
  (56 shorter events, 6.7 us)
Async XLA Ops:
  0.0 17.8 %copy-start = (s32[128,1024]{1,0:T(8,128)S(1)}, s32[128,1024]{1,0:T(8,128)}, u32[]{:S(2)}) copy-start(s32[128,1024]{1,0:T(8,128)} %param.7) | copy-start | bytes 1572868
  0.0 11.5 %copy-start.2 = (s32[1,8192]{1,0:T(1,128)S(1)}, s32[1,8192]{1,0:T(1,128)}, u32[]{:S(2)}) copy-start(s32[1,8192]{1,0:T(1,128)} %param.10) | copy-start | bytes 98308
  0.0 11.5 %copy-start.3 = (s32[1,8192]{1,0:T(1,128)S(1)}, s32[1,8192]{1,0:T(1,128)}, u32[]{:S(2)}) copy-start(s32[1,8192]{1,0:T(1,128)} %param.9) | copy-start | bytes 98308
  0.0 41.3 %all-to-all-start = ((f32[128,8,512]{2,1,0:T(8,128)}), f32[128,8,512]{2,1,0:T(8,128)S(1)}, u32[]{:S(2)}, u32[]{:S(2)}) async-start(f32[128,8,512]{2,1,0:T(8,128)} %bitcast.18), calls=%async_computation | async-start | bytes 4194304 | tf_op jit(solution)/shard_map/all_to_all | solution.py:272
  11.6 18.1 %collective-permute-start.3 = (s32[2,8192]{1,0:T(2,128)S(1)}, s32[2,8192]{1,0:T(2,128)S(1)}, u32[]{:S(2)}, u32[]{:S(2)}) collective-permute-start(s32[2,8192]{1,0:T(2,128)S(1)} %get-tuple-element.62), channel_id=1, source_target_pairs={{32,0},{33,1},{34,2},{35,3},{36,4},{37,5},{38,6},{39,7},{40,8},{41... | collective-permute-start | bytes 196616 | tf_op jit(solution)/shard_map/ppermute | solution.py:39
  14.9 23.2 %collective-permute-start.4 = (s32[2,8192]{1,0:T(2,128)S(1)}, s32[2,8192]{1,0:T(2,128)S(1)}, u32[]{:S(2)}, u32[]{:S(2)}) collective-permute-start(s32[2,8192]{1,0:T(2,128)S(1)} %get-tuple-element.62), channel_id=1, source_target_pairs={{64,0},{65,1},{66,2},{67,3},{68,4},{69,5},{70,6},{71,7},{72,8},{73... | collective-permute-start | bytes 196616 | tf_op jit(solution)/shard_map/ppermute | solution.py:39
  15.1 26.1 %collective-permute-start.5 = (s32[2,8192]{1,0:T(2,128)S(1)}, s32[2,8192]{1,0:T(2,128)S(1)}, u32[]{:S(2)}, u32[]{:S(2)}) collective-permute-start(s32[2,8192]{1,0:T(2,128)S(1)} %get-tuple-element.62), channel_id=1, source_target_pairs={{96,0},{97,1},{98,2},{99,3},{100,4},{101,5},{102,6},{103,7},{104,8... | collective-permute-start | bytes 196616 | tf_op jit(solution)/shard_map/ppermute | solution.py:39
  42.2 8.1 %collective-permute-start = (f32[128,512]{1,0:T(8,128)S(1)}, f32[128,512]{1,0:T(8,128)S(1)}, u32[]{:S(2)}, u32[]{:S(2)}) collective-permute-start(f32[128,512]{1,0:T(8,128)S(1)} %fusion), channel_id=1, source_target_pairs={{4,0},{5,1},{6,2},{7,3},{8,4},{9,5},{10,6},{11,7},{12,8},{13,9},{1... | collective-permute-start | bytes 786440 | tf_op jit(solution)/shard_map/ppermute | solution.py:39
  44.1 7.1 %collective-permute-start.1 = (f32[128,512]{1,0:T(8,128)S(1)}, f32[128,512]{1,0:T(8,128)S(1)}, u32[]{:S(2)}, u32[]{:S(2)}) collective-permute-start(f32[128,512]{1,0:T(8,128)S(1)} %fusion), channel_id=1, source_target_pairs={{8,0},{9,1},{10,2},{11,3},{12,4},{13,5},{14,6},{15,7},{0,8},{1,9},... | collective-permute-start | bytes 786440 | tf_op jit(solution)/shard_map/ppermute | solution.py:39
  44.6 9.4 %collective-permute-start.2 = (f32[128,512]{1,0:T(8,128)S(1)}, f32[128,512]{1,0:T(8,128)S(1)}, u32[]{:S(2)}, u32[]{:S(2)}) collective-permute-start(f32[128,512]{1,0:T(8,128)S(1)} %fusion), channel_id=1, source_target_pairs={{12,0},{13,1},{14,2},{15,3},{0,4},{1,5},{2,6},{3,7},{4,8},{5,9},{6... | collective-permute-start | bytes 786440 | tf_op jit(solution)/shard_map/ppermute | solution.py:39
  56.8 17.0 %collective-permute-start.6 = (f32[512,512]{1,0:T(8,128)}, f32[512,512]{1,0:T(8,128)S(1)}, u32[]{:S(2)}, u32[]{:S(2)}) collective-permute-start(f32[512,512]{1,0:T(8,128)} %constant_dynamic-update-slice_fusion.refs_0_), channel_id=1, source_target_pairs={{1,0},{2,1},{3,2},{0,3},{5,4},{6,5},{7,6},{4,7},{9,8},{10,9},{11,1... | collective-permute-start | bytes 3145736 | tf_op jit(solution)/shard_map/ppermute | solution.py:39
  58.8 15.4 %collective-permute-start.7 = (f32[512,512]{1,0:T(8,128)}, f32[512,512]{1,0:T(8,128)S(1)}, u32[]{:S(2)}, u32[]{:S(2)}) collective-permute-start(f32[512,512]{1,0:T(8,128)} %constant_dynamic-update-slice_fusion.refs_0_), channel_id=1, source_target_pairs={{3,0},{0,1},{1,2},{2,3},{7,4},{4,5},{5,6},{6,7},{11,8},{8,9},{9,10... | collective-permute-start | bytes 3145736 | tf_op jit(solution)/shard_map/ppermute | solution.py:39
  58.8 20.1 %collective-permute-start.10 = (f32[512,512]{1,0:T(8,128)}, f32[512,512]{1,0:T(8,128)}, u32[]{:S(2)}, u32[]{:S(2)}) collective-permute-start(f32[512,512]{1,0:T(8,128)} %constant_dynamic-update-slice_fusion.refs_0_), channel_id=1, source_target_pairs={{16,0},{17,1},{18,2},{19,3},{20,4},{21,5},{22,6},{23,7},{24,8},{25... | collective-permute-start | bytes 3145736 | tf_op jit(solution)/shard_map/ppermute | solution.py:39
  74.2 7.2 %collective-permute-start.11 = (f32[512,512]{1,0:T(8,128)S(1)}, f32[512,512]{1,0:T(8,128)S(1)}, u32[]{:S(2)}, u32[]{:S(2)}) collective-permute-start(f32[512,512]{1,0:T(8,128)S(1)} %collective-permute-done.6.refs_0_), channel_id=1, source_target_pairs={{16,0},{17,1},{18,2},{19,3},{20,4},{21,5},{22,6},{23,7},{24,8},{25... | collective-permute-start | bytes 3145736 | tf_op jit(solution)/shard_map/ppermute | solution.py:39
  77.3 4.1 %collective-permute-start.12 = (f32[512,512]{1,0:T(8,128)S(1)}, f32[512,512]{1,0:T(8,128)S(1)}, u32[]{:S(2)}, u32[]{:S(2)}) collective-permute-start(f32[512,512]{1,0:T(8,128)S(1)} %collective-permute-done.7.refs_2_), channel_id=1, source_target_pairs={{16,0},{17,1},{18,2},{19,3},{20,4},{21,5},{22,6},{23,7},{24,8},{25... | collective-permute-start | bytes 3145736 | tf_op jit(solution)/shard_map/ppermute | solution.py:39
  77.4 13.4 %collective-permute-start.8 = (f32[256,512]{1,0:T(8,128)S(1)}, f32[256,512]{1,0:T(8,128)S(1)}, u32[]{:S(2)}, u32[]{:S(2)}) collective-permute-start(f32[256,512]{1,0:T(8,128)S(1)} %slice.14), channel_id=1, source_target_pairs={{1,0},{2,1},{3,2},{0,3},{5,4},{6,5},{7,6},{4,7},{9,8},{10,9},{11,1... | collective-permute-start | bytes 1572872 | tf_op jit(solution)/shard_map/ppermute | solution.py:39
  77.8 13.0 %collective-permute-start.9 = (f32[256,512]{1,0:T(8,128)S(1)}, f32[256,512]{1,0:T(8,128)S(1)}, u32[]{:S(2)}, u32[]{:S(2)}) collective-permute-start(f32[256,512]{1,0:T(8,128)S(1)} %slice.15), channel_id=1, source_target_pairs={{3,0},{0,1},{1,2},{2,3},{7,4},{4,5},{5,6},{6,7},{11,8},{8,9},{9,10... | collective-permute-start | bytes 1572872 | tf_op jit(solution)/shard_map/ppermute | solution.py:39
  78.9 3.8 %slice-start.2 = ((s8[8388608]{0:T(1024)(128)(4,1)}), s8[4194304]{0:T(1024)(128)(4,1)S(1)}, s32[]{:S(2)}) async-start(s8[8388608]{0:T(1024)(128)(4,1)} %bitcast.16), calls=%async_computation.3 | async-start | bytes 8388608
  81.4 2.3 %slice-start.3 = ((s8[8388608]{0:T(1024)(128)(4,1)}), s8[4194304]{0:T(1024)(128)(4,1)S(1)}, s32[]{:S(2)}) async-start(s8[8388608]{0:T(1024)(128)(4,1)} %bitcast.16), calls=%async_computation.4 | async-start | bytes 8388608
  82.7 11.6 %slice-start = ((s8[8388608]{0:T(1024)(128)(4,1)}), s8[4194304]{0:T(1024)(128)(4,1)S(1)}, s32[]{:S(2)}) async-start(s8[8388608]{0:T(1024)(128)(4,1)} %bitcast.14), calls=%async_computation.1 | async-start | bytes 8388608
  83.7 10.6 %slice-start.1 = ((s8[8388608]{0:T(1024)(128)(4,1)}), s8[4194304]{0:T(1024)(128)(4,1)S(1)}, s32[]{:S(2)}) async-start(s8[8388608]{0:T(1024)(128)(4,1)} %bitcast.14), calls=%async_computation.2 | async-start | bytes 8388608
  83.7 10.6 %copy-start.1 = (s32[4]{0:T(128)S(1)}, s32[4]{0:T(128)}, u32[]{:S(2)}) copy-start(s32[4]{0:T(128)} %get-tuple-element.38.flag_ref) | copy-start | bytes 52
  90.9 2.7 %collective-permute-start.13 = (f32[256,512]{1,0:T(8,128)S(1)}, f32[256,512]{1,0:T(8,128)S(1)}, u32[]{:S(2)}, u32[]{:S(2)}) collective-permute-start(f32[256,512]{1,0:T(8,128)S(1)} %collective-permute-done.8.b0), channel_id=1, source_target_pairs={{16,0},{17,1},{18,2},{19,3},{20,4},{21,5},{22,6},{23,7},{24,8},{25... | collective-permute-start | bytes 1572872 | tf_op jit(solution)/shard_map/ppermute | solution.py:39
  92.0 2.3 %collective-permute-start.14 = (f32[256,512]{1,0:T(8,128)S(1)}, f32[256,512]{1,0:T(8,128)S(1)}, u32[]{:S(2)}, u32[]{:S(2)}) collective-permute-start(f32[256,512]{1,0:T(8,128)S(1)} %collective-permute-done.9.b1), channel_id=1, source_target_pairs={{16,0},{17,1},{18,2},{19,3},{20,4},{21,5},{22,6},{23,7},{24,8},{25... | collective-permute-start | bytes 1572872 | tf_op jit(solution)/shard_map/ppermute | solution.py:39
  100.6 9.7 %collective-permute-start.15 = (f32[128,512]{1,0:T(8,128)S(1)}, f32[128,512]{1,0:T(8,128)S(1)}, u32[]{:S(2)}, u32[]{:S(2)}) collective-permute-start(f32[128,512]{1,0:T(8,128)S(1)} %get-tuple-element.50), channel_id=1, source_target_pairs={{64,0},{65,1},{66,2},{67,3},{68,4},{69,5},{70,6},{71,7},{72,8},{73... | collective-permute-start | bytes 786440 | tf_op jit(solution)/shard_map/ppermute | solution.py:39
  100.7 15.4 %collective-permute-start.16 = (f32[128,512]{1,0:T(8,128)S(1)}, f32[128,512]{1,0:T(8,128)S(1)}, u32[]{:S(2)}, u32[]{:S(2)}) collective-permute-start(f32[128,512]{1,0:T(8,128)S(1)} %get-tuple-element.51), channel_id=1, source_target_pairs={{96,0},{97,1},{98,2},{99,3},{100,4},{101,5},{102,6},{103,7},{104,8... | collective-permute-start | bytes 786440 | tf_op jit(solution)/shard_map/ppermute | solution.py:39
  108.5 7.5 %collective-permute-start.17 = (f32[128,512]{1,0:T(8,128)S(1)}, f32[128,512]{1,0:T(8,128)S(1)}, u32[]{:S(2)}, u32[]{:S(2)}) collective-permute-start(f32[128,512]{1,0:T(8,128)S(1)} %get-tuple-element.52), channel_id=1, source_target_pairs={{32,0},{33,1},{34,2},{35,3},{36,4},{37,5},{38,6},{39,7},{40,8},{41... | collective-permute-start | bytes 786440 | tf_op jit(solution)/shard_map/ppermute | solution.py:39

commit v4 on v3

--- a/solution.py
+++ b/solution.py
@@ -18,7 +18,6 @@
 BLOCK = CORES * RING * PER
 BF16 = jnp.bfloat16
 F32 = jnp.float32
-HBM = pl.BlockSpec(memory_space=pltpu.HBM)
 SMEM = pl.BlockSpec(memory_space=pltpu.SMEM)
 VMEM = pl.BlockSpec(memory_space=pltpu.VMEM)
 LIMIT = 16
@@ -60,59 +59,43 @@
     return high, (value - high.astype(F32)).astype(BF16)
 
 
-def count_kernel(row_ref, col_ref, out_ref, rest_hbm, flag_ref, rest_ref):
+def counts_of(row_ref, col_ref, step):
+    inner = row_ref.shape[1]
+    rows = lax.broadcasted_iota(jnp.int32, (RING // 2 * OCT, inner), 0)
+    cols = lax.broadcasted_iota(jnp.int32, (2 * BLOCK, inner), 0)
+    row_hot = jnp.where(rows == row_ref[pl.ds(step, 1), :], 1.0, 0.0).astype(BF16)
+    col_hot = jnp.where(cols == col_ref[pl.ds(step, 1), :], 1.0, 0.0).astype(BF16)
+    counts = lax.dot_general(
+        row_hot, col_hot, (((1,), (1,)), ((), ())), preferred_element_type=F32
+    )
+    return jnp.concatenate([counts[:OCT], counts[OCT:]], axis=1)
+
+
+def count_kernel(row_ref, col_ref, out_ref, flag_ref):
     reader = pl.program_id(0)
-    inner = row_ref.shape[1]
-
-    def counts_of(d):
-        rows = lax.broadcasted_iota(jnp.int32, (RING // 2 * OCT, inner), 0)
-        cols = lax.broadcasted_iota(jnp.int32, (2 * BLOCK, inner), 0)
-        step = reader * DIRS + d
-        row_hot = jnp.where(rows == row_ref[pl.ds(step, 1), :], 1.0, 0.0).astype(BF16)
-        col_hot = jnp.where(cols == col_ref[pl.ds(step, 1), :], 1.0, 0.0).astype(BF16)
-        return lax.dot_general(
-            row_hot, col_hot, (((1,), (1,)), ((), ())), preferred_element_type=F32
-        )
-
     tops = []
     for d in range(DIRS):
-        counts = counts_of(d)
-        rounded = counts.astype(BF16)
+        counts = counts_of(row_ref, col_ref, reader * DIRS + d)
         for s in range(RING):
-            i, j = s // 2 * OCT, s % 2 * BLOCK
-            out_ref[s, 0, d * OCT : (d + 1) * OCT, :] = rounded[i : i + OCT, j : j + BLOCK]
+            block = counts[:, s * BLOCK : (s + 1) * BLOCK]
+            out_ref[s, 0, d * OCT : (d + 1) * OCT, :] = block.astype(BF16)
         tops.append(jnp.max(counts, axis=0, keepdims=True))
     large = jnp.max(functools.reduce(jnp.maximum, tops)) > 256.0
     flag_ref[reader] = large.astype(jnp.int32)
 
-    @pl.when(large)
-    def _():
-        @pl.loop(0, DIRS)
-        def _(d):
-            counts = counts_of(d)
-            rest = (counts - counts.astype(BF16).astype(F32)).astype(BF16)
-            for s in range(RING):
-                i, j = s // 2 * OCT, s % 2 * BLOCK
-                rest_ref[s] = rest[i : i + OCT, j : j + BLOCK]
-            start = pl.multiple_of(d * OCT, OCT)
-            pltpu.sync_copy(rest_ref, rest_hbm.at[:, reader, pl.ds(start, OCT), :])
-
 
 def count(row_codes, col_codes):
-    steps, inner = row_codes.shape
-    shape = (RING, RING, DIRS * OCT, BLOCK)
+    codes = pl.BlockSpec(row_codes.shape, lambda k: (0, 0))
     return pl.pallas_call(
         count_kernel,
         grid=(RING,),
-        in_specs=[pl.BlockSpec((steps, inner), lambda k: (0, 0))] * 2,
-        out_specs=[pl.BlockSpec((RING, 1, DIRS * OCT, BLOCK), lambda k: (0, k, 0, 0)), HBM, SMEM],
+        in_specs=[codes, codes],
+        out_specs=[pl.BlockSpec((RING, 1, DIRS * OCT, BLOCK), lambda k: (0, k, 0, 0)), SMEM],
         out_shape=[
-            jax.ShapeDtypeStruct(shape, BF16),
-            jax.ShapeDtypeStruct(shape, BF16),
+            jax.ShapeDtypeStruct((RING, RING, DIRS * OCT, BLOCK), BF16),
             jax.ShapeDtypeStruct((RING,), jnp.int32),
         ],
-        scratch_shapes=[pltpu.VMEM((RING, OCT, BLOCK), BF16)],
-        compiler_params=pltpu.CompilerParams(vmem_limit_bytes=60 << 20),
+        compiler_params=pltpu.CompilerParams(vmem_limit_bytes=20 << 20),
         cost_estimate=pl.CostEstimate(
             flops=100_000_000, bytes_accessed=1 << 20, transcendentals=0
         ),
@@ -198,9 +181,8 @@
 
 
 def finish_kernel(
-    readers, flag_ref, ids_ref, b0, b1, b2, b3, x_ref, rows0, rows1, rows3, count_ref, k_ref, rest_hbm,
-    out0, out1,
-    rows2, xh, xl, rest,
+    readers, flag_ref, ids_ref, b0, b1, b2, b3, x_ref, rows0, rows1, rows3, count_ref, k_ref,
+    row_ref, col_ref, out0, out1, rows2, xh, xl,
 ):
     def store(owner, k, values):
         rows2[k, owner * PER : (owner + 1) * PER, :] = values
@@ -220,10 +202,10 @@
         def _():
             @pl.loop(0, DIRS)
             def _(d):
-                start = pl.multiple_of(d * OCT, OCT)
-                pltpu.sync_copy(rest_hbm.at[:, k, pl.ds(start, OCT), :], rest)
+                exact = counts_of(row_ref, col_ref, k * DIRS + d)
+                rest = (exact - exact.astype(BF16).astype(F32)).astype(BF16)
                 rows = [ref[k] for ref in (rows0, rows1, rows2, rows3)]
-                total = product([rest[s] for s in range(RING)], rows)
+                total = product([rest], rows)
                 total += xh[d, there, :].astype(F32) + xl[d, there, :].astype(F32)
                 high, low = parts(total)
                 xh[d, there, :] = high
@@ -241,25 +223,24 @@
         out[...] = total[i * OCT : (i + 1) * OCT]
 
 
-def finish(readers, flags, ids, arrays, x, rows, counts, kernels, rest):
+def finish(readers, flags, ids, arrays, x, rows, counts, kernels, codes):
     n = len(readers)
     return pl.pallas_call(
         functools.partial(finish_kernel, readers),
-        in_specs=[SMEM] + [VMEM] * 11 + [HBM],
+        in_specs=[SMEM] + [VMEM] * 13,
         out_specs=[VMEM] * 2,
         out_shape=[jax.ShapeDtypeStruct((OCT, WIDTH), F32)] * 2,
         scratch_shapes=[
             pltpu.VMEM((RING, BLOCK, 2 * WIDTH), BF16),
             pltpu.VMEM((DIRS, n * OCT, WIDTH), BF16),
             pltpu.VMEM((DIRS, n * OCT, WIDTH), BF16),
-            pltpu.VMEM((RING, OCT, BLOCK), BF16),
         ],
         compiler_params=pltpu.CompilerParams(vmem_limit_bytes=LIMIT << 20),
         cost_estimate=pl.CostEstimate(
             flops=6_000_000_000, bytes_accessed=2 << 20, transcendentals=0
         ),
         name="finish",
-    )(flags, ids, *arrays, x, *rows, counts, kernels, rest)
+    )(flags, ids, *arrays, x, *rows, counts, kernels, *codes)
 
 
 def body(partials, partial_ids, read_lists, sources, targets, kernels):
@@ -316,17 +297,17 @@
     line, codes, ids = lax.optimization_barrier((line, codes, ids))
     line = jnp.concatenate(line, axis=0)
     near1, near3 = along_s(line, 1), along_s(line, 3)
-    counts, rest, flags = count(*codes)
-    near1, near3, counts, rest, flags = lax.optimization_barrier(
-        (near1, near3, counts, rest, flags)
+    counts, flags = count(*codes)
+    (rows0,) = gather((0,), ids, [line, across(line)])
+    near1, near3, counts, flags, rows0 = lax.optimization_barrier(
+        (near1, near3, counts, flags, rows0)
     )
     low, high = along_s(near1[: 2 * OCT], 1), along_s(near3[2 * OCT :], 3)
-    (rows0,) = gather((0,), ids, [line, across(line)])
     rows1, rows3 = gather((1, 3), ids, [near1, across(near1), near3, across(near3)])
     rows = (rows0, rows1, rows3)
     x = collect((0, 1, 3), counts, rows)
     low, high, x = lax.optimization_barrier((low, high, x))
-    last = (flags, ids, [low, high, across(low), across(high)], x, rows, counts, kernels, rest)
+    last = (flags, ids, [low, high, across(low), across(high)], x, rows, counts, kernels, codes)
     out2, out1 = finish((2, 1), *last)
     out3, out0 = finish((3, 0), *last)
     return out0 + along_z(out2, -2) + along_z(out1, -1) + along_z(out3, -3)

time: 117 us -> 112 us (0.957)
  local copies, waits for them, and re-layouts: 6.65 us -> 2.92 us
  Pallas kernels: 36.4 us -> 33.1 us
  waiting for transfers between devices: 38 us -> 41.3 us
    ppermute x18, waiting for transfers between devices: 37.9 us -> 41.3 us  [fetch(): return lax.ppermute(value, AXES, pairs)]
    unnamed x19 -> x13, local copies, waits for them, and re-layouts: 3.11 us -> 0.08 us
    pallas_call x2, Pallas kernels: 3.74 us -> 2.05 us  [gather(): pl.pallas_call(functools.partial(gather_kernel, blocks), in_specs=[VMEM]...]
    pallas_call x1, Pallas kernels: 12.7 us -> 11.3 us  [count(): pl.pallas_call(count_kernel, grid=(RING,), in_specs=[codes, codes], out_s...]
  transfers between devices with their start and end apart: 19 -> 19, of which waited for: 11 -> 13; matrix products, arithmetic and copies ran while one was open for 4% -> 3% of each run, Pallas kernels for 26% -> 24%
where the time goes in v4:
time: 112 us
  waiting for transfers between devices  41.3 us (37%)
  Pallas kernels  33.1 us (30%)
  starting transfers between devices  31.8 us (28%)
  local copies, waits for them, and re-layouts  2.92 us (3%)
  other arithmetic  1.72 us (2%)
    ppermute x18, waiting for transfers between devices, fetch(): return lax.ppermute(value, AXES, pairs)  41.3 us
    ppermute x18, starting transfers between devices, fetch(): return lax.ppermute(value, AXES, pairs)  20.3 us
    pallas_call x2, Pallas kernels, finish(): pl.pallas_call(functools.partial(finish_kernel, readers), in_specs=[SMEM]...  12.5 us
    all_to_all x1, starting transfers between devices, body(): lax.all_to_all(partials, AXES, split_axis=0, concat_axis=0, tiled=True)  11.5 us
    pallas_call x1, Pallas kernels, count(): pl.pallas_call(count_kernel, grid=(RING,), in_specs=[codes, codes], out_s...  11.3 us
    pallas_call x1, Pallas kernels, collect(): pl.pallas_call(functools.partial(collect_kernel, blocks), in_specs=[VMEM]...  7.26 us
  transfers between devices with their start and end apart: 19, of which 13 were waited for; matrix products, arithmetic and copies ran while one was open for 3% of the time, Pallas kernels for 24%

profile of v4, /device:TPU:1, one launch (start us, length us, event | category | flops | bytes accessed | tf_op | source)
XLA Modules:
  0.0 112.0 jit_solution(4881032628943844211)
XLA Ops:
  0.0 11.5 %all-to-all-start = ((f32[128,8,512]{2,1,0:T(8,128)}), f32[128,8,512]{2,1,0:T(8,128)S(1)}, u32[]{:S(2)}, u32[]{:S(2)}) async-start(f32[128,8,512]{2,1,0:T(8,128)} %bitcast.16), calls=%async_computation | async-start | bytes 4194304 | tf_op jit(solution)/shard_map/all_to_all | solution.py:253
  11.6 3.3 %collective-permute-start.3 = (s32[2,8192]{1,0:T(2,128)S(1)}, s32[2,8192]{1,0:T(2,128)S(1)}, u32[]{:S(2)}, u32[]{:S(2)}) collective-permute-start(s32[2,8192]{1,0:T(2,128)S(1)} %get-tuple-element.60), channel_id=1, source_target_pairs={{32,0},{33,1},{34,2},{35,3},{36,4},{37,5},{38,6},{39,7},{40,8},{41... | collective-permute-start | bytes 196616 | tf_op jit(solution)/shard_map/ppermute | solution.py:38
  15.1 0.8 collective-permute-start.5
  15.8 0.9 fusion.50
  17.9 11.8 %collective-permute-done.3 = s32[2,8192]{1,0:T(2,128)S(1)} collective-permute-done((s32[2,8192]{1,0:T(2,128)S(1)}, s32[2,8192]{1,0:T(2,128)S(1)}, u32[]{:S(2)}, u32[]{:S(2)}) %collective-permute-start.3) | collective-permute-done | bytes 65568 | tf_op jit(solution)/shard_map/ppermute | solution.py:38
  29.7 8.4 %collective-permute-done.4 = s32[2,8192]{1,0:T(2,128)S(1)} collective-permute-done((s32[2,8192]{1,0:T(2,128)S(1)}, s32[2,8192]{1,0:T(2,128)S(1)}, u32[]{:S(2)}, u32[]{:S(2)}) %collective-permute-start.4) | collective-permute-done | bytes 65568 | tf_op jit(solution)/shard_map/ppermute | solution.py:38
  38.1 3.0 %collective-permute-done.5 = s32[2,8192]{1,0:T(2,128)S(1)} collective-permute-done((s32[2,8192]{1,0:T(2,128)S(1)}, s32[2,8192]{1,0:T(2,128)S(1)}, u32[]{:S(2)}, u32[]{:S(2)}) %collective-permute-start.5) | collective-permute-done | bytes 65568 | tf_op jit(solution)/shard_map/ppermute | solution.py:38
  41.3 0.9 fusion
  42.2 1.9 %collective-permute-start = (f32[128,512]{1,0:T(8,128)S(1)}, f32[128,512]{1,0:T(8,128)S(1)}, u32[]{:S(2)}, u32[]{:S(2)}) collective-permute-start(f32[128,512]{1,0:T(8,128)S(1)} %fusion), channel_id=1, source_target_pairs={{4,0},{5,1},{6,2},{7,3},{8,4},{9,5},{10,6},{11,7},{12,8},{13,9},{1... | collective-permute-start | bytes 786440 | tf_op jit(solution)/shard_map/ppermute | solution.py:38
  44.6 0.7 collective-permute-start.2
  45.3 0.7 slice_reduce_fusion.1
  46.8 3.4 %collective-permute-done = f32[128,512]{1,0:T(8,128)S(1)} collective-permute-done((f32[128,512]{1,0:T(8,128)S(1)}, f32[128,512]{1,0:T(8,128)S(1)}, u32[]{:S(2)}, u32[]{:S(2)}) %collective-permute-start) | collective-permute-done | bytes 262176 | tf_op jit(solution)/shard_map/ppermute | solution.py:38
  50.2 0.9 collective-permute-done.1
  51.2 2.8 %collective-permute-done.2 = f32[128,512]{1,0:T(8,128)S(1)} collective-permute-done((f32[128,512]{1,0:T(8,128)S(1)}, f32[128,512]{1,0:T(8,128)S(1)}, u32[]{:S(2)}, u32[]{:S(2)}) %collective-permute-start.2) | collective-permute-done | bytes 262176 | tf_op jit(solution)/shard_map/ppermute | solution.py:38
  54.1 1.8 %collective-permute-start.8 = (f32[512,512]{1,0:T(8,128)S(1)}, f32[512,512]{1,0:T(8,128)S(1)}, u32[]{:S(2)}, u32[]{:S(2)}) collective-permute-start(f32[512,512]{1,0:T(8,128)S(1)} %constant_dynamic-update-slice_fusion.refs_0_), channel_id=1, source_target_pairs={{16,0},{17,1},{18,2},{19,3},{20,4},{21,5},{22,6},{23,7},{24,8},{25... | collective-permute-start | bytes 3145736 | tf_op jit(solution)/shard_map/ppermute | solution.py:38
  56.2 1.1 %collective-permute-start.7 = (f32[512,512]{1,0:T(8,128)S(1)}, f32[512,512]{1,0:T(8,128)S(1)}, u32[]{:S(2)}, u32[]{:S(2)}) collective-permute-start(f32[512,512]{1,0:T(8,128)S(1)} %constant_dynamic-update-slice_fusion.refs_0_), channel_id=1, source_target_pairs={{3,0},{0,1},{1,2},{2,3},{7,4},{4,5},{5,6},{6,7},{11,8},{8,9},{9,10... | collective-permute-start | bytes 3145736 | tf_op jit(solution)/shard_map/ppermute | solution.py:38
  57.4 11.3 %count.1 = (bf16[4,4,1024,256]{3,2,1,0:T(8,128)(2,1)S(1)}, s32[4]{0:T(128)S(1)}) custom-call(s32[32,1024]{1,0:T(8,128)S(1)} %get-tuple-element.32.row_ref, s32[32,1024]{1,0:T(8,128)S(1)} %get-tuple-element.33.col_ref), custom_call_target="tpu_custom_call" | custom-call | flops 100000000 | bytes 1048576 | tf_op jit(solution)/shard_map/count/pallas_call | solution.py:89
  68.7 0.8 gather.9.refs_0_.rows0
  69.8 1.5 %collective-permute-done.7.refs_2_ = f32[512,512]{1,0:T(8,128)S(1)} collective-permute-done((f32[512,512]{1,0:T(8,128)S(1)}, f32[512,512]{1,0:T(8,128)S(1)}, u32[]{:S(2)}, u32[]{:S(2)}) %collective-permute-start.7) | collective-permute-done | bytes 1048608 | tf_op jit(solution)/shard_map/ppermute | solution.py:38
  71.4 3.1 %collective-permute-start.11 = (f32[512,512]{1,0:T(8,128)S(1)}, f32[512,512]{1,0:T(8,128)S(1)}, u32[]{:S(2)}, u32[]{:S(2)}) collective-permute-start(f32[512,512]{1,0:T(8,128)S(1)} %collective-permute-done.6.refs_0_), channel_id=1, source_target_pairs={{16,0},{17,1},{18,2},{19,3},{20,4},{21,5},{22,6},{23,7},{24,8},{25... | collective-permute-start | bytes 3145736 | tf_op jit(solution)/shard_map/ppermute | solution.py:38
  74.7 2.7 %collective-permute-start.9 = (f32[256,512]{1,0:T(8,128)S(1)}, f32[256,512]{1,0:T(8,128)S(1)}, u32[]{:S(2)}, u32[]{:S(2)}) collective-permute-start(f32[256,512]{1,0:T(8,128)S(1)} %slice.14), channel_id=1, source_target_pairs={{1,0},{2,1},{3,2},{0,3},{5,4},{6,5},{7,6},{4,7},{9,8},{10,9},{11,1... | collective-permute-start | bytes 1572872 | tf_op jit(solution)/shard_map/ppermute | solution.py:38
  77.3 1.0 collective-permute-done.12.refs_3_
  78.3 1.3 %gather.10 = (bf16[4,256,1024]{2,1,0:T(8,128)(2,1)S(1)}, bf16[4,256,1024]{2,1,0:T(8,128)(2,1)S(1)}) custom-call(s32[32,128]{1,0:T(8,128)S(1)} %broadcast_select_fusion.ids_ref, f32[512,512]{1,0:T(8,128)S(1)} %collective-permute-done.6.refs_0_, f32[512,512]{1,0:T(8,128)S(1)} %collective-permute-done.11.refs_1_, ...), custom_call_target="tpu_custom_call" | custom-call | flops 3000000000 | bytes 2097152 | tf_op jit(solution)/shard_map/gather/pallas_call | solution.py:134
  79.6 7.3 %collect.1.x_ref = f32[4,1024,512]{2,1,0:T(8,128)S(1)} custom-call(bf16[4,4,1024,256]{3,2,1,0:T(8,128)(2,1)S(1)} %get-tuple-element.40.count_ref, bf16[4,256,1024]{2,1,0:T(8,128)(2,1)S(1)} %gather.9.refs_0_.rows0, bf16[4,256,1024]{2,1,0:T(8,128)(2,1)S(1)} %get-tuple-element.42.refs_1_.rows1, bf16[4,256,1024]{2,1,0:T(8,128)(2,1)S(1)} %get-tuple-element.43.refs_2_.rows3), custom_call_target="tpu_custom_call" | custom-call | flops 6600000000 | bytes 3145728 | tf_op jit(solution)/shard_map/collect/pallas_call | solution.py:170
  87.5 1.4 %collective-permute-done.13.b2 = f32[256,512]{1,0:T(8,128)S(1)} collective-permute-done((f32[256,512]{1,0:T(8,128)S(1)}, f32[256,512]{1,0:T(8,128)S(1)}, u32[]{:S(2)}, u32[]{:S(2)}) %collective-permute-start.13) | collective-permute-done | bytes 524320 | tf_op jit(solution)/shard_map/ppermute | solution.py:38
  88.9 0.7 collective-permute-done.14.b3
  89.7 6.1 %finish.3 = (f32[128,512]{1,0:T(8,128)S(1)}, f32[128,512]{1,0:T(8,128)S(1)}) custom-call(s32[4]{0:T(128)S(1)} %get-tuple-element.37.flag_ref, s32[32,128]{1,0:T(8,128)S(1)} %broadcast_select_fusion.ids_ref, f32[256,512]{1,0:T(8,128)S(1)} %collective-permute-done.9.b0, f32[256,512]{1,0:T(8,128)S(1)} %collective-permute-done.10.b1, ...), custom_call_target="tpu_custom_call" | custom-call | flops 6000000000 | bytes 2097152 | tf_op jit(solution)/shard_map/finish/pallas_call | solution.py:228
  95.9 1.3 %collective-permute-start.16 = (f32[128,512]{1,0:T(8,128)S(1)}, f32[128,512]{1,0:T(8,128)S(1)}, u32[]{:S(2)}, u32[]{:S(2)}) collective-permute-start(f32[128,512]{1,0:T(8,128)S(1)} %get-tuple-element.49), channel_id=1, source_target_pairs={{96,0},{97,1},{98,2},{99,3},{100,4},{101,5},{102,6},{103,7},{104,8... | collective-permute-start | bytes 786440 | tf_op jit(solution)/shard_map/ppermute | solution.py:38
  97.2 6.4 %finish.2 = (f32[128,512]{1,0:T(8,128)S(1)}, f32[128,512]{1,0:T(8,128)S(1)}) custom-call(s32[4]{0:T(128)S(1)} %get-tuple-element.37.flag_ref, s32[32,128]{1,0:T(8,128)S(1)} %broadcast_select_fusion.ids_ref, f32[256,512]{1,0:T(8,128)S(1)} %collective-permute-done.9.b0, f32[256,512]{1,0:T(8,128)S(1)} %collective-permute-done.10.b1, ...), custom_call_target="tpu_custom_call" | custom-call | flops 6000000000 | bytes 2097152 | tf_op jit(solution)/shard_map/finish/pallas_call | solution.py:228
  103.6 1.8 %collective-permute-start.17 = (f32[128,512]{1,0:T(8,128)S(1)}, f32[128,512]{1,0:T(8,128)S(1)}, u32[]{:S(2)}, u32[]{:S(2)}) collective-permute-start(f32[128,512]{1,0:T(8,128)S(1)} %get-tuple-element.50), channel_id=1, source_target_pairs={{32,0},{33,1},{34,2},{35,3},{36,4},{37,5},{38,6},{39,7},{40,8},{41... | collective-permute-start | bytes 786440 | tf_op jit(solution)/shard_map/ppermute | solution.py:38
  105.4 5.8 %collective-permute-done.16 = f32[128,512]{1,0:T(8,128)S(1)} collective-permute-done((f32[128,512]{1,0:T(8,128)S(1)}, f32[128,512]{1,0:T(8,128)S(1)}, u32[]{:S(2)}, u32[]{:S(2)}) %collective-permute-start.16) | collective-permute-done | bytes 262176 | tf_op jit(solution)/shard_map/ppermute | solution.py:38
  111.3 0.8 add_add_fusion
  (49 shorter events, 4.4 us)
Async XLA Ops:
  0.0 17.8 %copy-start = (s32[128,1024]{1,0:T(8,128)S(1)}, s32[128,1024]{1,0:T(8,128)}, u32[]{:S(2)}) copy-start(s32[128,1024]{1,0:T(8,128)} %param.7) | copy-start | bytes 1572868
  0.0 11.5 %copy-start.1 = (s32[1,8192]{1,0:T(1,128)S(1)}, s32[1,8192]{1,0:T(1,128)}, u32[]{:S(2)}) copy-start(s32[1,8192]{1,0:T(1,128)} %param.10) | copy-start | bytes 98308
  0.0 11.5 %copy-start.2 = (s32[1,8192]{1,0:T(1,128)S(1)}, s32[1,8192]{1,0:T(1,128)}, u32[]{:S(2)}) copy-start(s32[1,8192]{1,0:T(1,128)} %param.9) | copy-start | bytes 98308
  0.0 41.3 %all-to-all-start = ((f32[128,8,512]{2,1,0:T(8,128)}), f32[128,8,512]{2,1,0:T(8,128)S(1)}, u32[]{:S(2)}, u32[]{:S(2)}) async-start(f32[128,8,512]{2,1,0:T(8,128)} %bitcast.16), calls=%async_computation | async-start | bytes 4194304 | tf_op jit(solution)/shard_map/all_to_all | solution.py:253
  11.6 18.1 %collective-permute-start.3 = (s32[2,8192]{1,0:T(2,128)S(1)}, s32[2,8192]{1,0:T(2,128)S(1)}, u32[]{:S(2)}, u32[]{:S(2)}) collective-permute-start(s32[2,8192]{1,0:T(2,128)S(1)} %get-tuple-element.60), channel_id=1, source_target_pairs={{32,0},{33,1},{34,2},{35,3},{36,4},{37,5},{38,6},{39,7},{40,8},{41... | collective-permute-start | bytes 196616 | tf_op jit(solution)/shard_map/ppermute | solution.py:38
  14.9 23.2 %collective-permute-start.4 = (s32[2,8192]{1,0:T(2,128)S(1)}, s32[2,8192]{1,0:T(2,128)S(1)}, u32[]{:S(2)}, u32[]{:S(2)}) collective-permute-start(s32[2,8192]{1,0:T(2,128)S(1)} %get-tuple-element.60), channel_id=1, source_target_pairs={{64,0},{65,1},{66,2},{67,3},{68,4},{69,5},{70,6},{71,7},{72,8},{73... | collective-permute-start | bytes 196616 | tf_op jit(solution)/shard_map/ppermute | solution.py:38
  15.1 26.1 %collective-permute-start.5 = (s32[2,8192]{1,0:T(2,128)S(1)}, s32[2,8192]{1,0:T(2,128)S(1)}, u32[]{:S(2)}, u32[]{:S(2)}) collective-permute-start(s32[2,8192]{1,0:T(2,128)S(1)} %get-tuple-element.60), channel_id=1, source_target_pairs={{96,0},{97,1},{98,2},{99,3},{100,4},{101,5},{102,6},{103,7},{104,8... | collective-permute-start | bytes 196616 | tf_op jit(solution)/shard_map/ppermute | solution.py:38
  42.2 8.1 %collective-permute-start = (f32[128,512]{1,0:T(8,128)S(1)}, f32[128,512]{1,0:T(8,128)S(1)}, u32[]{:S(2)}, u32[]{:S(2)}) collective-permute-start(f32[128,512]{1,0:T(8,128)S(1)} %fusion), channel_id=1, source_target_pairs={{4,0},{5,1},{6,2},{7,3},{8,4},{9,5},{10,6},{11,7},{12,8},{13,9},{1... | collective-permute-start | bytes 786440 | tf_op jit(solution)/shard_map/ppermute | solution.py:38
  44.1 7.1 %collective-permute-start.1 = (f32[128,512]{1,0:T(8,128)S(1)}, f32[128,512]{1,0:T(8,128)S(1)}, u32[]{:S(2)}, u32[]{:S(2)}) collective-permute-start(f32[128,512]{1,0:T(8,128)S(1)} %fusion), channel_id=1, source_target_pairs={{8,0},{9,1},{10,2},{11,3},{12,4},{13,5},{14,6},{15,7},{0,8},{1,9},... | collective-permute-start | bytes 786440 | tf_op jit(solution)/shard_map/ppermute | solution.py:38
  44.6 9.4 %collective-permute-start.2 = (f32[128,512]{1,0:T(8,128)S(1)}, f32[128,512]{1,0:T(8,128)S(1)}, u32[]{:S(2)}, u32[]{:S(2)}) collective-permute-start(f32[128,512]{1,0:T(8,128)S(1)} %fusion), channel_id=1, source_target_pairs={{12,0},{13,1},{14,2},{15,3},{0,4},{1,5},{2,6},{3,7},{4,8},{5,9},{6... | collective-permute-start | bytes 786440 | tf_op jit(solution)/shard_map/ppermute | solution.py:38
  54.1 14.6 %collective-permute-start.8 = (f32[512,512]{1,0:T(8,128)S(1)}, f32[512,512]{1,0:T(8,128)S(1)}, u32[]{:S(2)}, u32[]{:S(2)}) collective-permute-start(f32[512,512]{1,0:T(8,128)S(1)} %constant_dynamic-update-slice_fusion.refs_0_), channel_id=1, source_target_pairs={{16,0},{17,1},{18,2},{19,3},{20,4},{21,5},{22,6},{23,7},{24,8},{25... | collective-permute-start | bytes 3145736 | tf_op jit(solution)/shard_map/ppermute | solution.py:38
  55.9 13.9 %collective-permute-start.6 = (f32[512,512]{1,0:T(8,128)S(1)}, f32[512,512]{1,0:T(8,128)S(1)}, u32[]{:S(2)}, u32[]{:S(2)}) collective-permute-start(f32[512,512]{1,0:T(8,128)S(1)} %constant_dynamic-update-slice_fusion.refs_0_), channel_id=1, source_target_pairs={{1,0},{2,1},{3,2},{0,3},{5,4},{6,5},{7,6},{4,7},{9,8},{10,9},{11,1... | collective-permute-start | bytes 3145736 | tf_op jit(solution)/shard_map/ppermute | solution.py:38
  56.2 15.2 %collective-permute-start.7 = (f32[512,512]{1,0:T(8,128)S(1)}, f32[512,512]{1,0:T(8,128)S(1)}, u32[]{:S(2)}, u32[]{:S(2)}) collective-permute-start(f32[512,512]{1,0:T(8,128)S(1)} %constant_dynamic-update-slice_fusion.refs_0_), channel_id=1, source_target_pairs={{3,0},{0,1},{1,2},{2,3},{7,4},{4,5},{5,6},{6,7},{11,8},{8,9},{9,10... | collective-permute-start | bytes 3145736 | tf_op jit(solution)/shard_map/ppermute | solution.py:38
  71.4 6.0 %collective-permute-start.11 = (f32[512,512]{1,0:T(8,128)S(1)}, f32[512,512]{1,0:T(8,128)S(1)}, u32[]{:S(2)}, u32[]{:S(2)}) collective-permute-start(f32[512,512]{1,0:T(8,128)S(1)} %collective-permute-done.6.refs_0_), channel_id=1, source_target_pairs={{16,0},{17,1},{18,2},{19,3},{20,4},{21,5},{22,6},{23,7},{24,8},{25... | collective-permute-start | bytes 3145736 | tf_op jit(solution)/shard_map/ppermute | solution.py:38
  74.5 3.8 %collective-permute-start.12 = (f32[512,512]{1,0:T(8,128)S(1)}, f32[512,512]{1,0:T(8,128)S(1)}, u32[]{:S(2)}, u32[]{:S(2)}) collective-permute-start(f32[512,512]{1,0:T(8,128)S(1)} %collective-permute-done.7.refs_2_), channel_id=1, source_target_pairs={{16,0},{17,1},{18,2},{19,3},{20,4},{21,5},{22,6},{23,7},{24,8},{25... | collective-permute-start | bytes 3145736 | tf_op jit(solution)/shard_map/ppermute | solution.py:38
  74.6 12.3 %collective-permute-start.10 = (f32[256,512]{1,0:T(8,128)S(1)}, f32[256,512]{1,0:T(8,128)S(1)}, u32[]{:S(2)}, u32[]{:S(2)}) collective-permute-start(f32[256,512]{1,0:T(8,128)S(1)} %slice.15), channel_id=1, source_target_pairs={{3,0},{0,1},{1,2},{2,3},{7,4},{4,5},{5,6},{6,7},{11,8},{8,9},{9,10... | collective-permute-start | bytes 1572872 | tf_op jit(solution)/shard_map/ppermute | solution.py:38
  74.7 12.2 %collective-permute-start.9 = (f32[256,512]{1,0:T(8,128)S(1)}, f32[256,512]{1,0:T(8,128)S(1)}, u32[]{:S(2)}, u32[]{:S(2)}) collective-permute-start(f32[256,512]{1,0:T(8,128)S(1)} %slice.14), channel_id=1, source_target_pairs={{1,0},{2,1},{3,2},{0,3},{5,4},{6,5},{7,6},{4,7},{9,8},{10,9},{11,1... | collective-permute-start | bytes 1572872 | tf_op jit(solution)/shard_map/ppermute | solution.py:38
  79.6 10.1 %slice-start = ((s8[8388608]{0:T(1024)(128)(4,1)}), s8[4194304]{0:T(1024)(128)(4,1)S(1)}, s32[]{:S(2)}) async-start(s8[8388608]{0:T(1024)(128)(4,1)} %bitcast.14), calls=%async_computation.1 | async-start | bytes 8388608
  79.6 10.1 %slice-start.1 = ((s8[8388608]{0:T(1024)(128)(4,1)}), s8[4194304]{0:T(1024)(128)(4,1)S(1)}, s32[]{:S(2)}) async-start(s8[8388608]{0:T(1024)(128)(4,1)} %bitcast.14), calls=%async_computation.2 | async-start | bytes 8388608
  86.9 2.0 %collective-permute-start.13 = (f32[256,512]{1,0:T(8,128)S(1)}, f32[256,512]{1,0:T(8,128)S(1)}, u32[]{:S(2)}, u32[]{:S(2)}) collective-permute-start(f32[256,512]{1,0:T(8,128)S(1)} %collective-permute-done.9.b0), channel_id=1, source_target_pairs={{16,0},{17,1},{18,2},{19,3},{20,4},{21,5},{22,6},{23,7},{24,8},{25... | collective-permute-start | bytes 1572872 | tf_op jit(solution)/shard_map/ppermute | solution.py:38
  87.4 2.3 %collective-permute-start.14 = (f32[256,512]{1,0:T(8,128)S(1)}, f32[256,512]{1,0:T(8,128)S(1)}, u32[]{:S(2)}, u32[]{:S(2)}) collective-permute-start(f32[256,512]{1,0:T(8,128)S(1)} %collective-permute-done.10.b1), channel_id=1, source_target_pairs={{16,0},{17,1},{18,2},{19,3},{20,4},{21,5},{22,6},{23,7},{24,8},{25... | collective-permute-start | bytes 1572872 | tf_op jit(solution)/shard_map/ppermute | solution.py:38
  95.8 9.6 %collective-permute-start.15 = (f32[128,512]{1,0:T(8,128)S(1)}, f32[128,512]{1,0:T(8,128)S(1)}, u32[]{:S(2)}, u32[]{:S(2)}) collective-permute-start(f32[128,512]{1,0:T(8,128)S(1)} %get-tuple-element.48), channel_id=1, source_target_pairs={{64,0},{65,1},{66,2},{67,3},{68,4},{69,5},{70,6},{71,7},{72,8},{73... | collective-permute-start | bytes 786440 | tf_op jit(solution)/shard_map/ppermute | solution.py:38
  95.9 15.4 %collective-permute-start.16 = (f32[128,512]{1,0:T(8,128)S(1)}, f32[128,512]{1,0:T(8,128)S(1)}, u32[]{:S(2)}, u32[]{:S(2)}) collective-permute-start(f32[128,512]{1,0:T(8,128)S(1)} %get-tuple-element.49), channel_id=1, source_target_pairs={{96,0},{97,1},{98,2},{99,3},{100,4},{101,5},{102,6},{103,7},{104,8... | collective-permute-start | bytes 786440 | tf_op jit(solution)/shard_map/ppermute | solution.py:38
  103.6 7.7 %collective-permute-start.17 = (f32[128,512]{1,0:T(8,128)S(1)}, f32[128,512]{1,0:T(8,128)S(1)}, u32[]{:S(2)}, u32[]{:S(2)}) collective-permute-start(f32[128,512]{1,0:T(8,128)S(1)} %get-tuple-element.50), channel_id=1, source_target_pairs={{32,0},{33,1},{34,2},{35,3},{36,4},{37,5},{38,6},{39,7},{40,8},{41... | collective-permute-start | bytes 786440 | tf_op jit(solution)/shard_map/ppermute | solution.py:38

commit v5 on v4

--- a/solution.py
+++ b/solution.py
@@ -20,7 +20,8 @@
 F32 = jnp.float32
 SMEM = pl.BlockSpec(memory_space=pltpu.SMEM)
 VMEM = pl.BlockSpec(memory_space=pltpu.VMEM)
-LIMIT = 16
+PAIR = 2
+ORDER = (2, 1, 3, 0)
 
 
 def device_of(x, y, z, c):
@@ -95,7 +96,7 @@
             jax.ShapeDtypeStruct((RING, RING, DIRS * OCT, BLOCK), BF16),
             jax.ShapeDtypeStruct((RING,), jnp.int32),
         ],
-        compiler_params=pltpu.CompilerParams(vmem_limit_bytes=20 << 20),
+        compiler_params=pltpu.CompilerParams(vmem_limit_bytes=12 << 20),
         cost_estimate=pl.CostEstimate(
             flops=100_000_000, bytes_accessed=1 << 20, transcendentals=0
         ),
@@ -136,7 +137,7 @@
         in_specs=[VMEM] * (1 + 2 * n),
         out_specs=[VMEM] * n,
         out_shape=[jax.ShapeDtypeStruct((RING, BLOCK, 2 * WIDTH), BF16)] * n,
-        compiler_params=pltpu.CompilerParams(vmem_limit_bytes=16 << 20),
+        compiler_params=pltpu.CompilerParams(vmem_limit_bytes=6 << 20),
         cost_estimate=pl.CostEstimate(
             flops=n * 1_500_000_000, bytes_accessed=n << 20, transcendentals=0
         ),
@@ -153,46 +154,48 @@
     return both[:, :WIDTH] + both[:, WIDTH:]
 
 
-def collect_kernel(blocks, count_ref, *refs):
+def collect_kernel(blocks, first, count_ref, *refs):
     rows, out_ref = refs[:-1], refs[-1]
 
-    @pl.loop(0, RING)
+    @pl.loop(0, PAIR)
     def _(k):
         for m in range(0, DIRS, 2):
             here = slice(m * OCT, (m + 2) * OCT)
             out_ref[k, here, :] = product(
-                [count_ref[s, k, here, :] for s in blocks], [ref[k] for ref in rows]
+                [count_ref[s, first + k, here, :] for s in blocks],
+                [ref[first + k] for ref in rows],
             )
 
 
-def collect(blocks, counts, rows):
+def collect(blocks, first, counts, rows):
     n = len(blocks)
     return pl.pallas_call(
-        functools.partial(collect_kernel, blocks),
+        functools.partial(collect_kernel, blocks, first),
         in_specs=[VMEM] * (1 + n),
         out_specs=VMEM,
-        out_shape=jax.ShapeDtypeStruct((RING, DIRS * OCT, WIDTH), F32),
+        out_shape=jax.ShapeDtypeStruct((PAIR, DIRS * OCT, WIDTH), F32),
         compiler_params=pltpu.CompilerParams(vmem_limit_bytes=8 << 20),
         cost_estimate=pl.CostEstimate(
-            flops=n * 2_200_000_000, bytes_accessed=n << 20, transcendentals=0
+            flops=n * 1_100_000_000, bytes_accessed=n << 20, transcendentals=0
         ),
         name="collect",
     )(counts, *rows)
 
 
 def finish_kernel(
-    readers, flag_ref, ids_ref, b0, b1, b2, b3, x_ref, rows0, rows1, rows3, count_ref, k_ref,
+    first, flag_ref, ids_ref, b0, b1, b2, b3, x_ref, rows0, rows1, rows3, count_ref, k_ref,
     row_ref, col_ref, out0, out1, rows2, xh, xl,
 ):
     def store(owner, k, values):
         rows2[k, owner * PER : (owner + 1) * PER, :] = values
 
     pick(ids_ref, 2 * 2 * RING, (b0, b1, b2, b3), store)
-    for i, k in enumerate(readers):
+    for i in range(PAIR):
+        k = first + i
         there = slice(i * OCT, (i + 1) * OCT)
         for m in range(0, DIRS, 2):
             here = slice(m * OCT, (m + 2) * OCT)
-            total = x_ref[k, here, :] + product([count_ref[2, k, here, :]], [rows2[k]])
+            total = x_ref[i, here, :] + product([count_ref[2, k, here, :]], [rows2[k]])
             high, low = parts(total)
             for j in range(2):
                 xh[m + j, there, :] = high[j * OCT : (j + 1) * OCT]
@@ -223,19 +226,18 @@
         out[...] = total[i * OCT : (i + 1) * OCT]
 
 
-def finish(readers, flags, ids, arrays, x, rows, counts, kernels, codes):
-    n = len(readers)
+def finish(first, flags, ids, arrays, x, rows, counts, kernels, codes):
     return pl.pallas_call(
-        functools.partial(finish_kernel, readers),
+        functools.partial(finish_kernel, first),
         in_specs=[SMEM] + [VMEM] * 13,
         out_specs=[VMEM] * 2,
         out_shape=[jax.ShapeDtypeStruct((OCT, WIDTH), F32)] * 2,
         scratch_shapes=[
             pltpu.VMEM((RING, BLOCK, 2 * WIDTH), BF16),
-            pltpu.VMEM((DIRS, n * OCT, WIDTH), BF16),
-            pltpu.VMEM((DIRS, n * OCT, WIDTH), BF16),
+            pltpu.VMEM((DIRS, PAIR * OCT, WIDTH), BF16),
+            pltpu.VMEM((DIRS, PAIR * OCT, WIDTH), BF16),
         ],
-        compiler_params=pltpu.CompilerParams(vmem_limit_bytes=LIMIT << 20),
+        compiler_params=pltpu.CompilerParams(vmem_limit_bytes=12 << 20),
         cost_estimate=pl.CostEstimate(
             flops=6_000_000_000, bytes_accessed=2 << 20, transcendentals=0
         ),
@@ -264,15 +266,15 @@
             (((z + k) % RING * CORES + c) * (RING * RING) + gy, z * (PLANE * PER)),
             (1, PLANE * PER),
         )
-        for k in range(RING)
+        for k in ORDER
     ]
     reads = jnp.concatenate(reads, axis=0).reshape(RING, PLANE, PER)
     ids = jnp.take(reads.transpose(1, 0, 2).reshape(PLANE, RING * PER), order, axis=0)
 
     lists = jnp.concatenate([sources, targets], axis=0)
-    ring_lists = [lists] + [along_z(lists, k) for k in range(1, RING)]
-
-    stacked = jnp.stack(ring_lists)
+    ring_lists = {0: lists, **{k: along_z(lists, k) for k in range(1, RING)}}
+
+    stacked = jnp.stack([ring_lists[k] for k in ORDER])
     slot, target = stacked[:, 0], stacked[:, 1]
     owner = slot // PER
     core = (owner // (RING * RING)) % CORES
@@ -298,19 +300,21 @@
     line = jnp.concatenate(line, axis=0)
     near1, near3 = along_s(line, 1), along_s(line, 3)
     counts, flags = count(*codes)
+    near1, near3, counts, flags = lax.optimization_barrier((near1, near3, counts, flags))
+    low, high = along_s(near1[: 2 * OCT], 1), along_s(near3[2 * OCT :], 3)
     (rows0,) = gather((0,), ids, [line, across(line)])
-    near1, near3, counts, flags, rows0 = lax.optimization_barrier(
-        (near1, near3, counts, flags, rows0)
-    )
-    low, high = along_s(near1[: 2 * OCT], 1), along_s(near3[2 * OCT :], 3)
     rows1, rows3 = gather((1, 3), ids, [near1, across(near1), near3, across(near3)])
     rows = (rows0, rows1, rows3)
-    x = collect((0, 1, 3), counts, rows)
-    low, high, x = lax.optimization_barrier((low, high, x))
-    last = (flags, ids, [low, high, across(low), across(high)], x, rows, counts, kernels, codes)
-    out2, out1 = finish((2, 1), *last)
-    out3, out0 = finish((3, 0), *last)
-    return out0 + along_z(out2, -2) + along_z(out1, -1) + along_z(out3, -3)
+    x = [collect((0, 1, 3), 0, counts, rows), None]
+    low, high, x[0], rows = lax.optimization_barrier((low, high, x[0], rows))
+    far = [low, high, across(low), across(high)]
+    x[1] = collect((0, 1, 3), PAIR, counts, rows)
+    last = (rows, counts, kernels, codes)
+    out2, out1 = finish(0, flags, ids, far, x[0], *last)
+    ring2, ring1 = along_z(out2, -2), along_z(out1, -1)
+    out3, out0 = finish(PAIR, flags, ids, far, x[1], *last)
+    ring3 = along_z(out3, -3)
+    return out0 + ring3 + ring2 + ring1
 
 
 def solution(mesh):

time: 112 us -> 108 us (0.964)
  waiting for transfers between devices: 41.3 us -> 33.9 us
  starting transfers between devices: 31.8 us -> 35.2 us
    ppermute x18, waiting for transfers between devices: 41.3 us -> 31.7 us  [fetch(): return lax.ppermute(value, AXES, pairs)]
    ppermute x18, starting transfers between devices: 20.3 us -> 23.7 us  [fetch(): return lax.ppermute(value, AXES, pairs)]
    all_to_all x1, waiting for transfers between devices: 0.09 us -> 2.15 us  [body(): lax.all_to_all(partials, AXES, split_axis=0, concat_axis=0, tiled=True)]
    pallas_call x3 -> x4, Pallas kernels: 19.8 us -> 19.6 us  [the longest x2 12.5 us: finish(): pl.pallas_call(functools.partial(finish_kernel, first), in_specs=[SMEM] +...]
  transfers between devices with their start and end apart: 19 -> 19, of which waited for: 13 -> 9; matrix products, arithmetic and copies ran while one was open for 3% -> 3% of each run, Pallas kernels for 24% -> 25%
where the time goes in v5:
time: 108 us
  starting transfers between devices  35.2 us (33%)
  waiting for transfers between devices  33.9 us (31%)
  Pallas kernels  33 us (31%)
  local copies, waits for them, and re-layouts  2.92 us (3%)
  other arithmetic  1.73 us (2%)
    ppermute x18, waiting for transfers between devices, fetch(): return lax.ppermute(value, AXES, pairs)  31.7 us
    ppermute x18, starting transfers between devices, fetch(): return lax.ppermute(value, AXES, pairs)  23.7 us
    pallas_call x2, Pallas kernels, finish(): pl.pallas_call(functools.partial(finish_kernel, first), in_specs=[SMEM] +...  12.5 us
    all_to_all x1, starting transfers between devices, body(): lax.all_to_all(partials, AXES, split_axis=0, concat_axis=0, tiled=True)  11.5 us
    pallas_call x1, Pallas kernels, count(): pl.pallas_call(count_kernel, grid=(RING,), in_specs=[codes, codes], out_s...  11.4 us
    pallas_call x2, Pallas kernels, collect(): pl.pallas_call(functools.partial(collect_kernel, blocks, first), in_specs...  7.15 us
  transfers between devices with their start and end apart: 19, of which 9 were waited for; matrix products, arithmetic and copies ran while one was open for 3% of the time, Pallas kernels for 25%

profile of v5, /device:TPU:1, one launch (start us, length us, event | category | flops | bytes accessed | tf_op | source)
XLA Modules:
  0.0 107.9 jit_solution(7884334941345765192)
XLA Ops:
  0.0 11.5 %all-to-all-start = ((f32[128,8,512]{2,1,0:T(8,128)}), f32[128,8,512]{2,1,0:T(8,128)S(1)}, u32[]{:S(2)}, u32[]{:S(2)}) async-start(f32[128,8,512]{2,1,0:T(8,128)} %bitcast.16), calls=%async_computation | async-start | bytes 4194304 | tf_op jit(solution)/shard_map/all_to_all | solution.py:255
  11.6 1.6 %collective-permute-start.5 = (s32[2,8192]{1,0:T(2,128)S(1)}, s32[2,8192]{1,0:T(2,128)S(1)}, u32[]{:S(2)}, u32[]{:S(2)}) collective-permute-start(s32[2,8192]{1,0:T(2,128)S(1)} %get-tuple-element.63), channel_id=1, source_target_pairs={{96,0},{97,1},{98,2},{99,3},{100,4},{101,5},{102,6},{103,7},{104,8... | collective-permute-start | bytes 196616 | tf_op jit(solution)/shard_map/ppermute | solution.py:39
  13.2 1.8 %collective-permute-start.4 = (s32[2,8192]{1,0:T(2,128)S(1)}, s32[2,8192]{1,0:T(2,128)S(1)}, u32[]{:S(2)}, u32[]{:S(2)}) collective-permute-start(s32[2,8192]{1,0:T(2,128)S(1)} %get-tuple-element.63), channel_id=1, source_target_pairs={{32,0},{33,1},{34,2},{35,3},{36,4},{37,5},{38,6},{39,7},{40,8},{41... | collective-permute-start | bytes 196616 | tf_op jit(solution)/shard_map/ppermute | solution.py:39
  15.0 1.4 %collective-permute-start.3 = (s32[2,8192]{1,0:T(2,128)S(1)}, s32[2,8192]{1,0:T(2,128)S(1)}, u32[]{:S(2)}, u32[]{:S(2)}) collective-permute-start(s32[2,8192]{1,0:T(2,128)S(1)} %get-tuple-element.63), channel_id=1, source_target_pairs={{64,0},{65,1},{66,2},{67,3},{68,4},{69,5},{70,6},{71,7},{72,8},{73... | collective-permute-start | bytes 196616 | tf_op jit(solution)/shard_map/ppermute | solution.py:39
  16.4 0.9 fusion.50
  18.5 16.2 %collective-permute-done.5 = s32[2,8192]{1,0:T(2,128)S(1)} collective-permute-done((s32[2,8192]{1,0:T(2,128)S(1)}, s32[2,8192]{1,0:T(2,128)S(1)}, u32[]{:S(2)}, u32[]{:S(2)}) %collective-permute-start.5) | collective-permute-done | bytes 65568 | tf_op jit(solution)/shard_map/ppermute | solution.py:39
  34.7 4.4 %collective-permute-done.3 = s32[2,8192]{1,0:T(2,128)S(1)} collective-permute-done((s32[2,8192]{1,0:T(2,128)S(1)}, s32[2,8192]{1,0:T(2,128)S(1)}, u32[]{:S(2)}, u32[]{:S(2)}) %collective-permute-start.3) | collective-permute-done | bytes 65568 | tf_op jit(solution)/shard_map/ppermute | solution.py:39
  39.1 2.2 %all-to-all-done = f32[128,8,512]{2,1,0:T(8,128)S(1)} async-done(((f32[128,8,512]{2,1,0:T(8,128)}), f32[128,8,512]{2,1,0:T(8,128)S(1)}, u32[]{:S(2)}, u32[]{:S(2)}) %all-to-all-start) | async-done | bytes 2097184 | tf_op jit(solution)/shard_map/all_to_all | solution.py:255
  41.3 0.9 fusion
  42.8 2.5 %collective-permute-start.1 = (f32[128,512]{1,0:T(8,128)S(1)}, f32[128,512]{1,0:T(8,128)S(1)}, u32[]{:S(2)}, u32[]{:S(2)}) collective-permute-start(f32[128,512]{1,0:T(8,128)S(1)} %fusion), channel_id=1, source_target_pairs={{8,0},{9,1},{10,2},{11,3},{12,4},{13,5},{14,6},{15,7},{0,8},{1,9},... | collective-permute-start | bytes 786440 | tf_op jit(solution)/shard_map/ppermute | solution.py:39
  45.3 0.9 collective-permute-start
  46.2 0.7 slice_reduce_fusion.1
  47.8 1.2 %collective-permute-done.2 = f32[128,512]{1,0:T(8,128)S(1)} collective-permute-done((f32[128,512]{1,0:T(8,128)S(1)}, f32[128,512]{1,0:T(8,128)S(1)}, u32[]{:S(2)}, u32[]{:S(2)}) %collective-permute-start.2) | collective-permute-done | bytes 262176 | tf_op jit(solution)/shard_map/ppermute | solution.py:39
  49.0 3.2 %collective-permute-done.1 = f32[128,512]{1,0:T(8,128)S(1)} collective-permute-done((f32[128,512]{1,0:T(8,128)S(1)}, f32[128,512]{1,0:T(8,128)S(1)}, u32[]{:S(2)}, u32[]{:S(2)}) %collective-permute-start.1) | collective-permute-done | bytes 262176 | tf_op jit(solution)/shard_map/ppermute | solution.py:39
  53.1 2.2 %collective-permute-start.6 = (f32[512,512]{1,0:T(8,128)S(1)}, f32[512,512]{1,0:T(8,128)S(1)}, u32[]{:S(2)}, u32[]{:S(2)}) collective-permute-start(f32[512,512]{1,0:T(8,128)S(1)} %constant_dynamic-update-slice_fusion.refs_0_), channel_id=1, source_target_pairs={{1,0},{2,1},{3,2},{0,3},{5,4},{6,5},{7,6},{4,7},{9,8},{10,9},{11,1... | collective-permute-start | bytes 3145736 | tf_op jit(solution)/shard_map/ppermute | solution.py:39
  55.3 2.7 %collective-permute-start.10 = (f32[512,512]{1,0:T(8,128)S(1)}, f32[512,512]{1,0:T(8,128)S(1)}, u32[]{:S(2)}, u32[]{:S(2)}) collective-permute-start(f32[512,512]{1,0:T(8,128)S(1)} %constant_dynamic-update-slice_fusion.refs_0_), channel_id=1, source_target_pairs={{16,0},{17,1},{18,2},{19,3},{20,4},{21,5},{22,6},{23,7},{24,8},{25... | collective-permute-start | bytes 3145736 | tf_op jit(solution)/shard_map/ppermute | solution.py:39
  58.0 11.4 %count.1 = (bf16[4,4,1024,256]{3,2,1,0:T(8,128)(2,1)S(1)}, s32[4]{0:T(128)S(1)}) custom-call(s32[32,1024]{1,0:T(8,128)S(1)} %get-tuple-element.34.row_ref, s32[32,1024]{1,0:T(8,128)S(1)} %get-tuple-element.35.col_ref), custom_call_target="tpu_custom_call" | custom-call | flops 100000000 | bytes 1048576 | tf_op jit(solution)/shard_map/count/pallas_call | solution.py:90
  69.3 1.4 %collective-permute-start.11 = (f32[512,512]{1,0:T(8,128)S(1)}, f32[512,512]{1,0:T(8,128)S(1)}, u32[]{:S(2)}, u32[]{:S(2)}) collective-permute-start(f32[512,512]{1,0:T(8,128)S(1)} %collective-permute-done.6.refs_0_), channel_id=1, source_target_pairs={{16,0},{17,1},{18,2},{19,3},{20,4},{21,5},{22,6},{23,7},{24,8},{25... | collective-permute-start | bytes 3145736 | tf_op jit(solution)/shard_map/ppermute | solution.py:39
  70.8 1.2 %collective-permute-start.9 = (f32[256,512]{1,0:T(8,128)S(1)}, f32[256,512]{1,0:T(8,128)S(1)}, u32[]{:S(2)}, u32[]{:S(2)}) collective-permute-start(f32[256,512]{1,0:T(8,128)S(1)} %slice.15), channel_id=1, source_target_pairs={{3,0},{0,1},{1,2},{2,3},{7,4},{4,5},{5,6},{6,7},{11,8},{8,9},{9,10... | collective-permute-start | bytes 1572872 | tf_op jit(solution)/shard_map/ppermute | solution.py:39
  72.0 1.6 %collective-permute-start.8 = (f32[256,512]{1,0:T(8,128)S(1)}, f32[256,512]{1,0:T(8,128)S(1)}, u32[]{:S(2)}, u32[]{:S(2)}) collective-permute-start(f32[256,512]{1,0:T(8,128)S(1)} %slice.14), channel_id=1, source_target_pairs={{1,0},{2,1},{3,2},{0,3},{5,4},{6,5},{7,6},{4,7},{9,8},{10,9},{11,1... | collective-permute-start | bytes 1572872 | tf_op jit(solution)/shard_map/ppermute | solution.py:39
  73.6 0.7 gather.9.refs_0_.rows0
  74.5 1.3 %gather.10 = (bf16[4,256,1024]{2,1,0:T(8,128)(2,1)S(1)}, bf16[4,256,1024]{2,1,0:T(8,128)(2,1)S(1)}) custom-call(s32[32,128]{1,0:T(8,128)S(1)} %broadcast_select_fusion.ids_ref, f32[512,512]{1,0:T(8,128)S(1)} %collective-permute-done.6.refs_0_, f32[512,512]{1,0:T(8,128)S(1)} %collective-permute-done.11.refs_1_, ...), custom_call_target="tpu_custom_call" | custom-call | flops 3000000000 | bytes 2097152 | tf_op jit(solution)/shard_map/gather/pallas_call | solution.py:135
  75.9 3.6 %collect.2.x_ref = f32[2,1024,512]{2,1,0:T(8,128)S(1)} custom-call(bf16[4,4,1024,256]{3,2,1,0:T(8,128)(2,1)S(1)} %get-tuple-element.42.count_ref, bf16[4,256,1024]{2,1,0:T(8,128)(2,1)S(1)} %gather.9.refs_0_.rows0, bf16[4,256,1024]{2,1,0:T(8,128)(2,1)S(1)} %get-tuple-element.48.refs_1_.rows1, bf16[4,256,1024]{2,1,0:T(8,128)(2,1)S(1)} %get-tuple-element.49.refs_2_.rows3), custom_call_target="tpu_custom_call" | custom-call | flops 3300000000 | bytes 3145728 | tf_op jit(solution)/shard_map/collect/pallas_call | solution.py:172
  79.5 1.0 collective-permute-done.9.b1
  80.4 1.4 %collective-permute-start.13 = (f32[256,512]{1,0:T(8,128)S(1)}, f32[256,512]{1,0:T(8,128)S(1)}, u32[]{:S(2)}, u32[]{:S(2)}) collective-permute-start(f32[256,512]{1,0:T(8,128)S(1)} %collective-permute-done.8.b0), channel_id=1, source_target_pairs={{16,0},{17,1},{18,2},{19,3},{20,4},{21,5},{22,6},{23,7},{24,8},{25... | collective-permute-start | bytes 1572872 | tf_op jit(solution)/shard_map/ppermute | solution.py:39
  81.8 3.6 %collect.3.x_ref = f32[2,1024,512]{2,1,0:T(8,128)S(1)} custom-call(bf16[4,4,1024,256]{3,2,1,0:T(8,128)(2,1)S(1)} %get-tuple-element.42.count_ref, bf16[4,256,1024]{2,1,0:T(8,128)(2,1)S(1)} %gather.9.refs_0_.rows0, bf16[4,256,1024]{2,1,0:T(8,128)(2,1)S(1)} %get-tuple-element.48.refs_1_.rows1, bf16[4,256,1024]{2,1,0:T(8,128)(2,1)S(1)} %get-tuple-element.49.refs_2_.rows3), custom_call_target="tpu_custom_call" | custom-call | flops 3300000000 | bytes 3145728 | tf_op jit(solution)/shard_map/collect/pallas_call | solution.py:172
  85.4 6.2 %finish.3 = (f32[128,512]{1,0:T(8,128)S(1)}, f32[128,512]{1,0:T(8,128)S(1)}) custom-call(s32[4]{0:T(128)S(1)} %get-tuple-element.38.flag_ref, s32[32,128]{1,0:T(8,128)S(1)} %broadcast_select_fusion.ids_ref, f32[256,512]{1,0:T(8,128)S(1)} %collective-permute-done.8.b0, f32[256,512]{1,0:T(8,128)S(1)} %collective-permute-done.9.b1, ...), custom_call_target="tpu_custom_call" | custom-call | flops 6000000000 | bytes 2097152 | tf_op jit(solution)/shard_map/finish/pallas_call | solution.py:230
  91.7 1.1 %collective-permute-start.16 = (f32[128,512]{1,0:T(8,128)S(1)}, f32[128,512]{1,0:T(8,128)S(1)}, u32[]{:S(2)}, u32[]{:S(2)}) collective-permute-start(f32[128,512]{1,0:T(8,128)S(1)} %get-tuple-element.53), channel_id=1, source_target_pairs={{64,0},{65,1},{66,2},{67,3},{68,4},{69,5},{70,6},{71,7},{72,8},{73... | collective-permute-start | bytes 786440 | tf_op jit(solution)/shard_map/ppermute | solution.py:39
  93.3 6.2 %finish.2 = (f32[128,512]{1,0:T(8,128)S(1)}, f32[128,512]{1,0:T(8,128)S(1)}) custom-call(s32[4]{0:T(128)S(1)} %get-tuple-element.38.flag_ref, s32[32,128]{1,0:T(8,128)S(1)} %broadcast_select_fusion.ids_ref, f32[256,512]{1,0:T(8,128)S(1)} %collective-permute-done.8.b0, f32[256,512]{1,0:T(8,128)S(1)} %collective-permute-done.9.b1, ...), custom_call_target="tpu_custom_call" | custom-call | flops 6000000000 | bytes 2097152 | tf_op jit(solution)/shard_map/finish/pallas_call | solution.py:230
  99.6 2.2 %collective-permute-start.15 = (f32[128,512]{1,0:T(8,128)S(1)}, f32[128,512]{1,0:T(8,128)S(1)}, u32[]{:S(2)}, u32[]{:S(2)}) collective-permute-start(f32[128,512]{1,0:T(8,128)S(1)} %get-tuple-element.51), channel_id=1, source_target_pairs={{32,0},{33,1},{34,2},{35,3},{36,4},{37,5},{38,6},{39,7},{40,8},{41... | collective-permute-start | bytes 786440 | tf_op jit(solution)/shard_map/ppermute | solution.py:39
  101.8 5.3 %collective-permute-done.17 = f32[128,512]{1,0:T(8,128)S(1)} collective-permute-done((f32[128,512]{1,0:T(8,128)S(1)}, f32[128,512]{1,0:T(8,128)S(1)}, u32[]{:S(2)}, u32[]{:S(2)}) %collective-permute-start.17) | collective-permute-done | bytes 262176 | tf_op jit(solution)/shard_map/ppermute | solution.py:39
  107.1 0.8 add_add_fusion
  (50 shorter events, 4.4 us)
Async XLA Ops:
  0.0 18.4 %copy-start = (s32[128,1024]{1,0:T(8,128)S(1)}, s32[128,1024]{1,0:T(8,128)}, u32[]{:S(2)}) copy-start(s32[128,1024]{1,0:T(8,128)} %param.7) | copy-start | bytes 1572868
  0.0 11.5 %copy-start.1 = (s32[1,8192]{1,0:T(1,128)S(1)}, s32[1,8192]{1,0:T(1,128)}, u32[]{:S(2)}) copy-start(s32[1,8192]{1,0:T(1,128)} %param.10) | copy-start | bytes 98308
  0.0 11.5 %copy-start.2 = (s32[1,8192]{1,0:T(1,128)S(1)}, s32[1,8192]{1,0:T(1,128)}, u32[]{:S(2)}) copy-start(s32[1,8192]{1,0:T(1,128)} %param.9) | copy-start | bytes 98308
  0.0 41.3 %all-to-all-start = ((f32[128,8,512]{2,1,0:T(8,128)}), f32[128,8,512]{2,1,0:T(8,128)S(1)}, u32[]{:S(2)}, u32[]{:S(2)}) async-start(f32[128,8,512]{2,1,0:T(8,128)} %bitcast.16), calls=%async_computation | async-start | bytes 4194304 | tf_op jit(solution)/shard_map/all_to_all | solution.py:255
  11.6 23.1 %collective-permute-start.5 = (s32[2,8192]{1,0:T(2,128)S(1)}, s32[2,8192]{1,0:T(2,128)S(1)}, u32[]{:S(2)}, u32[]{:S(2)}) collective-permute-start(s32[2,8192]{1,0:T(2,128)S(1)} %get-tuple-element.63), channel_id=1, source_target_pairs={{96,0},{97,1},{98,2},{99,3},{100,4},{101,5},{102,6},{103,7},{104,8... | collective-permute-start | bytes 196616 | tf_op jit(solution)/shard_map/ppermute | solution.py:39
  13.2 21.5 %collective-permute-start.4 = (s32[2,8192]{1,0:T(2,128)S(1)}, s32[2,8192]{1,0:T(2,128)S(1)}, u32[]{:S(2)}, u32[]{:S(2)}) collective-permute-start(s32[2,8192]{1,0:T(2,128)S(1)} %get-tuple-element.63), channel_id=1, source_target_pairs={{32,0},{33,1},{34,2},{35,3},{36,4},{37,5},{38,6},{39,7},{40,8},{41... | collective-permute-start | bytes 196616 | tf_op jit(solution)/shard_map/ppermute | solution.py:39
  15.0 24.1 %collective-permute-start.3 = (s32[2,8192]{1,0:T(2,128)S(1)}, s32[2,8192]{1,0:T(2,128)S(1)}, u32[]{:S(2)}, u32[]{:S(2)}) collective-permute-start(s32[2,8192]{1,0:T(2,128)S(1)} %get-tuple-element.63), channel_id=1, source_target_pairs={{64,0},{65,1},{66,2},{67,3},{68,4},{69,5},{70,6},{71,7},{72,8},{73... | collective-permute-start | bytes 196616 | tf_op jit(solution)/shard_map/ppermute | solution.py:39
  42.2 6.8 %collective-permute-start.2 = (f32[128,512]{1,0:T(8,128)S(1)}, f32[128,512]{1,0:T(8,128)S(1)}, u32[]{:S(2)}, u32[]{:S(2)}) collective-permute-start(f32[128,512]{1,0:T(8,128)S(1)} %fusion), channel_id=1, source_target_pairs={{12,0},{13,1},{14,2},{15,3},{0,4},{1,5},{2,6},{3,7},{4,8},{5,9},{6... | collective-permute-start | bytes 786440 | tf_op jit(solution)/shard_map/ppermute | solution.py:39
  42.8 9.4 %collective-permute-start.1 = (f32[128,512]{1,0:T(8,128)S(1)}, f32[128,512]{1,0:T(8,128)S(1)}, u32[]{:S(2)}, u32[]{:S(2)}) collective-permute-start(f32[128,512]{1,0:T(8,128)S(1)} %fusion), channel_id=1, source_target_pairs={{8,0},{9,1},{10,2},{11,3},{12,4},{13,5},{14,6},{15,7},{0,8},{1,9},... | collective-permute-start | bytes 786440 | tf_op jit(solution)/shard_map/ppermute | solution.py:39
  45.3 7.1 %collective-permute-start = (f32[128,512]{1,0:T(8,128)S(1)}, f32[128,512]{1,0:T(8,128)S(1)}, u32[]{:S(2)}, u32[]{:S(2)}) collective-permute-start(f32[128,512]{1,0:T(8,128)S(1)} %fusion), channel_id=1, source_target_pairs={{4,0},{5,1},{6,2},{7,3},{8,4},{9,5},{10,6},{11,7},{12,8},{13,9},{1... | collective-permute-start | bytes 786440 | tf_op jit(solution)/shard_map/ppermute | solution.py:39
  52.5 16.8 %collective-permute-start.7 = (f32[512,512]{1,0:T(8,128)S(1)}, f32[512,512]{1,0:T(8,128)S(1)}, u32[]{:S(2)}, u32[]{:S(2)}) collective-permute-start(f32[512,512]{1,0:T(8,128)S(1)} %constant_dynamic-update-slice_fusion.refs_0_), channel_id=1, source_target_pairs={{3,0},{0,1},{1,2},{2,3},{7,4},{4,5},{5,6},{6,7},{11,8},{8,9},{9,10... | collective-permute-start | bytes 3145736 | tf_op jit(solution)/shard_map/ppermute | solution.py:39
  53.1 16.3 %collective-permute-start.6 = (f32[512,512]{1,0:T(8,128)S(1)}, f32[512,512]{1,0:T(8,128)S(1)}, u32[]{:S(2)}, u32[]{:S(2)}) collective-permute-start(f32[512,512]{1,0:T(8,128)S(1)} %constant_dynamic-update-slice_fusion.refs_0_), channel_id=1, source_target_pairs={{1,0},{2,1},{3,2},{0,3},{5,4},{6,5},{7,6},{4,7},{9,8},{10,9},{11,1... | collective-permute-start | bytes 3145736 | tf_op jit(solution)/shard_map/ppermute | solution.py:39
  55.3 18.3 %collective-permute-start.10 = (f32[512,512]{1,0:T(8,128)S(1)}, f32[512,512]{1,0:T(8,128)S(1)}, u32[]{:S(2)}, u32[]{:S(2)}) collective-permute-start(f32[512,512]{1,0:T(8,128)S(1)} %constant_dynamic-update-slice_fusion.refs_0_), channel_id=1, source_target_pairs={{16,0},{17,1},{18,2},{19,3},{20,4},{21,5},{22,6},{23,7},{24,8},{25... | collective-permute-start | bytes 3145736 | tf_op jit(solution)/shard_map/ppermute | solution.py:39
  69.3 5.0 %collective-permute-start.11 = (f32[512,512]{1,0:T(8,128)S(1)}, f32[512,512]{1,0:T(8,128)S(1)}, u32[]{:S(2)}, u32[]{:S(2)}) collective-permute-start(f32[512,512]{1,0:T(8,128)S(1)} %collective-permute-done.6.refs_0_), channel_id=1, source_target_pairs={{16,0},{17,1},{18,2},{19,3},{20,4},{21,5},{22,6},{23,7},{24,8},{25... | collective-permute-start | bytes 3145736 | tf_op jit(solution)/shard_map/ppermute | solution.py:39
  70.7 3.8 %collective-permute-start.12 = (f32[512,512]{1,0:T(8,128)S(1)}, f32[512,512]{1,0:T(8,128)S(1)}, u32[]{:S(2)}, u32[]{:S(2)}) collective-permute-start(f32[512,512]{1,0:T(8,128)S(1)} %collective-permute-done.7.refs_2_), channel_id=1, source_target_pairs={{16,0},{17,1},{18,2},{19,3},{20,4},{21,5},{22,6},{23,7},{24,8},{25... | collective-permute-start | bytes 3145736 | tf_op jit(solution)/shard_map/ppermute | solution.py:39
  70.8 9.6 %collective-permute-start.9 = (f32[256,512]{1,0:T(8,128)S(1)}, f32[256,512]{1,0:T(8,128)S(1)}, u32[]{:S(2)}, u32[]{:S(2)}) collective-permute-start(f32[256,512]{1,0:T(8,128)S(1)} %slice.15), channel_id=1, source_target_pairs={{3,0},{0,1},{1,2},{2,3},{7,4},{4,5},{5,6},{6,7},{11,8},{8,9},{9,10... | collective-permute-start | bytes 1572872 | tf_op jit(solution)/shard_map/ppermute | solution.py:39
  72.0 8.4 %collective-permute-start.8 = (f32[256,512]{1,0:T(8,128)S(1)}, f32[256,512]{1,0:T(8,128)S(1)}, u32[]{:S(2)}, u32[]{:S(2)}) collective-permute-start(f32[256,512]{1,0:T(8,128)S(1)} %slice.14), channel_id=1, source_target_pairs={{1,0},{2,1},{3,2},{0,3},{5,4},{6,5},{7,6},{4,7},{9,8},{10,9},{11,1... | collective-permute-start | bytes 1572872 | tf_op jit(solution)/shard_map/ppermute | solution.py:39
  75.8 9.6 %slice-start = ((s8[8388608]{0:T(1024)(128)(4,1)}), s8[4194304]{0:T(1024)(128)(4,1)S(1)}, s32[]{:S(2)}) async-start(s8[8388608]{0:T(1024)(128)(4,1)} %bitcast.14), calls=%async_computation.1 | async-start | bytes 8388608
  79.4 6.0 %slice-start.1 = ((s8[8388608]{0:T(1024)(128)(4,1)}), s8[4194304]{0:T(1024)(128)(4,1)S(1)}, s32[]{:S(2)}) async-start(s8[8388608]{0:T(1024)(128)(4,1)} %bitcast.14), calls=%async_computation.2 | async-start | bytes 8388608
  80.4 5.0 %collective-permute-start.13 = (f32[256,512]{1,0:T(8,128)S(1)}, f32[256,512]{1,0:T(8,128)S(1)}, u32[]{:S(2)}, u32[]{:S(2)}) collective-permute-start(f32[256,512]{1,0:T(8,128)S(1)} %collective-permute-done.8.b0), channel_id=1, source_target_pairs={{16,0},{17,1},{18,2},{19,3},{20,4},{21,5},{22,6},{23,7},{24,8},{25... | collective-permute-start | bytes 1572872 | tf_op jit(solution)/shard_map/ppermute | solution.py:39
  81.8 3.6 %collective-permute-start.14 = (f32[256,512]{1,0:T(8,128)S(1)}, f32[256,512]{1,0:T(8,128)S(1)}, u32[]{:S(2)}, u32[]{:S(2)}) collective-permute-start(f32[256,512]{1,0:T(8,128)S(1)} %collective-permute-done.9.b1), channel_id=1, source_target_pairs={{16,0},{17,1},{18,2},{19,3},{20,4},{21,5},{22,6},{23,7},{24,8},{25... | collective-permute-start | bytes 1572872 | tf_op jit(solution)/shard_map/ppermute | solution.py:39
  91.7 10.1 %collective-permute-start.16 = (f32[128,512]{1,0:T(8,128)S(1)}, f32[128,512]{1,0:T(8,128)S(1)}, u32[]{:S(2)}, u32[]{:S(2)}) collective-permute-start(f32[128,512]{1,0:T(8,128)S(1)} %get-tuple-element.53), channel_id=1, source_target_pairs={{64,0},{65,1},{66,2},{67,3},{68,4},{69,5},{70,6},{71,7},{72,8},{73... | collective-permute-start | bytes 786440 | tf_op jit(solution)/shard_map/ppermute | solution.py:39
  92.8 14.3 %collective-permute-start.17 = (f32[128,512]{1,0:T(8,128)S(1)}, f32[128,512]{1,0:T(8,128)S(1)}, u32[]{:S(2)}, u32[]{:S(2)}) collective-permute-start(f32[128,512]{1,0:T(8,128)S(1)} %get-tuple-element.54), channel_id=1, source_target_pairs={{96,0},{97,1},{98,2},{99,3},{100,4},{101,5},{102,6},{103,7},{104,8... | collective-permute-start | bytes 786440 | tf_op jit(solution)/shard_map/ppermute | solution.py:39
  99.6 7.5 %collective-permute-start.15 = (f32[128,512]{1,0:T(8,128)S(1)}, f32[128,512]{1,0:T(8,128)S(1)}, u32[]{:S(2)}, u32[]{:S(2)}) collective-permute-start(f32[128,512]{1,0:T(8,128)S(1)} %get-tuple-element.51), channel_id=1, source_target_pairs={{32,0},{33,1},{34,2},{35,3},{36,4},{37,5},{38,6},{39,7},{40,8},{41... | collective-permute-start | bytes 786440 | tf_op jit(solution)/shard_map/ppermute | solution.py:39

commit v6 on v5

--- a/solution.py
+++ b/solution.py
@@ -121,20 +121,21 @@
 
 def gather_kernel(blocks, ids_ref, *refs):
     n = len(blocks)
+    per = len(refs) // n - 1
     for i, s in enumerate(blocks):
-        rows = refs[2 * n + i]
+        rows = refs[per * n + i]
 
         def store(owner, k, values, rows=rows):
             rows[k, owner * PER : (owner + 1) * PER, :] = values
 
-        pick(ids_ref, s * 2 * RING, refs[2 * i : 2 * i + 2], store)
+        pick(ids_ref, s * 2 * RING, refs[per * i : per * (i + 1)], store)
 
 
 def gather(blocks, ids, arrays):
     n = len(blocks)
     return pl.pallas_call(
         functools.partial(gather_kernel, blocks),
-        in_specs=[VMEM] * (1 + 2 * n),
+        in_specs=[VMEM] * (1 + len(arrays)),
         out_specs=[VMEM] * n,
         out_shape=[jax.ShapeDtypeStruct((RING, BLOCK, 2 * WIDTH), BF16)] * n,
         compiler_params=pltpu.CompilerParams(vmem_limit_bytes=6 << 20),
@@ -183,19 +184,16 @@
 
 
 def finish_kernel(
-    first, flag_ref, ids_ref, b0, b1, b2, b3, x_ref, rows0, rows1, rows3, count_ref, k_ref,
-    row_ref, col_ref, out0, out1, rows2, xh, xl,
+    first, skip, flag_ref, x_ref, rows0, rows1, rows2, rows3, count_ref, k_ref, row_ref, col_ref,
+    *refs,
 ):
-    def store(owner, k, values):
-        rows2[k, owner * PER : (owner + 1) * PER, :] = values
-
-    pick(ids_ref, 2 * 2 * RING, (b0, b1, b2, b3), store)
-    for i in range(PAIR):
+    outs, xh, xl = refs[:-2], refs[-2], refs[-1]
+    for i in range(len(outs)):
         k = first + i
         there = slice(i * OCT, (i + 1) * OCT)
         for m in range(0, DIRS, 2):
             here = slice(m * OCT, (m + 2) * OCT)
-            total = x_ref[i, here, :] + product([count_ref[2, k, here, :]], [rows2[k]])
+            total = x_ref[skip + i, here, :] + product([count_ref[2, k, here, :]], [rows2[k]])
             high, low = parts(total)
             for j in range(2):
                 xh[m + j, there, :] = high[j * OCT : (j + 1) * OCT]
@@ -222,27 +220,23 @@
         high, low = parts(k_ref[d])
         term = dot(xh[d], high) + dot(xh[d], low) + dot(xl[d], high)
         total = term if total is None else total + term
-    for i, out in enumerate((out0, out1)):
+    for i, out in enumerate(outs):
         out[...] = total[i * OCT : (i + 1) * OCT]
 
 
-def finish(first, flags, ids, arrays, x, rows, counts, kernels, codes):
+def finish(first, n, flags, x, rows, counts, kernels, codes):
     return pl.pallas_call(
-        functools.partial(finish_kernel, first),
-        in_specs=[SMEM] + [VMEM] * 13,
-        out_specs=[VMEM] * 2,
-        out_shape=[jax.ShapeDtypeStruct((OCT, WIDTH), F32)] * 2,
-        scratch_shapes=[
-            pltpu.VMEM((RING, BLOCK, 2 * WIDTH), BF16),
-            pltpu.VMEM((DIRS, PAIR * OCT, WIDTH), BF16),
-            pltpu.VMEM((DIRS, PAIR * OCT, WIDTH), BF16),
-        ],
-        compiler_params=pltpu.CompilerParams(vmem_limit_bytes=12 << 20),
+        functools.partial(finish_kernel, first, first % PAIR),
+        in_specs=[SMEM] + [VMEM] * 9,
+        out_specs=[VMEM] * n,
+        out_shape=[jax.ShapeDtypeStruct((OCT, WIDTH), F32)] * n,
+        scratch_shapes=[pltpu.VMEM((DIRS, n * OCT, WIDTH), BF16)] * 2,
+        compiler_params=pltpu.CompilerParams(vmem_limit_bytes=10 << 20),
         cost_estimate=pl.CostEstimate(
-            flops=6_000_000_000, bytes_accessed=2 << 20, transcendentals=0
+            flops=n * 3_000_000_000, bytes_accessed=2 << 20, transcendentals=0
         ),
         name="finish",
-    )(flags, ids, *arrays, x, *rows, counts, kernels, *codes)
+    )(flags, x, *rows, counts, kernels, *codes)
 
 
 def body(partials, partial_ids, read_lists, sources, targets, kernels):
@@ -309,11 +303,13 @@
     low, high, x[0], rows = lax.optimization_barrier((low, high, x[0], rows))
     far = [low, high, across(low), across(high)]
     x[1] = collect((0, 1, 3), PAIR, counts, rows)
-    last = (rows, counts, kernels, codes)
-    out2, out1 = finish(0, flags, ids, far, x[0], *last)
+    (rows2,) = gather((2,), ids, far)
+    last = (rows[:2] + (rows2,) + rows[2:], counts, kernels, codes)
+    out2, out1 = finish(0, 2, flags, x[0], *last)
     ring2, ring1 = along_z(out2, -2), along_z(out1, -1)
-    out3, out0 = finish(PAIR, flags, ids, far, x[1], *last)
+    (out3,) = finish(2, 1, flags, x[1], *last)
     ring3 = along_z(out3, -3)
+    (out0,) = finish(3, 1, flags, x[1], *last)
     return out0 + ring3 + ring2 + ring1
 
 

time: 108 us -> 108 us (level)
  Pallas kernels: 33 us -> 38.1 us
  waiting for transfers between devices: 33.9 us -> 28.9 us
    ppermute x18, waiting for transfers between devices: 31.7 us -> 26.8 us  [fetch(): return lax.ppermute(value, AXES, pairs)]
    pallas_call x2 -> x3, Pallas kernels: 12.5 us -> 16.6 us  [finish(): pl.pallas_call(functools.partial(finish_kernel, first, first % PAIR), in_...]
    pallas_call x2 -> x3, Pallas kernels: 2.05 us -> 2.8 us  [gather(): pl.pallas_call(functools.partial(gather_kernel, blocks), in_specs=[VMEM]...]
  transfers between devices with their start and end apart: 19 -> 19, of which waited for: 9 -> 9; matrix products, arithmetic and copies ran while one was open for 3% -> 3% of each run, Pallas kernels for 25% -> 29%
where the time goes in v6:
time: 108 us
  Pallas kernels  38.1 us (35%)
  starting transfers between devices  35.2 us (33%)
  waiting for transfers between devices  28.9 us (27%)
  local copies, waits for them, and re-layouts  2.92 us (3%)
  other arithmetic  1.72 us (2%)
    ppermute x18, waiting for transfers between devices, fetch(): return lax.ppermute(value, AXES, pairs)  26.8 us
    ppermute x18, starting transfers between devices, fetch(): return lax.ppermute(value, AXES, pairs)  23.7 us
    pallas_call x3, Pallas kernels, finish(): pl.pallas_call(functools.partial(finish_kernel, first, first % PAIR), in_...  16.6 us
    all_to_all x1, starting transfers between devices, body(): lax.all_to_all(partials, AXES, split_axis=0, concat_axis=0, tiled=True)  11.5 us
    pallas_call x1, Pallas kernels, count(): pl.pallas_call(count_kernel, grid=(RING,), in_specs=[codes, codes], out_s...  11.4 us
    pallas_call x2, Pallas kernels, collect(): pl.pallas_call(functools.partial(collect_kernel, blocks, first), in_specs...  7.26 us
    pallas_call x3, Pallas kernels, gather(): pl.pallas_call(functools.partial(gather_kernel, blocks), in_specs=[VMEM]...  2.8 us
  transfers between devices with their start and end apart: 19, of which 9 were waited for; matrix products, arithmetic and copies ran while one was open for 3% of the time, Pallas kernels for 29%

profile of v6, /device:TPU:1, one launch (start us, length us, event | category | flops | bytes accessed | tf_op | source)
XLA Modules:
  0.0 108.0 jit_solution(6091093494493379203)
XLA Ops:
  0.0 11.5 %all-to-all-start = ((f32[128,8,512]{2,1,0:T(8,128)}), f32[128,8,512]{2,1,0:T(8,128)S(1)}, u32[]{:S(2)}, u32[]{:S(2)}) async-start(f32[128,8,512]{2,1,0:T(8,128)} %bitcast.16), calls=%async_computation | async-start | bytes 4194304 | tf_op jit(solution)/shard_map/all_to_all | solution.py:249
  11.6 1.6 %collective-permute-start.5 = (s32[2,8192]{1,0:T(2,128)S(1)}, s32[2,8192]{1,0:T(2,128)S(1)}, u32[]{:S(2)}, u32[]{:S(2)}) collective-permute-start(s32[2,8192]{1,0:T(2,128)S(1)} %get-tuple-element.59), channel_id=1, source_target_pairs={{96,0},{97,1},{98,2},{99,3},{100,4},{101,5},{102,6},{103,7},{104,8... | collective-permute-start | bytes 196616 | tf_op jit(solution)/shard_map/ppermute | solution.py:39
  13.2 1.8 %collective-permute-start.4 = (s32[2,8192]{1,0:T(2,128)S(1)}, s32[2,8192]{1,0:T(2,128)S(1)}, u32[]{:S(2)}, u32[]{:S(2)}) collective-permute-start(s32[2,8192]{1,0:T(2,128)S(1)} %get-tuple-element.59), channel_id=1, source_target_pairs={{32,0},{33,1},{34,2},{35,3},{36,4},{37,5},{38,6},{39,7},{40,8},{41... | collective-permute-start | bytes 196616 | tf_op jit(solution)/shard_map/ppermute | solution.py:39
  15.0 1.4 %collective-permute-start.3 = (s32[2,8192]{1,0:T(2,128)S(1)}, s32[2,8192]{1,0:T(2,128)S(1)}, u32[]{:S(2)}, u32[]{:S(2)}) collective-permute-start(s32[2,8192]{1,0:T(2,128)S(1)} %get-tuple-element.59), channel_id=1, source_target_pairs={{64,0},{65,1},{66,2},{67,3},{68,4},{69,5},{70,6},{71,7},{72,8},{73... | collective-permute-start | bytes 196616 | tf_op jit(solution)/shard_map/ppermute | solution.py:39
  16.4 0.9 fusion.50
  18.5 16.2 %collective-permute-done.5 = s32[2,8192]{1,0:T(2,128)S(1)} collective-permute-done((s32[2,8192]{1,0:T(2,128)S(1)}, s32[2,8192]{1,0:T(2,128)S(1)}, u32[]{:S(2)}, u32[]{:S(2)}) %collective-permute-start.5) | collective-permute-done | bytes 65568 | tf_op jit(solution)/shard_map/ppermute | solution.py:39
  34.7 4.4 %collective-permute-done.3 = s32[2,8192]{1,0:T(2,128)S(1)} collective-permute-done((s32[2,8192]{1,0:T(2,128)S(1)}, s32[2,8192]{1,0:T(2,128)S(1)}, u32[]{:S(2)}, u32[]{:S(2)}) %collective-permute-start.3) | collective-permute-done | bytes 65568 | tf_op jit(solution)/shard_map/ppermute | solution.py:39
  39.1 2.2 %all-to-all-done = f32[128,8,512]{2,1,0:T(8,128)S(1)} async-done(((f32[128,8,512]{2,1,0:T(8,128)}), f32[128,8,512]{2,1,0:T(8,128)S(1)}, u32[]{:S(2)}, u32[]{:S(2)}) %all-to-all-start) | async-done | bytes 2097184 | tf_op jit(solution)/shard_map/all_to_all | solution.py:249
  41.3 0.9 fusion
  42.8 2.5 %collective-permute-start.1 = (f32[128,512]{1,0:T(8,128)S(1)}, f32[128,512]{1,0:T(8,128)S(1)}, u32[]{:S(2)}, u32[]{:S(2)}) collective-permute-start(f32[128,512]{1,0:T(8,128)S(1)} %fusion), channel_id=1, source_target_pairs={{8,0},{9,1},{10,2},{11,3},{12,4},{13,5},{14,6},{15,7},{0,8},{1,9},... | collective-permute-start | bytes 786440 | tf_op jit(solution)/shard_map/ppermute | solution.py:39
  45.3 0.9 collective-permute-start
  47.8 1.2 %collective-permute-done.2 = f32[128,512]{1,0:T(8,128)S(1)} collective-permute-done((f32[128,512]{1,0:T(8,128)S(1)}, f32[128,512]{1,0:T(8,128)S(1)}, u32[]{:S(2)}, u32[]{:S(2)}) %collective-permute-start.2) | collective-permute-done | bytes 262176 | tf_op jit(solution)/shard_map/ppermute | solution.py:39
  49.0 3.2 %collective-permute-done.1 = f32[128,512]{1,0:T(8,128)S(1)} collective-permute-done((f32[128,512]{1,0:T(8,128)S(1)}, f32[128,512]{1,0:T(8,128)S(1)}, u32[]{:S(2)}, u32[]{:S(2)}) %collective-permute-start.1) | collective-permute-done | bytes 262176 | tf_op jit(solution)/shard_map/ppermute | solution.py:39
  53.1 2.2 %collective-permute-start.6 = (f32[512,512]{1,0:T(8,128)S(1)}, f32[512,512]{1,0:T(8,128)S(1)}, u32[]{:S(2)}, u32[]{:S(2)}) collective-permute-start(f32[512,512]{1,0:T(8,128)S(1)} %constant_dynamic-update-slice_fusion.refs_0_), channel_id=1, source_target_pairs={{1,0},{2,1},{3,2},{0,3},{5,4},{6,5},{7,6},{4,7},{9,8},{10,9},{11,1... | collective-permute-start | bytes 3145736 | tf_op jit(solution)/shard_map/ppermute | solution.py:39
  55.3 2.7 %collective-permute-start.10 = (f32[512,512]{1,0:T(8,128)S(1)}, f32[512,512]{1,0:T(8,128)S(1)}, u32[]{:S(2)}, u32[]{:S(2)}) collective-permute-start(f32[512,512]{1,0:T(8,128)S(1)} %constant_dynamic-update-slice_fusion.refs_0_), channel_id=1, source_target_pairs={{16,0},{17,1},{18,2},{19,3},{20,4},{21,5},{22,6},{23,7},{24,8},{25... | collective-permute-start | bytes 3145736 | tf_op jit(solution)/shard_map/ppermute | solution.py:39
  58.0 11.4 %count.1 = (bf16[4,4,1024,256]{3,2,1,0:T(8,128)(2,1)S(1)}, s32[4]{0:T(128)S(1)}) custom-call(s32[32,1024]{1,0:T(8,128)S(1)} %get-tuple-element.32.row_ref, s32[32,1024]{1,0:T(8,128)S(1)} %get-tuple-element.33.col_ref), custom_call_target="tpu_custom_call" | custom-call | flops 100000000 | bytes 1048576 | tf_op jit(solution)/shard_map/count/pallas_call | solution.py:90
  69.3 1.4 %collective-permute-start.11 = (f32[512,512]{1,0:T(8,128)S(1)}, f32[512,512]{1,0:T(8,128)S(1)}, u32[]{:S(2)}, u32[]{:S(2)}) collective-permute-start(f32[512,512]{1,0:T(8,128)S(1)} %collective-permute-done.6.refs_0_), channel_id=1, source_target_pairs={{16,0},{17,1},{18,2},{19,3},{20,4},{21,5},{22,6},{23,7},{24,8},{25... | collective-permute-start | bytes 3145736 | tf_op jit(solution)/shard_map/ppermute | solution.py:39
  70.8 1.2 %collective-permute-start.9 = (f32[256,512]{1,0:T(8,128)S(1)}, f32[256,512]{1,0:T(8,128)S(1)}, u32[]{:S(2)}, u32[]{:S(2)}) collective-permute-start(f32[256,512]{1,0:T(8,128)S(1)} %slice.15), channel_id=1, source_target_pairs={{3,0},{0,1},{1,2},{2,3},{7,4},{4,5},{5,6},{6,7},{11,8},{8,9},{9,10... | collective-permute-start | bytes 1572872 | tf_op jit(solution)/shard_map/ppermute | solution.py:39
  72.0 1.6 %collective-permute-start.8 = (f32[256,512]{1,0:T(8,128)S(1)}, f32[256,512]{1,0:T(8,128)S(1)}, u32[]{:S(2)}, u32[]{:S(2)}) collective-permute-start(f32[256,512]{1,0:T(8,128)S(1)} %slice.14), channel_id=1, source_target_pairs={{1,0},{2,1},{3,2},{0,3},{5,4},{6,5},{7,6},{4,7},{9,8},{10,9},{11,1... | collective-permute-start | bytes 1572872 | tf_op jit(solution)/shard_map/ppermute | solution.py:39
  73.6 0.7 gather.10.refs_0_.rows0
  74.5 1.3 %gather.11 = (bf16[4,256,1024]{2,1,0:T(8,128)(2,1)S(1)}, bf16[4,256,1024]{2,1,0:T(8,128)(2,1)S(1)}) custom-call(s32[32,128]{1,0:T(8,128)S(1)} %broadcast_select_fusion.ids_ref, f32[512,512]{1,0:T(8,128)S(1)} %collective-permute-done.6.refs_0_, f32[512,512]{1,0:T(8,128)S(1)} %collective-permute-done.11.refs_1_, ...), custom_call_target="tpu_custom_call" | custom-call | flops 3000000000 | bytes 2097152 | tf_op jit(solution)/shard_map/gather/pallas_call | solution.py:136
  75.9 3.6 %collect.2.x_ref = f32[2,1024,512]{2,1,0:T(8,128)S(1)} custom-call(bf16[4,4,1024,256]{3,2,1,0:T(8,128)(2,1)S(1)} %get-tuple-element.37.count_ref, bf16[4,256,1024]{2,1,0:T(8,128)(2,1)S(1)} %gather.10.refs_0_.rows0, bf16[4,256,1024]{2,1,0:T(8,128)(2,1)S(1)} %get-tuple-element.44.refs_1_.rows1, bf16[4,256,1024]{2,1,0:T(8,128)(2,1)S(1)} %get-tuple-element.45.refs_2_.rows3), custom_call_target="tpu_custom_call" | custom-call | flops 3300000000 | bytes 3145728 | tf_op jit(solution)/shard_map/collect/pallas_call | solution.py:173
  79.5 0.9 collective-permute-done.9.refs_1_
  80.4 1.4 %collective-permute-start.13 = (f32[256,512]{1,0:T(8,128)S(1)}, f32[256,512]{1,0:T(8,128)S(1)}, u32[]{:S(2)}, u32[]{:S(2)}) collective-permute-start(f32[256,512]{1,0:T(8,128)S(1)} %collective-permute-done.8.refs_0_), channel_id=1, source_target_pairs={{16,0},{17,1},{18,2},{19,3},{20,4},{21,5},{22,6},{23,7},{24,8},{25... | collective-permute-start | bytes 1572872 | tf_op jit(solution)/shard_map/ppermute | solution.py:39
  81.8 3.6 %collect.3.x_ref = f32[2,1024,512]{2,1,0:T(8,128)S(1)} custom-call(bf16[4,4,1024,256]{3,2,1,0:T(8,128)(2,1)S(1)} %get-tuple-element.37.count_ref, bf16[4,256,1024]{2,1,0:T(8,128)(2,1)S(1)} %gather.10.refs_0_.rows0, bf16[4,256,1024]{2,1,0:T(8,128)(2,1)S(1)} %get-tuple-element.44.refs_1_.rows1, bf16[4,256,1024]{2,1,0:T(8,128)(2,1)S(1)} %get-tuple-element.45.refs_2_.rows3), custom_call_target="tpu_custom_call" | custom-call | flops 3300000000 | bytes 3145728 | tf_op jit(solution)/shard_map/collect/pallas_call | solution.py:173
  85.5 0.7 gather.12.rows2
  86.2 5.5 %finish.5 = (f32[128,512]{1,0:T(8,128)S(1)}, f32[128,512]{1,0:T(8,128)S(1)}) custom-call(s32[4]{0:T(128)S(1)} %get-tuple-element.36.flag_ref, f32[2,1024,512]{2,1,0:T(8,128)S(1)} %collect.2.x_ref, bf16[4,256,1024]{2,1,0:T(8,128)(2,1)S(1)} %gather.10.refs_0_.rows0, bf16[4,256,1024]{2,1,0:T(8,128)(2,1)S(1)} %get-tuple-element.44.refs_1_.rows1, ...), custom_call_target="tpu_custom_call" | custom-call | flops 6000000000 | bytes 2097152 | tf_op jit(solution)/shard_map/finish/pallas_call | solution.py:228
  91.8 1.1 %collective-permute-start.16 = (f32[128,512]{1,0:T(8,128)S(1)}, f32[128,512]{1,0:T(8,128)S(1)}, u32[]{:S(2)}, u32[]{:S(2)}) collective-permute-start(f32[128,512]{1,0:T(8,128)S(1)} %get-tuple-element.49), channel_id=1, source_target_pairs={{64,0},{65,1},{66,2},{67,3},{68,4},{69,5},{70,6},{71,7},{72,8},{73... | collective-permute-start | bytes 786440 | tf_op jit(solution)/shard_map/ppermute | solution.py:39
  93.5 5.6 %finish.4 = f32[128,512]{1,0:T(8,128)S(1)} custom-call(s32[4]{0:T(128)S(1)} %get-tuple-element.36.flag_ref, f32[2,1024,512]{2,1,0:T(8,128)S(1)} %collect.3.x_ref, bf16[4,256,1024]{2,1,0:T(8,128)(2,1)S(1)} %gather.10.refs_0_.rows0, bf16[4,256,1024]{2,1,0:T(8,128)(2,1)S(1)} %get-tuple-element.44.refs_1_.rows1, bf16[4,256,1024]{2,1,0:T(8,128)(2,1)S(1)} %gather.12.rows2, ...), custom_call_target="tpu_custom_call" | custom-call | flops 3000000000 | bytes 2097152 | tf_op jit(solution)/shard_map/finish/pallas_call | solution.py:228
  99.0 2.2 %collective-permute-start.15 = (f32[128,512]{1,0:T(8,128)S(1)}, f32[128,512]{1,0:T(8,128)S(1)}, u32[]{:S(2)}, u32[]{:S(2)}) collective-permute-start(f32[128,512]{1,0:T(8,128)S(1)} %finish.4), channel_id=1, source_target_pairs={{32,0},{33,1},{34,2},{35,3},{36,4},{37,5},{38,6},{39,7},{40,8},{41... | collective-permute-start | bytes 786440 | tf_op jit(solution)/shard_map/ppermute | solution.py:39
  101.2 5.6 %finish.3 = f32[128,512]{1,0:T(8,128)S(1)} custom-call(s32[4]{0:T(128)S(1)} %get-tuple-element.36.flag_ref, f32[2,1024,512]{2,1,0:T(8,128)S(1)} %collect.3.x_ref, bf16[4,256,1024]{2,1,0:T(8,128)(2,1)S(1)} %gather.10.refs_0_.rows0, bf16[4,256,1024]{2,1,0:T(8,128)(2,1)S(1)} %get-tuple-element.44.refs_1_.rows1, bf16[4,256,1024]{2,1,0:T(8,128)(2,1)S(1)} %gather.12.rows2, ...), custom_call_target="tpu_custom_call" | custom-call | flops 3000000000 | bytes 2097152 | tf_op jit(solution)/shard_map/finish/pallas_call | solution.py:228
  107.2 0.8 add_add_fusion
  (52 shorter events, 5.5 us)
Async XLA Ops:
  0.0 18.4 %copy-start = (s32[128,1024]{1,0:T(8,128)S(1)}, s32[128,1024]{1,0:T(8,128)}, u32[]{:S(2)}) copy-start(s32[128,1024]{1,0:T(8,128)} %param.7) | copy-start | bytes 1572868
  0.0 11.5 %copy-start.1 = (s32[1,8192]{1,0:T(1,128)S(1)}, s32[1,8192]{1,0:T(1,128)}, u32[]{:S(2)}) copy-start(s32[1,8192]{1,0:T(1,128)} %param.10) | copy-start | bytes 98308
  0.0 11.5 %copy-start.2 = (s32[1,8192]{1,0:T(1,128)S(1)}, s32[1,8192]{1,0:T(1,128)}, u32[]{:S(2)}) copy-start(s32[1,8192]{1,0:T(1,128)} %param.9) | copy-start | bytes 98308
  0.0 41.3 %all-to-all-start = ((f32[128,8,512]{2,1,0:T(8,128)}), f32[128,8,512]{2,1,0:T(8,128)S(1)}, u32[]{:S(2)}, u32[]{:S(2)}) async-start(f32[128,8,512]{2,1,0:T(8,128)} %bitcast.16), calls=%async_computation | async-start | bytes 4194304 | tf_op jit(solution)/shard_map/all_to_all | solution.py:249
  11.6 23.1 %collective-permute-start.5 = (s32[2,8192]{1,0:T(2,128)S(1)}, s32[2,8192]{1,0:T(2,128)S(1)}, u32[]{:S(2)}, u32[]{:S(2)}) collective-permute-start(s32[2,8192]{1,0:T(2,128)S(1)} %get-tuple-element.59), channel_id=1, source_target_pairs={{96,0},{97,1},{98,2},{99,3},{100,4},{101,5},{102,6},{103,7},{104,8... | collective-permute-start | bytes 196616 | tf_op jit(solution)/shard_map/ppermute | solution.py:39
  13.2 21.5 %collective-permute-start.4 = (s32[2,8192]{1,0:T(2,128)S(1)}, s32[2,8192]{1,0:T(2,128)S(1)}, u32[]{:S(2)}, u32[]{:S(2)}) collective-permute-start(s32[2,8192]{1,0:T(2,128)S(1)} %get-tuple-element.59), channel_id=1, source_target_pairs={{32,0},{33,1},{34,2},{35,3},{36,4},{37,5},{38,6},{39,7},{40,8},{41... | collective-permute-start | bytes 196616 | tf_op jit(solution)/shard_map/ppermute | solution.py:39
  15.0 24.1 %collective-permute-start.3 = (s32[2,8192]{1,0:T(2,128)S(1)}, s32[2,8192]{1,0:T(2,128)S(1)}, u32[]{:S(2)}, u32[]{:S(2)}) collective-permute-start(s32[2,8192]{1,0:T(2,128)S(1)} %get-tuple-element.59), channel_id=1, source_target_pairs={{64,0},{65,1},{66,2},{67,3},{68,4},{69,5},{70,6},{71,7},{72,8},{73... | collective-permute-start | bytes 196616 | tf_op jit(solution)/shard_map/ppermute | solution.py:39
  42.2 6.8 %collective-permute-start.2 = (f32[128,512]{1,0:T(8,128)S(1)}, f32[128,512]{1,0:T(8,128)S(1)}, u32[]{:S(2)}, u32[]{:S(2)}) collective-permute-start(f32[128,512]{1,0:T(8,128)S(1)} %fusion), channel_id=1, source_target_pairs={{12,0},{13,1},{14,2},{15,3},{0,4},{1,5},{2,6},{3,7},{4,8},{5,9},{6... | collective-permute-start | bytes 786440 | tf_op jit(solution)/shard_map/ppermute | solution.py:39
  42.8 9.4 %collective-permute-start.1 = (f32[128,512]{1,0:T(8,128)S(1)}, f32[128,512]{1,0:T(8,128)S(1)}, u32[]{:S(2)}, u32[]{:S(2)}) collective-permute-start(f32[128,512]{1,0:T(8,128)S(1)} %fusion), channel_id=1, source_target_pairs={{8,0},{9,1},{10,2},{11,3},{12,4},{13,5},{14,6},{15,7},{0,8},{1,9},... | collective-permute-start | bytes 786440 | tf_op jit(solution)/shard_map/ppermute | solution.py:39
  45.3 7.1 %collective-permute-start = (f32[128,512]{1,0:T(8,128)S(1)}, f32[128,512]{1,0:T(8,128)S(1)}, u32[]{:S(2)}, u32[]{:S(2)}) collective-permute-start(f32[128,512]{1,0:T(8,128)S(1)} %fusion), channel_id=1, source_target_pairs={{4,0},{5,1},{6,2},{7,3},{8,4},{9,5},{10,6},{11,7},{12,8},{13,9},{1... | collective-permute-start | bytes 786440 | tf_op jit(solution)/shard_map/ppermute | solution.py:39
  52.5 16.8 %collective-permute-start.7 = (f32[512,512]{1,0:T(8,128)S(1)}, f32[512,512]{1,0:T(8,128)S(1)}, u32[]{:S(2)}, u32[]{:S(2)}) collective-permute-start(f32[512,512]{1,0:T(8,128)S(1)} %constant_dynamic-update-slice_fusion.refs_0_), channel_id=1, source_target_pairs={{3,0},{0,1},{1,2},{2,3},{7,4},{4,5},{5,6},{6,7},{11,8},{8,9},{9,10... | collective-permute-start | bytes 3145736 | tf_op jit(solution)/shard_map/ppermute | solution.py:39
  53.1 16.3 %collective-permute-start.6 = (f32[512,512]{1,0:T(8,128)S(1)}, f32[512,512]{1,0:T(8,128)S(1)}, u32[]{:S(2)}, u32[]{:S(2)}) collective-permute-start(f32[512,512]{1,0:T(8,128)S(1)} %constant_dynamic-update-slice_fusion.refs_0_), channel_id=1, source_target_pairs={{1,0},{2,1},{3,2},{0,3},{5,4},{6,5},{7,6},{4,7},{9,8},{10,9},{11,1... | collective-permute-start | bytes 3145736 | tf_op jit(solution)/shard_map/ppermute | solution.py:39
  55.3 18.3 %collective-permute-start.10 = (f32[512,512]{1,0:T(8,128)S(1)}, f32[512,512]{1,0:T(8,128)S(1)}, u32[]{:S(2)}, u32[]{:S(2)}) collective-permute-start(f32[512,512]{1,0:T(8,128)S(1)} %constant_dynamic-update-slice_fusion.refs_0_), channel_id=1, source_target_pairs={{16,0},{17,1},{18,2},{19,3},{20,4},{21,5},{22,6},{23,7},{24,8},{25... | collective-permute-start | bytes 3145736 | tf_op jit(solution)/shard_map/ppermute | solution.py:39
  69.3 5.0 %collective-permute-start.11 = (f32[512,512]{1,0:T(8,128)S(1)}, f32[512,512]{1,0:T(8,128)S(1)}, u32[]{:S(2)}, u32[]{:S(2)}) collective-permute-start(f32[512,512]{1,0:T(8,128)S(1)} %collective-permute-done.6.refs_0_), channel_id=1, source_target_pairs={{16,0},{17,1},{18,2},{19,3},{20,4},{21,5},{22,6},{23,7},{24,8},{25... | collective-permute-start | bytes 3145736 | tf_op jit(solution)/shard_map/ppermute | solution.py:39
  70.7 3.8 %collective-permute-start.12 = (f32[512,512]{1,0:T(8,128)S(1)}, f32[512,512]{1,0:T(8,128)S(1)}, u32[]{:S(2)}, u32[]{:S(2)}) collective-permute-start(f32[512,512]{1,0:T(8,128)S(1)} %collective-permute-done.7.refs_2_), channel_id=1, source_target_pairs={{16,0},{17,1},{18,2},{19,3},{20,4},{21,5},{22,6},{23,7},{24,8},{25... | collective-permute-start | bytes 3145736 | tf_op jit(solution)/shard_map/ppermute | solution.py:39
  70.8 9.6 %collective-permute-start.9 = (f32[256,512]{1,0:T(8,128)S(1)}, f32[256,512]{1,0:T(8,128)S(1)}, u32[]{:S(2)}, u32[]{:S(2)}) collective-permute-start(f32[256,512]{1,0:T(8,128)S(1)} %slice.15), channel_id=1, source_target_pairs={{3,0},{0,1},{1,2},{2,3},{7,4},{4,5},{5,6},{6,7},{11,8},{8,9},{9,10... | collective-permute-start | bytes 1572872 | tf_op jit(solution)/shard_map/ppermute | solution.py:39
  72.0 8.4 %collective-permute-start.8 = (f32[256,512]{1,0:T(8,128)S(1)}, f32[256,512]{1,0:T(8,128)S(1)}, u32[]{:S(2)}, u32[]{:S(2)}) collective-permute-start(f32[256,512]{1,0:T(8,128)S(1)} %slice.14), channel_id=1, source_target_pairs={{1,0},{2,1},{3,2},{0,3},{5,4},{6,5},{7,6},{4,7},{9,8},{10,9},{11,1... | collective-permute-start | bytes 1572872 | tf_op jit(solution)/shard_map/ppermute | solution.py:39
  75.8 10.4 %slice-start = ((s8[8388608]{0:T(1024)(128)(4,1)}), s8[4194304]{0:T(1024)(128)(4,1)S(1)}, s32[]{:S(2)}) async-start(s8[8388608]{0:T(1024)(128)(4,1)} %bitcast.14), calls=%async_computation.1 | async-start | bytes 8388608
  79.5 6.7 %slice-start.1 = ((s8[8388608]{0:T(1024)(128)(4,1)}), s8[4194304]{0:T(1024)(128)(4,1)S(1)}, s32[]{:S(2)}) async-start(s8[8388608]{0:T(1024)(128)(4,1)} %bitcast.14), calls=%async_computation.2 | async-start | bytes 8388608
  80.4 5.0 %collective-permute-start.13 = (f32[256,512]{1,0:T(8,128)S(1)}, f32[256,512]{1,0:T(8,128)S(1)}, u32[]{:S(2)}, u32[]{:S(2)}) collective-permute-start(f32[256,512]{1,0:T(8,128)S(1)} %collective-permute-done.8.refs_0_), channel_id=1, source_target_pairs={{16,0},{17,1},{18,2},{19,3},{20,4},{21,5},{22,6},{23,7},{24,8},{25... | collective-permute-start | bytes 1572872 | tf_op jit(solution)/shard_map/ppermute | solution.py:39
  81.8 3.7 %collective-permute-start.14 = (f32[256,512]{1,0:T(8,128)S(1)}, f32[256,512]{1,0:T(8,128)S(1)}, u32[]{:S(2)}, u32[]{:S(2)}) collective-permute-start(f32[256,512]{1,0:T(8,128)S(1)} %collective-permute-done.9.refs_1_), channel_id=1, source_target_pairs={{16,0},{17,1},{18,2},{19,3},{20,4},{21,5},{22,6},{23,7},{24,8},{25... | collective-permute-start | bytes 1572872 | tf_op jit(solution)/shard_map/ppermute | solution.py:39
  91.8 15.0 %collective-permute-start.16 = (f32[128,512]{1,0:T(8,128)S(1)}, f32[128,512]{1,0:T(8,128)S(1)}, u32[]{:S(2)}, u32[]{:S(2)}) collective-permute-start(f32[128,512]{1,0:T(8,128)S(1)} %get-tuple-element.49), channel_id=1, source_target_pairs={{64,0},{65,1},{66,2},{67,3},{68,4},{69,5},{70,6},{71,7},{72,8},{73... | collective-permute-start | bytes 786440 | tf_op jit(solution)/shard_map/ppermute | solution.py:39
  92.9 14.3 %collective-permute-start.17 = (f32[128,512]{1,0:T(8,128)S(1)}, f32[128,512]{1,0:T(8,128)S(1)}, u32[]{:S(2)}, u32[]{:S(2)}) collective-permute-start(f32[128,512]{1,0:T(8,128)S(1)} %get-tuple-element.50), channel_id=1, source_target_pairs={{96,0},{97,1},{98,2},{99,3},{100,4},{101,5},{102,6},{103,7},{104,8... | collective-permute-start | bytes 786440 | tf_op jit(solution)/shard_map/ppermute | solution.py:39
  99.0 8.2 %collective-permute-start.15 = (f32[128,512]{1,0:T(8,128)S(1)}, f32[128,512]{1,0:T(8,128)S(1)}, u32[]{:S(2)}, u32[]{:S(2)}) collective-permute-start(f32[128,512]{1,0:T(8,128)S(1)} %finish.4), channel_id=1, source_target_pairs={{32,0},{33,1},{34,2},{35,3},{36,4},{37,5},{38,6},{39,7},{40,8},{41... | collective-permute-start | bytes 786440 | tf_op jit(solution)/shard_map/ppermute | solution.py:39

commit v7 on v6

--- a/solution.py
+++ b/solution.py
@@ -184,8 +184,8 @@
 
 
 def finish_kernel(
-    first, skip, flag_ref, x_ref, rows0, rows1, rows2, rows3, count_ref, k_ref, row_ref, col_ref,
-    *refs,
+    first, flag_ref, x_ref, rows0, rows1, rows2, rows3, count_ref, kh_ref, kl_ref,
+    row_ref, col_ref, *refs,
 ):
     outs, xh, xl = refs[:-2], refs[-2], refs[-1]
     for i in range(len(outs)):
@@ -193,7 +193,8 @@
         there = slice(i * OCT, (i + 1) * OCT)
         for m in range(0, DIRS, 2):
             here = slice(m * OCT, (m + 2) * OCT)
-            total = x_ref[skip + i, here, :] + product([count_ref[2, k, here, :]], [rows2[k]])
+            old = x_ref[k % PAIR, here, :]
+            total = old + product([count_ref[2, k, here, :]], [rows2[k]])
             high, low = parts(total)
             for j in range(2):
                 xh[m + j, there, :] = high[j * OCT : (j + 1) * OCT]
@@ -213,12 +214,11 @@
                 xl[d, there, :] = low
 
     def dot(a, b):
-        return lax.dot_general(a, b, (((1,), (1,)), ((), ())), preferred_element_type=F32)
+        return jnp.dot(a, b, preferred_element_type=F32)
 
     total = None
     for d in range(DIRS):
-        high, low = parts(k_ref[d])
-        term = dot(xh[d], high) + dot(xh[d], low) + dot(xl[d], high)
+        term = dot(xh[d], kh_ref[d]) + dot(xh[d], kl_ref[d]) + dot(xl[d], kh_ref[d])
         total = term if total is None else total + term
     for i, out in enumerate(outs):
         out[...] = total[i * OCT : (i + 1) * OCT]
@@ -226,8 +226,8 @@
 
 def finish(first, n, flags, x, rows, counts, kernels, codes):
     return pl.pallas_call(
-        functools.partial(finish_kernel, first, first % PAIR),
-        in_specs=[SMEM] + [VMEM] * 9,
+        functools.partial(finish_kernel, first),
+        in_specs=[SMEM] + [VMEM] * 10,
         out_specs=[VMEM] * n,
         out_shape=[jax.ShapeDtypeStruct((OCT, WIDTH), F32)] * n,
         scratch_shapes=[pltpu.VMEM((DIRS, n * OCT, WIDTH), BF16)] * 2,
@@ -236,7 +236,27 @@
             flops=n * 3_000_000_000, bytes_accessed=2 << 20, transcendentals=0
         ),
         name="finish",
-    )(flags, x, *rows, counts, kernels, *codes)
+    )(flags, x, *rows, counts, *kernels, *codes)
+
+
+def turn_kernel(k_ref, high_ref, low_ref):
+    high_ref[0], low_ref[0] = parts(k_ref[0].T)
+
+
+def turn(kernels):
+    spec = pl.BlockSpec((1, WIDTH, WIDTH), lambda d: (d, 0, 0))
+    return pl.pallas_call(
+        turn_kernel,
+        grid=(DIRS,),
+        in_specs=[spec],
+        out_specs=[spec] * 2,
+        out_shape=[jax.ShapeDtypeStruct(kernels.shape, BF16)] * 2,
+        compiler_params=pltpu.CompilerParams(vmem_limit_bytes=12 << 20),
+        cost_estimate=pl.CostEstimate(
+            flops=100_000_000, bytes_accessed=1 << 20, transcendentals=0
+        ),
+        name="turn",
+    )(kernels)
 
 
 def body(partials, partial_ids, read_lists, sources, targets, kernels):
@@ -282,6 +302,7 @@
     per_dir = sources.shape[1] // DIRS
     codes = [code.reshape(RING * DIRS, per_dir) for code in (row_codes, column)]
 
+    received, *kernels = lax.optimization_barrier((received, *turn(kernels)))
     octants = jnp.arange(OCT, dtype=jnp.int32)
     column_ids = lax.dynamic_slice_in_dim(partial_ids, device * per_owner, per_owner, 1).reshape(-1)
     selector = (octants[:, None] == column_ids[None, :]).astype(F32)

time: 108 us -> 110 us (1.019)
  local copies, waits for them, and re-layouts: 2.92 us -> 11.7 us
  waiting for transfers between devices: 28.9 us -> 23.6 us
  Pallas kernels: 38.1 us -> 36 us
    unnamed x13 -> x19, local copies, waits for them, and re-layouts: 0.08 us -> 8.82 us
    ppermute x18, waiting for transfers between devices: 26.8 us -> 21.4 us  [fetch(): return lax.ppermute(value, AXES, pairs)]
    pallas_call x3 -> x4, Pallas kernels: 16.6 us -> 14.6 us  [the longest x3 11.8 us: finish(): pl.pallas_call(functools.partial(finish_kernel, first), in_specs=[SMEM] +...]
  transfers between devices with their start and end apart: 19 -> 19, of which waited for: 9 -> 9; matrix products, arithmetic and copies ran while one was open for 3% -> 3% of each run, Pallas kernels for 29% -> 27%
where the time goes in v7:
time: 110 us; the launch traced here: 109 us
  Pallas kernels  36 us (33%)
  starting transfers between devices  35.2 us (32%)
  waiting for transfers between devices  23.6 us (21%)
  local copies, waits for them, and re-layouts  11.7 us (11%)
  other arithmetic  1.72 us (2%)
    ppermute x18, starting transfers between devices, fetch(): return lax.ppermute(value, AXES, pairs)  23.7 us
    ppermute x18, waiting for transfers between devices, fetch(): return lax.ppermute(value, AXES, pairs)  21.4 us
    pallas_call x3, Pallas kernels, finish(): pl.pallas_call(functools.partial(finish_kernel, first), in_specs=[SMEM] +...  11.8 us
    all_to_all x1, starting transfers between devices, body(): lax.all_to_all(partials, AXES, split_axis=0, concat_axis=0, tiled=True)  11.5 us
    pallas_call x1, Pallas kernels, count(): pl.pallas_call(count_kernel, grid=(RING,), in_specs=[codes, codes], out_s...  11.4 us
    unnamed x19, local copies, waits for them, and re-layouts  8.82 us
    pallas_call x2, Pallas kernels, collect(): pl.pallas_call(functools.partial(collect_kernel, blocks, first), in_specs...  7.26 us
    pallas_call x3, Pallas kernels, gather(): pl.pallas_call(functools.partial(gather_kernel, blocks), in_specs=[VMEM]...  2.8 us
  transfers between devices with their start and end apart: 19, of which 9 were waited for; matrix products, arithmetic and copies ran while one was open for 3% of the time, Pallas kernels for 27%

profile of v7, /device:TPU:1, one launch (start us, length us, event | category | flops | bytes accessed | tf_op | source)
XLA Modules:
  0.0 109.3 jit_solution(2548235985821468699)
XLA Ops:
  0.0 11.5 %all-to-all-start = ((f32[128,8,512]{2,1,0:T(8,128)}), f32[128,8,512]{2,1,0:T(8,128)S(1)}, u32[]{:S(2)}, u32[]{:S(2)}) async-start(f32[128,8,512]{2,1,0:T(8,128)} %bitcast.14), calls=%async_computation | async-start | bytes 4194304 | tf_op jit(solution)/shard_map/all_to_all | solution.py:269
  11.6 1.6 %collective-permute-start.5 = (s32[2,8192]{1,0:T(2,128)S(1)}, s32[2,8192]{1,0:T(2,128)S(1)}, u32[]{:S(2)}, u32[]{:S(2)}) collective-permute-start(s32[2,8192]{1,0:T(2,128)S(1)} %get-tuple-element.69), channel_id=1, source_target_pairs={{96,0},{97,1},{98,2},{99,3},{100,4},{101,5},{102,6},{103,7},{104,8... | collective-permute-start | bytes 196616 | tf_op jit(solution)/shard_map/ppermute | solution.py:39
  13.2 1.8 %collective-permute-start.4 = (s32[2,8192]{1,0:T(2,128)S(1)}, s32[2,8192]{1,0:T(2,128)S(1)}, u32[]{:S(2)}, u32[]{:S(2)}) collective-permute-start(s32[2,8192]{1,0:T(2,128)S(1)} %get-tuple-element.69), channel_id=1, source_target_pairs={{32,0},{33,1},{34,2},{35,3},{36,4},{37,5},{38,6},{39,7},{40,8},{41... | collective-permute-start | bytes 196616 | tf_op jit(solution)/shard_map/ppermute | solution.py:39
  15.0 1.4 %collective-permute-start.3 = (s32[2,8192]{1,0:T(2,128)S(1)}, s32[2,8192]{1,0:T(2,128)S(1)}, u32[]{:S(2)}, u32[]{:S(2)}) collective-permute-start(s32[2,8192]{1,0:T(2,128)S(1)} %get-tuple-element.69), channel_id=1, source_target_pairs={{64,0},{65,1},{66,2},{67,3},{68,4},{69,5},{70,6},{71,7},{72,8},{73... | collective-permute-start | bytes 196616 | tf_op jit(solution)/shard_map/ppermute | solution.py:39
  18.5 3.4 %copy-done.5 = f32[8,512,512]{2,1,0:T(8,128)S(1)} copy-done((f32[8,512,512]{2,1,0:T(8,128)S(1)}, f32[8,512,512]{2,1,0:T(8,128)}, u32[]{:S(2)}) %copy-start.5) | copy-done | bytes 8388632
  21.9 2.8 %turn.1 = (bf16[8,512,512]{2,1,0:T(8,128)(2,1)S(1)}, bf16[8,512,512]{2,1,0:T(8,128)(2,1)S(1)}) custom-call(f32[8,512,512]{2,1,0:T(8,128)S(1)} %copy-done.5), custom_call_target="tpu_custom_call" | custom-call | flops 100000000 | bytes 1048576 | tf_op jit(solution)/shard_map/turn/pallas_call | solution.py:248
  24.7 1.9 %copy-done.1 = bf16[8,512,512]{2,1,0:T(8,128)(2,1)} copy-done((bf16[8,512,512]{2,1,0:T(8,128)(2,1)}, bf16[8,512,512]{2,1,0:T(8,128)(2,1)S(1)}, u32[]{:S(2)}) %copy-start.1) | copy-done | bytes 4194328
  26.7 2.0 %copy-done.3 = bf16[8,512,512]{2,1,0:T(8,128)(2,1)} copy-done((bf16[8,512,512]{2,1,0:T(8,128)(2,1)}, bf16[8,512,512]{2,1,0:T(8,128)(2,1)S(1)}, u32[]{:S(2)}) %copy-start.3) | copy-done | bytes 4194328
  28.7 6.0 %collective-permute-done.5 = s32[2,8192]{1,0:T(2,128)S(1)} collective-permute-done((s32[2,8192]{1,0:T(2,128)S(1)}, s32[2,8192]{1,0:T(2,128)S(1)}, u32[]{:S(2)}, u32[]{:S(2)}) %collective-permute-start.5) | collective-permute-done | bytes 65568 | tf_op jit(solution)/shard_map/ppermute | solution.py:39
  34.7 4.4 %collective-permute-done.3 = s32[2,8192]{1,0:T(2,128)S(1)} collective-permute-done((s32[2,8192]{1,0:T(2,128)S(1)}, s32[2,8192]{1,0:T(2,128)S(1)}, u32[]{:S(2)}, u32[]{:S(2)}) %collective-permute-start.3) | collective-permute-done | bytes 65568 | tf_op jit(solution)/shard_map/ppermute | solution.py:39
  39.1 2.2 %all-to-all-done = f32[128,8,512]{2,1,0:T(8,128)S(1)} async-done(((f32[128,8,512]{2,1,0:T(8,128)}), f32[128,8,512]{2,1,0:T(8,128)S(1)}, u32[]{:S(2)}, u32[]{:S(2)}) %all-to-all-start) | async-done | bytes 2097184 | tf_op jit(solution)/shard_map/all_to_all | solution.py:269
  42.8 2.5 %collective-permute-start.1 = (f32[128,512]{1,0:T(8,128)S(1)}, f32[128,512]{1,0:T(8,128)S(1)}, u32[]{:S(2)}, u32[]{:S(2)}) collective-permute-start(f32[128,512]{1,0:T(8,128)S(1)} %fusion), channel_id=1, source_target_pairs={{8,0},{9,1},{10,2},{11,3},{12,4},{13,5},{14,6},{15,7},{0,8},{1,9},... | collective-permute-start | bytes 786440 | tf_op jit(solution)/shard_map/ppermute | solution.py:39
  47.8 1.2 %collective-permute-done.2 = f32[128,512]{1,0:T(8,128)S(1)} collective-permute-done((f32[128,512]{1,0:T(8,128)S(1)}, f32[128,512]{1,0:T(8,128)S(1)}, u32[]{:S(2)}, u32[]{:S(2)}) %collective-permute-start.2) | collective-permute-done | bytes 262176 | tf_op jit(solution)/shard_map/ppermute | solution.py:39
  49.0 3.2 %collective-permute-done.1 = f32[128,512]{1,0:T(8,128)S(1)} collective-permute-done((f32[128,512]{1,0:T(8,128)S(1)}, f32[128,512]{1,0:T(8,128)S(1)}, u32[]{:S(2)}, u32[]{:S(2)}) %collective-permute-start.1) | collective-permute-done | bytes 262176 | tf_op jit(solution)/shard_map/ppermute | solution.py:39
  53.1 2.2 %collective-permute-start.6 = (f32[512,512]{1,0:T(8,128)S(1)}, f32[512,512]{1,0:T(8,128)S(1)}, u32[]{:S(2)}, u32[]{:S(2)}) collective-permute-start(f32[512,512]{1,0:T(8,128)S(1)} %constant_dynamic-update-slice_fusion.refs_0_), channel_id=1, source_target_pairs={{1,0},{2,1},{3,2},{0,3},{5,4},{6,5},{7,6},{4,7},{9,8},{10,9},{11,1... | collective-permute-start | bytes 3145736 | tf_op jit(solution)/shard_map/ppermute | solution.py:39
  55.3 2.7 %collective-permute-start.10 = (f32[512,512]{1,0:T(8,128)S(1)}, f32[512,512]{1,0:T(8,128)S(1)}, u32[]{:S(2)}, u32[]{:S(2)}) collective-permute-start(f32[512,512]{1,0:T(8,128)S(1)} %constant_dynamic-update-slice_fusion.refs_0_), channel_id=1, source_target_pairs={{16,0},{17,1},{18,2},{19,3},{20,4},{21,5},{22,6},{23,7},{24,8},{25... | collective-permute-start | bytes 3145736 | tf_op jit(solution)/shard_map/ppermute | solution.py:39
  58.0 11.4 %count.1 = (bf16[4,4,1024,256]{3,2,1,0:T(8,128)(2,1)S(1)}, s32[4]{0:T(128)S(1)}) custom-call(s32[32,1024]{1,0:T(8,128)S(1)} %get-tuple-element.40.row_ref, s32[32,1024]{1,0:T(8,128)S(1)} %get-tuple-element.41.col_ref), custom_call_target="tpu_custom_call" | custom-call | flops 100000000 | bytes 1048576 | tf_op jit(solution)/shard_map/count/pallas_call | solution.py:90
  69.3 1.4 %collective-permute-start.11 = (f32[512,512]{1,0:T(8,128)S(1)}, f32[512,512]{1,0:T(8,128)S(1)}, u32[]{:S(2)}, u32[]{:S(2)}) collective-permute-start(f32[512,512]{1,0:T(8,128)S(1)} %collective-permute-done.6.refs_0_), channel_id=1, source_target_pairs={{16,0},{17,1},{18,2},{19,3},{20,4},{21,5},{22,6},{23,7},{24,8},{25... | collective-permute-start | bytes 3145736 | tf_op jit(solution)/shard_map/ppermute | solution.py:39
  70.8 1.2 %collective-permute-start.9 = (f32[256,512]{1,0:T(8,128)S(1)}, f32[256,512]{1,0:T(8,128)S(1)}, u32[]{:S(2)}, u32[]{:S(2)}) collective-permute-start(f32[256,512]{1,0:T(8,128)S(1)} %slice.15), channel_id=1, source_target_pairs={{3,0},{0,1},{1,2},{2,3},{7,4},{4,5},{5,6},{6,7},{11,8},{8,9},{9,10... | collective-permute-start | bytes 1572872 | tf_op jit(solution)/shard_map/ppermute | solution.py:39
  72.0 1.6 %collective-permute-start.8 = (f32[256,512]{1,0:T(8,128)S(1)}, f32[256,512]{1,0:T(8,128)S(1)}, u32[]{:S(2)}, u32[]{:S(2)}) collective-permute-start(f32[256,512]{1,0:T(8,128)S(1)} %slice.14), channel_id=1, source_target_pairs={{1,0},{2,1},{3,2},{0,3},{5,4},{6,5},{7,6},{4,7},{9,8},{10,9},{11,1... | collective-permute-start | bytes 1572872 | tf_op jit(solution)/shard_map/ppermute | solution.py:39
  74.5 1.3 %gather.11 = (bf16[4,256,1024]{2,1,0:T(8,128)(2,1)S(1)}, bf16[4,256,1024]{2,1,0:T(8,128)(2,1)S(1)}) custom-call(s32[32,128]{1,0:T(8,128)S(1)} %broadcast_select_fusion.ids_ref, f32[512,512]{1,0:T(8,128)S(1)} %collective-permute-done.6.refs_0_, f32[512,512]{1,0:T(8,128)S(1)} %collective-permute-done.11.refs_1_, ...), custom_call_target="tpu_custom_call" | custom-call | flops 3000000000 | bytes 2097152 | tf_op jit(solution)/shard_map/gather/pallas_call | solution.py:136
  75.8 3.6 %collect.2.x_ref = f32[2,1024,512]{2,1,0:T(8,128)S(1)} custom-call(bf16[4,4,1024,256]{3,2,1,0:T(8,128)(2,1)S(1)} %get-tuple-element.45.count_ref, bf16[4,256,1024]{2,1,0:T(8,128)(2,1)S(1)} %gather.10.refs_0_.rows0, bf16[4,256,1024]{2,1,0:T(8,128)(2,1)S(1)} %get-tuple-element.52.refs_1_.rows1, bf16[4,256,1024]{2,1,0:T(8,128)(2,1)S(1)} %get-tuple-element.53.refs_2_.rows3), custom_call_target="tpu_custom_call" | custom-call | flops 3300000000 | bytes 3145728 | tf_op jit(solution)/shard_map/collect/pallas_call | solution.py:173
  79.5 1.0 collective-permute-done.9.refs_1_
  80.4 1.4 %collective-permute-start.13 = (f32[256,512]{1,0:T(8,128)S(1)}, f32[256,512]{1,0:T(8,128)S(1)}, u32[]{:S(2)}, u32[]{:S(2)}) collective-permute-start(f32[256,512]{1,0:T(8,128)S(1)} %collective-permute-done.8.refs_0_), channel_id=1, source_target_pairs={{16,0},{17,1},{18,2},{19,3},{20,4},{21,5},{22,6},{23,7},{24,8},{25... | collective-permute-start | bytes 1572872 | tf_op jit(solution)/shard_map/ppermute | solution.py:39
  81.8 3.6 %collect.3.x_ref = f32[2,1024,512]{2,1,0:T(8,128)S(1)} custom-call(bf16[4,4,1024,256]{3,2,1,0:T(8,128)(2,1)S(1)} %get-tuple-element.45.count_ref, bf16[4,256,1024]{2,1,0:T(8,128)(2,1)S(1)} %gather.10.refs_0_.rows0, bf16[4,256,1024]{2,1,0:T(8,128)(2,1)S(1)} %get-tuple-element.52.refs_1_.rows1, bf16[4,256,1024]{2,1,0:T(8,128)(2,1)S(1)} %get-tuple-element.53.refs_2_.rows3), custom_call_target="tpu_custom_call" | custom-call | flops 3300000000 | bytes 3145728 | tf_op jit(solution)/shard_map/collect/pallas_call | solution.py:173
  86.2 1.4 %copy-done.2 = bf16[8,512,512]{2,1,0:T(8,128)(2,1)S(1)} copy-done((bf16[8,512,512]{2,1,0:T(8,128)(2,1)S(1)}, bf16[8,512,512]{2,1,0:T(8,128)(2,1)}, u32[]{:S(2)}) %copy-start.2) | copy-done | bytes 4194328
  87.6 5.5 %finish.5 = (f32[128,512]{1,0:T(8,128)S(1)}, f32[128,512]{1,0:T(8,128)S(1)}) custom-call(s32[4]{0:T(128)S(1)} %get-tuple-element.44.flag_ref, f32[2,1024,512]{2,1,0:T(8,128)S(1)} %collect.2.x_ref, bf16[4,256,1024]{2,1,0:T(8,128)(2,1)S(1)} %gather.10.refs_0_.rows0, bf16[4,256,1024]{2,1,0:T(8,128)(2,1)S(1)} %get-tuple-element.52.refs_1_.rows1, ...), custom_call_target="tpu_custom_call" | custom-call | flops 6000000000 | bytes 2097152 | tf_op jit(solution)/shard_map/finish/pallas_call | solution.py:228
  93.1 1.1 %collective-permute-start.16 = (f32[128,512]{1,0:T(8,128)S(1)}, f32[128,512]{1,0:T(8,128)S(1)}, u32[]{:S(2)}, u32[]{:S(2)}) collective-permute-start(f32[128,512]{1,0:T(8,128)S(1)} %get-tuple-element.59), channel_id=1, source_target_pairs={{64,0},{65,1},{66,2},{67,3},{68,4},{69,5},{70,6},{71,7},{72,8},{73... | collective-permute-start | bytes 786440 | tf_op jit(solution)/shard_map/ppermute | solution.py:39
  94.8 3.3 %finish.4 = f32[128,512]{1,0:T(8,128)S(1)} custom-call(s32[4]{0:T(128)S(1)} %get-tuple-element.44.flag_ref, f32[2,1024,512]{2,1,0:T(8,128)S(1)} %collect.3.x_ref, bf16[4,256,1024]{2,1,0:T(8,128)(2,1)S(1)} %gather.10.refs_0_.rows0, bf16[4,256,1024]{2,1,0:T(8,128)(2,1)S(1)} %get-tuple-element.52.refs_1_.rows1, bf16[4,256,1024]{2,1,0:T(8,128)(2,1)S(1)} %gather.12.rows2, ...), custom_call_target="tpu_custom_call" | custom-call | flops 3000000000 | bytes 2097152 | tf_op jit(solution)/shard_map/finish/pallas_call | solution.py:228
  98.1 2.2 %collective-permute-start.15 = (f32[128,512]{1,0:T(8,128)S(1)}, f32[128,512]{1,0:T(8,128)S(1)}, u32[]{:S(2)}, u32[]{:S(2)}) collective-permute-start(f32[128,512]{1,0:T(8,128)S(1)} %finish.4), channel_id=1, source_target_pairs={{32,0},{33,1},{34,2},{35,3},{36,4},{37,5},{38,6},{39,7},{40,8},{41... | collective-permute-start | bytes 786440 | tf_op jit(solution)/shard_map/ppermute | solution.py:39
  100.3 3.1 %finish.3 = f32[128,512]{1,0:T(8,128)S(1)} custom-call(s32[4]{0:T(128)S(1)} %get-tuple-element.44.flag_ref, f32[2,1024,512]{2,1,0:T(8,128)S(1)} %collect.3.x_ref, bf16[4,256,1024]{2,1,0:T(8,128)(2,1)S(1)} %gather.10.refs_0_.rows0, bf16[4,256,1024]{2,1,0:T(8,128)(2,1)S(1)} %get-tuple-element.52.refs_1_.rows1, bf16[4,256,1024]{2,1,0:T(8,128)(2,1)S(1)} %gather.12.rows2, ...), custom_call_target="tpu_custom_call" | custom-call | flops 3000000000 | bytes 2097152 | tf_op jit(solution)/shard_map/finish/pallas_call | solution.py:228
  103.3 5.2 %collective-permute-done.17 = f32[128,512]{1,0:T(8,128)S(1)} collective-permute-done((f32[128,512]{1,0:T(8,128)S(1)}, f32[128,512]{1,0:T(8,128)S(1)}, u32[]{:S(2)}, u32[]{:S(2)}) %collective-permute-start.17) | collective-permute-done | bytes 262176 | tf_op jit(solution)/shard_map/ppermute | solution.py:39
  (58 shorter events, 10.1 us)
Async XLA Ops:
  0.0 18.4 %copy-start = (s32[128,1024]{1,0:T(8,128)S(1)}, s32[128,1024]{1,0:T(8,128)}, u32[]{:S(2)}) copy-start(s32[128,1024]{1,0:T(8,128)} %param.7) | copy-start | bytes 1572868
  0.0 11.5 %copy-start.6 = (s32[1,8192]{1,0:T(1,128)S(1)}, s32[1,8192]{1,0:T(1,128)}, u32[]{:S(2)}) copy-start(s32[1,8192]{1,0:T(1,128)} %param.10) | copy-start | bytes 98308
  0.0 11.5 %copy-start.7 = (s32[1,8192]{1,0:T(1,128)S(1)}, s32[1,8192]{1,0:T(1,128)}, u32[]{:S(2)}) copy-start(s32[1,8192]{1,0:T(1,128)} %param.9) | copy-start | bytes 98308
  0.0 41.3 %all-to-all-start = ((f32[128,8,512]{2,1,0:T(8,128)}), f32[128,8,512]{2,1,0:T(8,128)S(1)}, u32[]{:S(2)}, u32[]{:S(2)}) async-start(f32[128,8,512]{2,1,0:T(8,128)} %bitcast.14), calls=%async_computation | async-start | bytes 4194304 | tf_op jit(solution)/shard_map/all_to_all | solution.py:269
  11.6 23.1 %collective-permute-start.5 = (s32[2,8192]{1,0:T(2,128)S(1)}, s32[2,8192]{1,0:T(2,128)S(1)}, u32[]{:S(2)}, u32[]{:S(2)}) collective-permute-start(s32[2,8192]{1,0:T(2,128)S(1)} %get-tuple-element.69), channel_id=1, source_target_pairs={{96,0},{97,1},{98,2},{99,3},{100,4},{101,5},{102,6},{103,7},{104,8... | collective-permute-start | bytes 196616 | tf_op jit(solution)/shard_map/ppermute | solution.py:39
  13.2 21.5 %collective-permute-start.4 = (s32[2,8192]{1,0:T(2,128)S(1)}, s32[2,8192]{1,0:T(2,128)S(1)}, u32[]{:S(2)}, u32[]{:S(2)}) collective-permute-start(s32[2,8192]{1,0:T(2,128)S(1)} %get-tuple-element.69), channel_id=1, source_target_pairs={{32,0},{33,1},{34,2},{35,3},{36,4},{37,5},{38,6},{39,7},{40,8},{41... | collective-permute-start | bytes 196616 | tf_op jit(solution)/shard_map/ppermute | solution.py:39
  15.0 24.1 %collective-permute-start.3 = (s32[2,8192]{1,0:T(2,128)S(1)}, s32[2,8192]{1,0:T(2,128)S(1)}, u32[]{:S(2)}, u32[]{:S(2)}) collective-permute-start(s32[2,8192]{1,0:T(2,128)S(1)} %get-tuple-element.69), channel_id=1, source_target_pairs={{64,0},{65,1},{66,2},{67,3},{68,4},{69,5},{70,6},{71,7},{72,8},{73... | collective-permute-start | bytes 196616 | tf_op jit(solution)/shard_map/ppermute | solution.py:39
  18.5 3.4 %copy-start.5 = (f32[8,512,512]{2,1,0:T(8,128)S(1)}, f32[8,512,512]{2,1,0:T(8,128)}, u32[]{:S(2)}) copy-start(f32[8,512,512]{2,1,0:T(8,128)} %k_ref.1) | copy-start | bytes 25165828
  24.7 2.0 %copy-start.1 = (bf16[8,512,512]{2,1,0:T(8,128)(2,1)}, bf16[8,512,512]{2,1,0:T(8,128)(2,1)S(1)}, u32[]{:S(2)}) copy-start(bf16[8,512,512]{2,1,0:T(8,128)(2,1)S(1)} %get-tuple-element.56.kh_ref) | copy-start | bytes 12582916
  26.7 2.0 %copy-start.3 = (bf16[8,512,512]{2,1,0:T(8,128)(2,1)}, bf16[8,512,512]{2,1,0:T(8,128)(2,1)S(1)}, u32[]{:S(2)}) copy-start(bf16[8,512,512]{2,1,0:T(8,128)(2,1)S(1)} %get-tuple-element.57.kl_ref) | copy-start | bytes 12582916
  42.2 6.8 %collective-permute-start.2 = (f32[128,512]{1,0:T(8,128)S(1)}, f32[128,512]{1,0:T(8,128)S(1)}, u32[]{:S(2)}, u32[]{:S(2)}) collective-permute-start(f32[128,512]{1,0:T(8,128)S(1)} %fusion), channel_id=1, source_target_pairs={{12,0},{13,1},{14,2},{15,3},{0,4},{1,5},{2,6},{3,7},{4,8},{5,9},{6... | collective-permute-start | bytes 786440 | tf_op jit(solution)/shard_map/ppermute | solution.py:39
  42.8 9.4 %collective-permute-start.1 = (f32[128,512]{1,0:T(8,128)S(1)}, f32[128,512]{1,0:T(8,128)S(1)}, u32[]{:S(2)}, u32[]{:S(2)}) collective-permute-start(f32[128,512]{1,0:T(8,128)S(1)} %fusion), channel_id=1, source_target_pairs={{8,0},{9,1},{10,2},{11,3},{12,4},{13,5},{14,6},{15,7},{0,8},{1,9},... | collective-permute-start | bytes 786440 | tf_op jit(solution)/shard_map/ppermute | solution.py:39
  45.3 7.1 %collective-permute-start = (f32[128,512]{1,0:T(8,128)S(1)}, f32[128,512]{1,0:T(8,128)S(1)}, u32[]{:S(2)}, u32[]{:S(2)}) collective-permute-start(f32[128,512]{1,0:T(8,128)S(1)} %fusion), channel_id=1, source_target_pairs={{4,0},{5,1},{6,2},{7,3},{8,4},{9,5},{10,6},{11,7},{12,8},{13,9},{1... | collective-permute-start | bytes 786440 | tf_op jit(solution)/shard_map/ppermute | solution.py:39
  52.5 16.8 %collective-permute-start.7 = (f32[512,512]{1,0:T(8,128)S(1)}, f32[512,512]{1,0:T(8,128)S(1)}, u32[]{:S(2)}, u32[]{:S(2)}) collective-permute-start(f32[512,512]{1,0:T(8,128)S(1)} %constant_dynamic-update-slice_fusion.refs_0_), channel_id=1, source_target_pairs={{3,0},{0,1},{1,2},{2,3},{7,4},{4,5},{5,6},{6,7},{11,8},{8,9},{9,10... | collective-permute-start | bytes 3145736 | tf_op jit(solution)/shard_map/ppermute | solution.py:39
  53.1 16.3 %collective-permute-start.6 = (f32[512,512]{1,0:T(8,128)S(1)}, f32[512,512]{1,0:T(8,128)S(1)}, u32[]{:S(2)}, u32[]{:S(2)}) collective-permute-start(f32[512,512]{1,0:T(8,128)S(1)} %constant_dynamic-update-slice_fusion.refs_0_), channel_id=1, source_target_pairs={{1,0},{2,1},{3,2},{0,3},{5,4},{6,5},{7,6},{4,7},{9,8},{10,9},{11,1... | collective-permute-start | bytes 3145736 | tf_op jit(solution)/shard_map/ppermute | solution.py:39
  55.3 18.3 %collective-permute-start.10 = (f32[512,512]{1,0:T(8,128)S(1)}, f32[512,512]{1,0:T(8,128)S(1)}, u32[]{:S(2)}, u32[]{:S(2)}) collective-permute-start(f32[512,512]{1,0:T(8,128)S(1)} %constant_dynamic-update-slice_fusion.refs_0_), channel_id=1, source_target_pairs={{16,0},{17,1},{18,2},{19,3},{20,4},{21,5},{22,6},{23,7},{24,8},{25... | collective-permute-start | bytes 3145736 | tf_op jit(solution)/shard_map/ppermute | solution.py:39
  69.3 5.0 %collective-permute-start.11 = (f32[512,512]{1,0:T(8,128)S(1)}, f32[512,512]{1,0:T(8,128)S(1)}, u32[]{:S(2)}, u32[]{:S(2)}) collective-permute-start(f32[512,512]{1,0:T(8,128)S(1)} %collective-permute-done.6.refs_0_), channel_id=1, source_target_pairs={{16,0},{17,1},{18,2},{19,3},{20,4},{21,5},{22,6},{23,7},{24,8},{25... | collective-permute-start | bytes 3145736 | tf_op jit(solution)/shard_map/ppermute | solution.py:39
  70.7 3.8 %collective-permute-start.12 = (f32[512,512]{1,0:T(8,128)S(1)}, f32[512,512]{1,0:T(8,128)S(1)}, u32[]{:S(2)}, u32[]{:S(2)}) collective-permute-start(f32[512,512]{1,0:T(8,128)S(1)} %collective-permute-done.7.refs_2_), channel_id=1, source_target_pairs={{16,0},{17,1},{18,2},{19,3},{20,4},{21,5},{22,6},{23,7},{24,8},{25... | collective-permute-start | bytes 3145736 | tf_op jit(solution)/shard_map/ppermute | solution.py:39
  70.8 9.6 %collective-permute-start.9 = (f32[256,512]{1,0:T(8,128)S(1)}, f32[256,512]{1,0:T(8,128)S(1)}, u32[]{:S(2)}, u32[]{:S(2)}) collective-permute-start(f32[256,512]{1,0:T(8,128)S(1)} %slice.15), channel_id=1, source_target_pairs={{3,0},{0,1},{1,2},{2,3},{7,4},{4,5},{5,6},{6,7},{11,8},{8,9},{9,10... | collective-permute-start | bytes 1572872 | tf_op jit(solution)/shard_map/ppermute | solution.py:39
  72.0 8.4 %collective-permute-start.8 = (f32[256,512]{1,0:T(8,128)S(1)}, f32[256,512]{1,0:T(8,128)S(1)}, u32[]{:S(2)}, u32[]{:S(2)}) collective-permute-start(f32[256,512]{1,0:T(8,128)S(1)} %slice.14), channel_id=1, source_target_pairs={{1,0},{2,1},{3,2},{0,3},{5,4},{6,5},{7,6},{4,7},{9,8},{10,9},{11,1... | collective-permute-start | bytes 1572872 | tf_op jit(solution)/shard_map/ppermute | solution.py:39
  80.4 5.0 %collective-permute-start.13 = (f32[256,512]{1,0:T(8,128)S(1)}, f32[256,512]{1,0:T(8,128)S(1)}, u32[]{:S(2)}, u32[]{:S(2)}) collective-permute-start(f32[256,512]{1,0:T(8,128)S(1)} %collective-permute-done.8.refs_0_), channel_id=1, source_target_pairs={{16,0},{17,1},{18,2},{19,3},{20,4},{21,5},{22,6},{23,7},{24,8},{25... | collective-permute-start | bytes 1572872 | tf_op jit(solution)/shard_map/ppermute | solution.py:39
  81.8 3.7 %collective-permute-start.14 = (f32[256,512]{1,0:T(8,128)S(1)}, f32[256,512]{1,0:T(8,128)S(1)}, u32[]{:S(2)}, u32[]{:S(2)}) collective-permute-start(f32[256,512]{1,0:T(8,128)S(1)} %collective-permute-done.9.refs_1_), channel_id=1, source_target_pairs={{16,0},{17,1},{18,2},{19,3},{20,4},{21,5},{22,6},{23,7},{24,8},{25... | collective-permute-start | bytes 1572872 | tf_op jit(solution)/shard_map/ppermute | solution.py:39
  81.8 4.4 %copy-start.4 = (bf16[8,512,512]{2,1,0:T(8,128)(2,1)S(1)}, bf16[8,512,512]{2,1,0:T(8,128)(2,1)}, u32[]{:S(2)}) copy-start(bf16[8,512,512]{2,1,0:T(8,128)(2,1)} %copy-done.3) | copy-start | bytes 12582916
  85.4 2.2 %copy-start.2 = (bf16[8,512,512]{2,1,0:T(8,128)(2,1)S(1)}, bf16[8,512,512]{2,1,0:T(8,128)(2,1)}, u32[]{:S(2)}) copy-start(bf16[8,512,512]{2,1,0:T(8,128)(2,1)} %copy-done.1) | copy-start | bytes 12582916
  93.1 10.2 %collective-permute-start.16 = (f32[128,512]{1,0:T(8,128)S(1)}, f32[128,512]{1,0:T(8,128)S(1)}, u32[]{:S(2)}, u32[]{:S(2)}) collective-permute-start(f32[128,512]{1,0:T(8,128)S(1)} %get-tuple-element.59), channel_id=1, source_target_pairs={{64,0},{65,1},{66,2},{67,3},{68,4},{69,5},{70,6},{71,7},{72,8},{73... | collective-permute-start | bytes 786440 | tf_op jit(solution)/shard_map/ppermute | solution.py:39
  94.2 14.3 %collective-permute-start.17 = (f32[128,512]{1,0:T(8,128)S(1)}, f32[128,512]{1,0:T(8,128)S(1)}, u32[]{:S(2)}, u32[]{:S(2)}) collective-permute-start(f32[128,512]{1,0:T(8,128)S(1)} %get-tuple-element.60), channel_id=1, source_target_pairs={{96,0},{97,1},{98,2},{99,3},{100,4},{101,5},{102,6},{103,7},{104,8... | collective-permute-start | bytes 786440 | tf_op jit(solution)/shard_map/ppermute | solution.py:39
  98.1 10.5 %collective-permute-start.15 = (f32[128,512]{1,0:T(8,128)S(1)}, f32[128,512]{1,0:T(8,128)S(1)}, u32[]{:S(2)}, u32[]{:S(2)}) collective-permute-start(f32[128,512]{1,0:T(8,128)S(1)} %finish.4), channel_id=1, source_target_pairs={{32,0},{33,1},{34,2},{35,3},{36,4},{37,5},{38,6},{39,7},{40,8},{41... | collective-permute-start | bytes 786440 | tf_op jit(solution)/shard_map/ppermute | solution.py:39

commit v8 on v7

--- a/solution.py
+++ b/solution.py
@@ -21,7 +21,7 @@
 SMEM = pl.BlockSpec(memory_space=pltpu.SMEM)
 VMEM = pl.BlockSpec(memory_space=pltpu.VMEM)
 PAIR = 2
-ORDER = (2, 1, 3, 0)
+ORDER = (2, 0, 1, 3)
 
 
 def device_of(x, y, z, c):
@@ -156,7 +156,7 @@
 
 
 def collect_kernel(blocks, first, count_ref, *refs):
-    rows, out_ref = refs[:-1], refs[-1]
+    rows, out_ref = refs[: len(blocks)], refs[-1]
 
     @pl.loop(0, PAIR)
     def _(k):
@@ -168,11 +168,11 @@
             )
 
 
-def collect(blocks, first, counts, rows):
+def collect(blocks, first, counts, rows, kernels):
     n = len(blocks)
     return pl.pallas_call(
         functools.partial(collect_kernel, blocks, first),
-        in_specs=[VMEM] * (1 + n),
+        in_specs=[VMEM] * (1 + n + len(kernels)),
         out_specs=VMEM,
         out_shape=jax.ShapeDtypeStruct((PAIR, DIRS * OCT, WIDTH), F32),
         compiler_params=pltpu.CompilerParams(vmem_limit_bytes=8 << 20),
@@ -180,7 +180,7 @@
             flops=n * 1_100_000_000, bytes_accessed=n << 20, transcendentals=0
         ),
         name="collect",
-    )(counts, *rows)
+    )(counts, *rows, *kernels)
 
 
 def finish_kernel(
@@ -320,18 +320,18 @@
     (rows0,) = gather((0,), ids, [line, across(line)])
     rows1, rows3 = gather((1, 3), ids, [near1, across(near1), near3, across(near3)])
     rows = (rows0, rows1, rows3)
-    x = [collect((0, 1, 3), 0, counts, rows), None]
+    x = [collect((0, 1, 3), 0, counts, rows, []), None]
     low, high, x[0], rows = lax.optimization_barrier((low, high, x[0], rows))
     far = [low, high, across(low), across(high)]
-    x[1] = collect((0, 1, 3), PAIR, counts, rows)
+    x[1] = collect((0, 1, 3), PAIR, counts, rows, kernels)
     (rows2,) = gather((2,), ids, far)
     last = (rows[:2] + (rows2,) + rows[2:], counts, kernels, codes)
-    out2, out1 = finish(0, 2, flags, x[0], *last)
-    ring2, ring1 = along_z(out2, -2), along_z(out1, -1)
-    (out3,) = finish(2, 1, flags, x[1], *last)
-    ring3 = along_z(out3, -3)
-    (out0,) = finish(3, 1, flags, x[1], *last)
-    return out0 + ring3 + ring2 + ring1
+    (out2,) = finish(0, 1, flags, x[0], *last)
+    ring2 = along_z(out2, -2)
+    out1, out3 = finish(2, 2, flags, x[1], *last)
+    ring1, ring3 = along_z(out1, -1), along_z(out3, -3)
+    (out0,) = finish(1, 1, flags, x[0], *last)
+    return out0 + ring2 + ring1 + ring3
 
 
 def solution(mesh):

time: 110 us -> 106 us (0.964)
  waiting for transfers between devices: 23.6 us -> 20.8 us
  local copies, waits for them, and re-layouts: 11.7 us -> 10.3 us
    all_to_all x1, waiting for transfers between devices: 2.15 us -> 0.07 us  [body(): lax.all_to_all(partials, AXES, split_axis=0, concat_axis=0, tiled=True)]
    unnamed x19, local copies, waits for them, and re-layouts: 8.82 us -> 7.42 us
  transfers between devices with their start and end apart: 19 -> 19, of which waited for: 9 -> 9; matrix products, arithmetic and copies ran while one was open for 3% -> 4% of each run, Pallas kernels for 27% -> 31%
where the time goes in v8:
time: 106 us; the launch traced here: 105 us
  Pallas kernels  36 us (34%)
  starting transfers between devices  35.2 us (33%)
  waiting for transfers between devices  20.8 us (20%)
  local copies, waits for them, and re-layouts  10.3 us (10%)
  other arithmetic  1.72 us (2%)
    ppermute x18, starting transfers between devices, fetch(): return lax.ppermute(value, AXES, pairs)  23.7 us
    ppermute x18, waiting for transfers between devices, fetch(): return lax.ppermute(value, AXES, pairs)  20.8 us
    pallas_call x3, Pallas kernels, finish(): pl.pallas_call(functools.partial(finish_kernel, first), in_specs=[SMEM] +...  11.8 us
    all_to_all x1, starting transfers between devices, body(): lax.all_to_all(partials, AXES, split_axis=0, concat_axis=0, tiled=True)  11.5 us
    pallas_call x1, Pallas kernels, count(): pl.pallas_call(count_kernel, grid=(RING,), in_specs=[codes, codes], out_s...  11.4 us
    unnamed x19, local copies, waits for them, and re-layouts  7.42 us
    pallas_call x2, Pallas kernels, collect(): pl.pallas_call(functools.partial(collect_kernel, blocks, first), in_specs...  7.26 us
    pallas_call x3, Pallas kernels, gather(): pl.pallas_call(functools.partial(gather_kernel, blocks), in_specs=[VMEM]...  2.81 us
  transfers between devices with their start and end apart: 19, of which 9 were waited for; matrix products, arithmetic and copies ran while one was open for 4% of the time, Pallas kernels for 31%

profile of v8, /device:TPU:1, one launch (start us, length us, event | category | flops | bytes accessed | tf_op | source)
XLA Modules:
  0.0 105.2 jit_solution(17129878152767451504)
XLA Ops:
  0.0 11.5 %all-to-all-start = ((f32[128,8,512]{2,1,0:T(8,128)}), f32[128,8,512]{2,1,0:T(8,128)S(1)}, u32[]{:S(2)}, u32[]{:S(2)}) async-start(f32[128,8,512]{2,1,0:T(8,128)} %bitcast.14), calls=%async_computation | async-start | bytes 4194304 | tf_op jit(solution)/shard_map/all_to_all | solution.py:269
  11.6 3.3 %collective-permute-start.4 = (s32[2,8192]{1,0:T(2,128)S(1)}, s32[2,8192]{1,0:T(2,128)S(1)}, u32[]{:S(2)}, u32[]{:S(2)}) collective-permute-start(s32[2,8192]{1,0:T(2,128)S(1)} %get-tuple-element.70), channel_id=1, source_target_pairs={{32,0},{33,1},{34,2},{35,3},{36,4},{37,5},{38,6},{39,7},{40,8},{41... | collective-permute-start | bytes 196616 | tf_op jit(solution)/shard_map/ppermute | solution.py:39
  14.9 1.5 %collective-permute-start.3 = (s32[2,8192]{1,0:T(2,128)S(1)}, s32[2,8192]{1,0:T(2,128)S(1)}, u32[]{:S(2)}, u32[]{:S(2)}) collective-permute-start(s32[2,8192]{1,0:T(2,128)S(1)} %get-tuple-element.70), channel_id=1, source_target_pairs={{64,0},{65,1},{66,2},{67,3},{68,4},{69,5},{70,6},{71,7},{72,8},{73... | collective-permute-start | bytes 196616 | tf_op jit(solution)/shard_map/ppermute | solution.py:39
  16.4 0.9 fusion.49
  18.5 3.4 %copy-done.5 = f32[8,512,512]{2,1,0:T(8,128)S(1)} copy-done((f32[8,512,512]{2,1,0:T(8,128)S(1)}, f32[8,512,512]{2,1,0:T(8,128)}, u32[]{:S(2)}) %copy-start.5) | copy-done | bytes 8388632
  21.9 2.8 %turn.1 = (bf16[8,512,512]{2,1,0:T(8,128)(2,1)S(1)}, bf16[8,512,512]{2,1,0:T(8,128)(2,1)S(1)}) custom-call(f32[8,512,512]{2,1,0:T(8,128)S(1)} %copy-done.5), custom_call_target="tpu_custom_call" | custom-call | flops 100000000 | bytes 1048576 | tf_op jit(solution)/shard_map/turn/pallas_call | solution.py:248
  24.7 1.9 %copy-done.1 = bf16[8,512,512]{2,1,0:T(8,128)(2,1)} copy-done((bf16[8,512,512]{2,1,0:T(8,128)(2,1)}, bf16[8,512,512]{2,1,0:T(8,128)(2,1)S(1)}, u32[]{:S(2)}) %copy-start.1) | copy-done | bytes 4194328
  26.7 2.0 %copy-done.3 = bf16[8,512,512]{2,1,0:T(8,128)(2,1)} copy-done((bf16[8,512,512]{2,1,0:T(8,128)(2,1)}, bf16[8,512,512]{2,1,0:T(8,128)(2,1)S(1)}, u32[]{:S(2)}) %copy-start.3) | copy-done | bytes 4194328
  28.7 1.0 collective-permute-done.4
  29.7 11.5 %collective-permute-done.5 = s32[2,8192]{1,0:T(2,128)S(1)} collective-permute-done((s32[2,8192]{1,0:T(2,128)S(1)}, s32[2,8192]{1,0:T(2,128)S(1)}, u32[]{:S(2)}, u32[]{:S(2)}) %collective-permute-start.5) | collective-permute-done | bytes 65568 | tf_op jit(solution)/shard_map/ppermute | solution.py:39
  41.3 0.9 fusion
  42.8 2.5 %collective-permute-start.1 = (f32[128,512]{1,0:T(8,128)S(1)}, f32[128,512]{1,0:T(8,128)S(1)}, u32[]{:S(2)}, u32[]{:S(2)}) collective-permute-start(f32[128,512]{1,0:T(8,128)S(1)} %fusion), channel_id=1, source_target_pairs={{8,0},{9,1},{10,2},{11,3},{12,4},{13,5},{14,6},{15,7},{0,8},{1,9},... | collective-permute-start | bytes 786440 | tf_op jit(solution)/shard_map/ppermute | solution.py:39
  45.3 0.9 collective-permute-start
  47.8 1.2 %collective-permute-done.2 = f32[128,512]{1,0:T(8,128)S(1)} collective-permute-done((f32[128,512]{1,0:T(8,128)S(1)}, f32[128,512]{1,0:T(8,128)S(1)}, u32[]{:S(2)}, u32[]{:S(2)}) %collective-permute-start.2) | collective-permute-done | bytes 262176 | tf_op jit(solution)/shard_map/ppermute | solution.py:39
  49.0 3.2 %collective-permute-done.1 = f32[128,512]{1,0:T(8,128)S(1)} collective-permute-done((f32[128,512]{1,0:T(8,128)S(1)}, f32[128,512]{1,0:T(8,128)S(1)}, u32[]{:S(2)}, u32[]{:S(2)}) %collective-permute-start.1) | collective-permute-done | bytes 262176 | tf_op jit(solution)/shard_map/ppermute | solution.py:39
  53.1 2.1 %collective-permute-start.6 = (f32[512,512]{1,0:T(8,128)S(1)}, f32[512,512]{1,0:T(8,128)S(1)}, u32[]{:S(2)}, u32[]{:S(2)}) collective-permute-start(f32[512,512]{1,0:T(8,128)S(1)} %constant_dynamic-update-slice_fusion.refs_0_), channel_id=1, source_target_pairs={{1,0},{2,1},{3,2},{0,3},{5,4},{6,5},{7,6},{4,7},{9,8},{10,9},{11,1... | collective-permute-start | bytes 3145736 | tf_op jit(solution)/shard_map/ppermute | solution.py:39
  55.3 2.7 %collective-permute-start.10 = (f32[512,512]{1,0:T(8,128)S(1)}, f32[512,512]{1,0:T(8,128)S(1)}, u32[]{:S(2)}, u32[]{:S(2)}) collective-permute-start(f32[512,512]{1,0:T(8,128)S(1)} %constant_dynamic-update-slice_fusion.refs_0_), channel_id=1, source_target_pairs={{16,0},{17,1},{18,2},{19,3},{20,4},{21,5},{22,6},{23,7},{24,8},{25... | collective-permute-start | bytes 3145736 | tf_op jit(solution)/shard_map/ppermute | solution.py:39
  58.0 11.4 %count.1 = (bf16[4,4,1024,256]{3,2,1,0:T(8,128)(2,1)S(1)}, s32[4]{0:T(128)S(1)}) custom-call(s32[32,1024]{1,0:T(8,128)S(1)} %get-tuple-element.40.row_ref, s32[32,1024]{1,0:T(8,128)S(1)} %get-tuple-element.41.col_ref), custom_call_target="tpu_custom_call" | custom-call | flops 100000000 | bytes 1048576 | tf_op jit(solution)/shard_map/count/pallas_call | solution.py:90
  69.3 1.4 %collective-permute-start.11 = (f32[512,512]{1,0:T(8,128)S(1)}, f32[512,512]{1,0:T(8,128)S(1)}, u32[]{:S(2)}, u32[]{:S(2)}) collective-permute-start(f32[512,512]{1,0:T(8,128)S(1)} %collective-permute-done.6.refs_0_), channel_id=1, source_target_pairs={{16,0},{17,1},{18,2},{19,3},{20,4},{21,5},{22,6},{23,7},{24,8},{25... | collective-permute-start | bytes 3145736 | tf_op jit(solution)/shard_map/ppermute | solution.py:39
  70.8 1.2 %collective-permute-start.9 = (f32[256,512]{1,0:T(8,128)S(1)}, f32[256,512]{1,0:T(8,128)S(1)}, u32[]{:S(2)}, u32[]{:S(2)}) collective-permute-start(f32[256,512]{1,0:T(8,128)S(1)} %slice.15), channel_id=1, source_target_pairs={{3,0},{0,1},{1,2},{2,3},{7,4},{4,5},{5,6},{6,7},{11,8},{8,9},{9,10... | collective-permute-start | bytes 1572872 | tf_op jit(solution)/shard_map/ppermute | solution.py:39
  72.0 1.6 %collective-permute-start.8 = (f32[256,512]{1,0:T(8,128)S(1)}, f32[256,512]{1,0:T(8,128)S(1)}, u32[]{:S(2)}, u32[]{:S(2)}) collective-permute-start(f32[256,512]{1,0:T(8,128)S(1)} %slice.14), channel_id=1, source_target_pairs={{1,0},{2,1},{3,2},{0,3},{5,4},{6,5},{7,6},{4,7},{9,8},{10,9},{11,1... | collective-permute-start | bytes 1572872 | tf_op jit(solution)/shard_map/ppermute | solution.py:39
  74.5 1.3 %gather.11 = (bf16[4,256,1024]{2,1,0:T(8,128)(2,1)S(1)}, bf16[4,256,1024]{2,1,0:T(8,128)(2,1)S(1)}) custom-call(s32[32,128]{1,0:T(8,128)S(1)} %broadcast_select_fusion.ids_ref, f32[512,512]{1,0:T(8,128)S(1)} %collective-permute-done.6.refs_0_, f32[512,512]{1,0:T(8,128)S(1)} %collective-permute-done.11.refs_1_, ...), custom_call_target="tpu_custom_call" | custom-call | flops 3000000000 | bytes 2097152 | tf_op jit(solution)/shard_map/gather/pallas_call | solution.py:136
  75.9 3.6 %collect.2.x_ref = f32[2,1024,512]{2,1,0:T(8,128)S(1)} custom-call(bf16[4,4,1024,256]{3,2,1,0:T(8,128)(2,1)S(1)} %get-tuple-element.47.count_ref, bf16[4,256,1024]{2,1,0:T(8,128)(2,1)S(1)} %gather.10.refs_0_.rows0, bf16[4,256,1024]{2,1,0:T(8,128)(2,1)S(1)} %get-tuple-element.53.refs_1_.rows1, bf16[4,256,1024]{2,1,0:T(8,128)(2,1)S(1)} %get-tuple-element.56.refs_2_.rows3), custom_call_target="tpu_custom_call" | custom-call | flops 3300000000 | bytes 3145728 | tf_op jit(solution)/shard_map/collect/pallas_call | solution.py:173
  79.5 0.9 collective-permute-done.9.refs_1_
  80.4 1.4 %collective-permute-start.13 = (f32[256,512]{1,0:T(8,128)S(1)}, f32[256,512]{1,0:T(8,128)S(1)}, u32[]{:S(2)}, u32[]{:S(2)}) collective-permute-start(f32[256,512]{1,0:T(8,128)S(1)} %collective-permute-done.8.refs_0_), channel_id=1, source_target_pairs={{16,0},{17,1},{18,2},{19,3},{20,4},{21,5},{22,6},{23,7},{24,8},{25... | collective-permute-start | bytes 1572872 | tf_op jit(solution)/shard_map/ppermute | solution.py:39
  81.8 3.6 %collect.3.x_ref = f32[2,1024,512]{2,1,0:T(8,128)S(1)} custom-call(bf16[4,4,1024,256]{3,2,1,0:T(8,128)(2,1)S(1)} %get-tuple-element.47.count_ref, bf16[4,256,1024]{2,1,0:T(8,128)(2,1)S(1)} %gather.10.refs_0_.rows0, bf16[4,256,1024]{2,1,0:T(8,128)(2,1)S(1)} %get-tuple-element.53.refs_1_.rows1, bf16[4,256,1024]{2,1,0:T(8,128)(2,1)S(1)} %get-tuple-element.56.refs_2_.rows3, ...), custom_call_target="tpu_custom_call" | custom-call | flops 3300000000 | bytes 3145728 | tf_op jit(solution)/shard_map/collect/pallas_call | solution.py:173
  86.2 3.1 %finish.4 = f32[128,512]{1,0:T(8,128)S(1)} custom-call(s32[4]{0:T(128)S(1)} %get-tuple-element.44.flag_ref, f32[2,1024,512]{2,1,0:T(8,128)S(1)} %collect.2.x_ref, bf16[4,256,1024]{2,1,0:T(8,128)(2,1)S(1)} %gather.10.refs_0_.rows0, bf16[4,256,1024]{2,1,0:T(8,128)(2,1)S(1)} %get-tuple-element.53.refs_1_.rows1, bf16[4,256,1024]{2,1,0:T(8,128)(2,1)S(1)} %gather.12.rows2, ...), custom_call_target="tpu_custom_call" | custom-call | flops 3000000000 | bytes 2097152 | tf_op jit(solution)/shard_map/finish/pallas_call | solution.py:228
  89.3 1.1 %collective-permute-start.15 = (f32[128,512]{1,0:T(8,128)S(1)}, f32[128,512]{1,0:T(8,128)S(1)}, u32[]{:S(2)}, u32[]{:S(2)}) collective-permute-start(f32[128,512]{1,0:T(8,128)S(1)} %finish.4), channel_id=1, source_target_pairs={{64,0},{65,1},{66,2},{67,3},{68,4},{69,5},{70,6},{71,7},{72,8},{73... | collective-permute-start | bytes 786440 | tf_op jit(solution)/shard_map/ppermute | solution.py:39
  90.4 5.7 %finish.5 = (f32[128,512]{1,0:T(8,128)S(1)}, f32[128,512]{1,0:T(8,128)S(1)}) custom-call(s32[4]{0:T(128)S(1)} %get-tuple-element.44.flag_ref, f32[2,1024,512]{2,1,0:T(8,128)S(1)} %collect.3.x_ref, bf16[4,256,1024]{2,1,0:T(8,128)(2,1)S(1)} %gather.10.refs_0_.rows0, bf16[4,256,1024]{2,1,0:T(8,128)(2,1)S(1)} %get-tuple-element.53.refs_1_.rows1, ...), custom_call_target="tpu_custom_call" | custom-call | flops 6000000000 | bytes 2097152 | tf_op jit(solution)/shard_map/finish/pallas_call | solution.py:228
  96.7 2.1 %collective-permute-start.17 = (f32[128,512]{1,0:T(8,128)S(1)}, f32[128,512]{1,0:T(8,128)S(1)}, u32[]{:S(2)}, u32[]{:S(2)}) collective-permute-start(f32[128,512]{1,0:T(8,128)S(1)} %get-tuple-element.60), channel_id=1, source_target_pairs={{32,0},{33,1},{34,2},{35,3},{36,4},{37,5},{38,6},{39,7},{40,8},{41... | collective-permute-start | bytes 786440 | tf_op jit(solution)/shard_map/ppermute | solution.py:39
  98.9 3.1 %finish.3 = f32[128,512]{1,0:T(8,128)S(1)} custom-call(s32[4]{0:T(128)S(1)} %get-tuple-element.44.flag_ref, f32[2,1024,512]{2,1,0:T(8,128)S(1)} %collect.2.x_ref, bf16[4,256,1024]{2,1,0:T(8,128)(2,1)S(1)} %gather.10.refs_0_.rows0, bf16[4,256,1024]{2,1,0:T(8,128)(2,1)S(1)} %get-tuple-element.53.refs_1_.rows1, bf16[4,256,1024]{2,1,0:T(8,128)(2,1)S(1)} %gather.12.rows2, ...), custom_call_target="tpu_custom_call" | custom-call | flops 3000000000 | bytes 2097152 | tf_op jit(solution)/shard_map/finish/pallas_call | solution.py:228
  101.9 2.5 %collective-permute-done.16 = f32[128,512]{1,0:T(8,128)S(1)} collective-permute-done((f32[128,512]{1,0:T(8,128)S(1)}, f32[128,512]{1,0:T(8,128)S(1)}, u32[]{:S(2)}, u32[]{:S(2)}) %collective-permute-start.16) | collective-permute-done | bytes 262176 | tf_op jit(solution)/shard_map/ppermute | solution.py:39
  (58 shorter events, 7.6 us)
Async XLA Ops:
  0.0 18.4 %copy-start = (s32[128,1024]{1,0:T(8,128)S(1)}, s32[128,1024]{1,0:T(8,128)}, u32[]{:S(2)}) copy-start(s32[128,1024]{1,0:T(8,128)} %param.7) | copy-start | bytes 1572868
  0.0 11.5 %copy-start.6 = (s32[1,8192]{1,0:T(1,128)S(1)}, s32[1,8192]{1,0:T(1,128)}, u32[]{:S(2)}) copy-start(s32[1,8192]{1,0:T(1,128)} %param.10) | copy-start | bytes 98308
  0.0 11.5 %copy-start.7 = (s32[1,8192]{1,0:T(1,128)S(1)}, s32[1,8192]{1,0:T(1,128)}, u32[]{:S(2)}) copy-start(s32[1,8192]{1,0:T(1,128)} %param.9) | copy-start | bytes 98308
  0.0 41.3 %all-to-all-start = ((f32[128,8,512]{2,1,0:T(8,128)}), f32[128,8,512]{2,1,0:T(8,128)S(1)}, u32[]{:S(2)}, u32[]{:S(2)}) async-start(f32[128,8,512]{2,1,0:T(8,128)} %bitcast.14), calls=%async_computation | async-start | bytes 4194304 | tf_op jit(solution)/shard_map/all_to_all | solution.py:269
  11.6 18.1 %collective-permute-start.4 = (s32[2,8192]{1,0:T(2,128)S(1)}, s32[2,8192]{1,0:T(2,128)S(1)}, u32[]{:S(2)}, u32[]{:S(2)}) collective-permute-start(s32[2,8192]{1,0:T(2,128)S(1)} %get-tuple-element.70), channel_id=1, source_target_pairs={{32,0},{33,1},{34,2},{35,3},{36,4},{37,5},{38,6},{39,7},{40,8},{41... | collective-permute-start | bytes 196616 | tf_op jit(solution)/shard_map/ppermute | solution.py:39
  14.9 26.2 %collective-permute-start.5 = (s32[2,8192]{1,0:T(2,128)S(1)}, s32[2,8192]{1,0:T(2,128)S(1)}, u32[]{:S(2)}, u32[]{:S(2)}) collective-permute-start(s32[2,8192]{1,0:T(2,128)S(1)} %get-tuple-element.70), channel_id=1, source_target_pairs={{96,0},{97,1},{98,2},{99,3},{100,4},{101,5},{102,6},{103,7},{104,8... | collective-permute-start | bytes 196616 | tf_op jit(solution)/shard_map/ppermute | solution.py:39
  14.9 26.2 %collective-permute-start.3 = (s32[2,8192]{1,0:T(2,128)S(1)}, s32[2,8192]{1,0:T(2,128)S(1)}, u32[]{:S(2)}, u32[]{:S(2)}) collective-permute-start(s32[2,8192]{1,0:T(2,128)S(1)} %get-tuple-element.70), channel_id=1, source_target_pairs={{64,0},{65,1},{66,2},{67,3},{68,4},{69,5},{70,6},{71,7},{72,8},{73... | collective-permute-start | bytes 196616 | tf_op jit(solution)/shard_map/ppermute | solution.py:39
  18.5 3.4 %copy-start.5 = (f32[8,512,512]{2,1,0:T(8,128)S(1)}, f32[8,512,512]{2,1,0:T(8,128)}, u32[]{:S(2)}) copy-start(f32[8,512,512]{2,1,0:T(8,128)} %k_ref.1) | copy-start | bytes 25165828
  24.7 2.0 %copy-start.1 = (bf16[8,512,512]{2,1,0:T(8,128)(2,1)}, bf16[8,512,512]{2,1,0:T(8,128)(2,1)S(1)}, u32[]{:S(2)}) copy-start(bf16[8,512,512]{2,1,0:T(8,128)(2,1)S(1)} %get-tuple-element.57.kh_ref.refs_3_) | copy-start | bytes 12582916
  26.7 2.0 %copy-start.3 = (bf16[8,512,512]{2,1,0:T(8,128)(2,1)}, bf16[8,512,512]{2,1,0:T(8,128)(2,1)S(1)}, u32[]{:S(2)}) copy-start(bf16[8,512,512]{2,1,0:T(8,128)(2,1)S(1)} %get-tuple-element.58.kl_ref.refs_4_) | copy-start | bytes 12582916
  42.2 6.8 %collective-permute-start.2 = (f32[128,512]{1,0:T(8,128)S(1)}, f32[128,512]{1,0:T(8,128)S(1)}, u32[]{:S(2)}, u32[]{:S(2)}) collective-permute-start(f32[128,512]{1,0:T(8,128)S(1)} %fusion), channel_id=1, source_target_pairs={{12,0},{13,1},{14,2},{15,3},{0,4},{1,5},{2,6},{3,7},{4,8},{5,9},{6... | collective-permute-start | bytes 786440 | tf_op jit(solution)/shard_map/ppermute | solution.py:39
  42.8 9.4 %collective-permute-start.1 = (f32[128,512]{1,0:T(8,128)S(1)}, f32[128,512]{1,0:T(8,128)S(1)}, u32[]{:S(2)}, u32[]{:S(2)}) collective-permute-start(f32[128,512]{1,0:T(8,128)S(1)} %fusion), channel_id=1, source_target_pairs={{8,0},{9,1},{10,2},{11,3},{12,4},{13,5},{14,6},{15,7},{0,8},{1,9},... | collective-permute-start | bytes 786440 | tf_op jit(solution)/shard_map/ppermute | solution.py:39
  45.3 7.1 %collective-permute-start = (f32[128,512]{1,0:T(8,128)S(1)}, f32[128,512]{1,0:T(8,128)S(1)}, u32[]{:S(2)}, u32[]{:S(2)}) collective-permute-start(f32[128,512]{1,0:T(8,128)S(1)} %fusion), channel_id=1, source_target_pairs={{4,0},{5,1},{6,2},{7,3},{8,4},{9,5},{10,6},{11,7},{12,8},{13,9},{1... | collective-permute-start | bytes 786440 | tf_op jit(solution)/shard_map/ppermute | solution.py:39
  52.5 16.8 %collective-permute-start.7 = (f32[512,512]{1,0:T(8,128)S(1)}, f32[512,512]{1,0:T(8,128)S(1)}, u32[]{:S(2)}, u32[]{:S(2)}) collective-permute-start(f32[512,512]{1,0:T(8,128)S(1)} %constant_dynamic-update-slice_fusion.refs_0_), channel_id=1, source_target_pairs={{3,0},{0,1},{1,2},{2,3},{7,4},{4,5},{5,6},{6,7},{11,8},{8,9},{9,10... | collective-permute-start | bytes 3145736 | tf_op jit(solution)/shard_map/ppermute | solution.py:39
  53.1 16.2 %collective-permute-start.6 = (f32[512,512]{1,0:T(8,128)S(1)}, f32[512,512]{1,0:T(8,128)S(1)}, u32[]{:S(2)}, u32[]{:S(2)}) collective-permute-start(f32[512,512]{1,0:T(8,128)S(1)} %constant_dynamic-update-slice_fusion.refs_0_), channel_id=1, source_target_pairs={{1,0},{2,1},{3,2},{0,3},{5,4},{6,5},{7,6},{4,7},{9,8},{10,9},{11,1... | collective-permute-start | bytes 3145736 | tf_op jit(solution)/shard_map/ppermute | solution.py:39
  55.3 18.3 %collective-permute-start.10 = (f32[512,512]{1,0:T(8,128)S(1)}, f32[512,512]{1,0:T(8,128)S(1)}, u32[]{:S(2)}, u32[]{:S(2)}) collective-permute-start(f32[512,512]{1,0:T(8,128)S(1)} %constant_dynamic-update-slice_fusion.refs_0_), channel_id=1, source_target_pairs={{16,0},{17,1},{18,2},{19,3},{20,4},{21,5},{22,6},{23,7},{24,8},{25... | collective-permute-start | bytes 3145736 | tf_op jit(solution)/shard_map/ppermute | solution.py:39
  69.3 5.0 %collective-permute-start.11 = (f32[512,512]{1,0:T(8,128)S(1)}, f32[512,512]{1,0:T(8,128)S(1)}, u32[]{:S(2)}, u32[]{:S(2)}) collective-permute-start(f32[512,512]{1,0:T(8,128)S(1)} %collective-permute-done.6.refs_0_), channel_id=1, source_target_pairs={{16,0},{17,1},{18,2},{19,3},{20,4},{21,5},{22,6},{23,7},{24,8},{25... | collective-permute-start | bytes 3145736 | tf_op jit(solution)/shard_map/ppermute | solution.py:39
  70.7 3.8 %collective-permute-start.12 = (f32[512,512]{1,0:T(8,128)S(1)}, f32[512,512]{1,0:T(8,128)S(1)}, u32[]{:S(2)}, u32[]{:S(2)}) collective-permute-start(f32[512,512]{1,0:T(8,128)S(1)} %collective-permute-done.7.refs_2_), channel_id=1, source_target_pairs={{16,0},{17,1},{18,2},{19,3},{20,4},{21,5},{22,6},{23,7},{24,8},{25... | collective-permute-start | bytes 3145736 | tf_op jit(solution)/shard_map/ppermute | solution.py:39
  70.8 9.6 %collective-permute-start.9 = (f32[256,512]{1,0:T(8,128)S(1)}, f32[256,512]{1,0:T(8,128)S(1)}, u32[]{:S(2)}, u32[]{:S(2)}) collective-permute-start(f32[256,512]{1,0:T(8,128)S(1)} %slice.15), channel_id=1, source_target_pairs={{3,0},{0,1},{1,2},{2,3},{7,4},{4,5},{5,6},{6,7},{11,8},{8,9},{9,10... | collective-permute-start | bytes 1572872 | tf_op jit(solution)/shard_map/ppermute | solution.py:39
  72.0 8.4 %collective-permute-start.8 = (f32[256,512]{1,0:T(8,128)S(1)}, f32[256,512]{1,0:T(8,128)S(1)}, u32[]{:S(2)}, u32[]{:S(2)}) collective-permute-start(f32[256,512]{1,0:T(8,128)S(1)} %slice.14), channel_id=1, source_target_pairs={{1,0},{2,1},{3,2},{0,3},{5,4},{6,5},{7,6},{4,7},{9,8},{10,9},{11,1... | collective-permute-start | bytes 1572872 | tf_op jit(solution)/shard_map/ppermute | solution.py:39
  75.8 6.0 %copy-start.2 = (bf16[8,512,512]{2,1,0:T(8,128)(2,1)S(1)}, bf16[8,512,512]{2,1,0:T(8,128)(2,1)}, u32[]{:S(2)}) copy-start(bf16[8,512,512]{2,1,0:T(8,128)(2,1)} %copy-done.1) | copy-start | bytes 12582916
  75.9 6.0 %copy-start.4 = (bf16[8,512,512]{2,1,0:T(8,128)(2,1)S(1)}, bf16[8,512,512]{2,1,0:T(8,128)(2,1)}, u32[]{:S(2)}) copy-start(bf16[8,512,512]{2,1,0:T(8,128)(2,1)} %copy-done.3) | copy-start | bytes 12582916
  80.4 5.0 %collective-permute-start.13 = (f32[256,512]{1,0:T(8,128)S(1)}, f32[256,512]{1,0:T(8,128)S(1)}, u32[]{:S(2)}, u32[]{:S(2)}) collective-permute-start(f32[256,512]{1,0:T(8,128)S(1)} %collective-permute-done.8.refs_0_), channel_id=1, source_target_pairs={{16,0},{17,1},{18,2},{19,3},{20,4},{21,5},{22,6},{23,7},{24,8},{25... | collective-permute-start | bytes 1572872 | tf_op jit(solution)/shard_map/ppermute | solution.py:39
  81.8 3.7 %collective-permute-start.14 = (f32[256,512]{1,0:T(8,128)S(1)}, f32[256,512]{1,0:T(8,128)S(1)}, u32[]{:S(2)}, u32[]{:S(2)}) collective-permute-start(f32[256,512]{1,0:T(8,128)S(1)} %collective-permute-done.9.refs_1_), channel_id=1, source_target_pairs={{16,0},{17,1},{18,2},{19,3},{20,4},{21,5},{22,6},{23,7},{24,8},{25... | collective-permute-start | bytes 1572872 | tf_op jit(solution)/shard_map/ppermute | solution.py:39
  89.3 12.6 %collective-permute-start.15 = (f32[128,512]{1,0:T(8,128)S(1)}, f32[128,512]{1,0:T(8,128)S(1)}, u32[]{:S(2)}, u32[]{:S(2)}) collective-permute-start(f32[128,512]{1,0:T(8,128)S(1)} %finish.4), channel_id=1, source_target_pairs={{64,0},{65,1},{66,2},{67,3},{68,4},{69,5},{70,6},{71,7},{72,8},{73... | collective-permute-start | bytes 786440 | tf_op jit(solution)/shard_map/ppermute | solution.py:39
  96.1 8.3 %collective-permute-start.16 = (f32[128,512]{1,0:T(8,128)S(1)}, f32[128,512]{1,0:T(8,128)S(1)}, u32[]{:S(2)}, u32[]{:S(2)}) collective-permute-start(f32[128,512]{1,0:T(8,128)S(1)} %get-tuple-element.59), channel_id=1, source_target_pairs={{96,0},{97,1},{98,2},{99,3},{100,4},{101,5},{102,6},{103,7},{104,8... | collective-permute-start | bytes 786440 | tf_op jit(solution)/shard_map/ppermute | solution.py:39
  96.7 7.7 %collective-permute-start.17 = (f32[128,512]{1,0:T(8,128)S(1)}, f32[128,512]{1,0:T(8,128)S(1)}, u32[]{:S(2)}, u32[]{:S(2)}) collective-permute-start(f32[128,512]{1,0:T(8,128)S(1)} %get-tuple-element.60), channel_id=1, source_target_pairs={{32,0},{33,1},{34,2},{35,3},{36,4},{37,5},{38,6},{39,7},{40,8},{41... | collective-permute-start | bytes 786440 | tf_op jit(solution)/shard_map/ppermute | solution.py:39

commit v9 on v8

--- a/solution.py
+++ b/solution.py
@@ -317,8 +317,8 @@
     counts, flags = count(*codes)
     near1, near3, counts, flags = lax.optimization_barrier((near1, near3, counts, flags))
     low, high = along_s(near1[: 2 * OCT], 1), along_s(near3[2 * OCT :], 3)
-    (rows0,) = gather((0,), ids, [line, across(line)])
-    rows1, rows3 = gather((1, 3), ids, [near1, across(near1), near3, across(near3)])
+    near = [line, across(line), near1, across(near1), near3, across(near3)]
+    rows0, rows1, rows3 = gather((0, 1, 3), ids, near)
     rows = (rows0, rows1, rows3)
     x = [collect((0, 1, 3), 0, counts, rows, []), None]
     low, high, x[0], rows = lax.optimization_barrier((low, high, x[0], rows))

time: 106 us -> 106 us (level)
    pallas_call x3 -> x2, Pallas kernels: 2.81 us -> 2.62 us  [gather(): pl.pallas_call(functools.partial(gather_kernel, blocks), in_specs=[VMEM]...]
  transfers between devices with their start and end apart: 19 -> 19, of which waited for: 9 -> 9; matrix products, arithmetic and copies ran while one was open for 4% -> 4% of each run, Pallas kernels for 31% -> 30%
where the time goes in v9:
time: 106 us; the launch traced here: 105 us
  Pallas kernels  35.8 us (34%)
  starting transfers between devices  35.2 us (33%)
  waiting for transfers between devices  21.1 us (20%)
  local copies, waits for them, and re-layouts  10.3 us (10%)
  other arithmetic  1.72 us (2%)
    ppermute x18, starting transfers between devices, fetch(): return lax.ppermute(value, AXES, pairs)  23.7 us
    ppermute x18, waiting for transfers between devices, fetch(): return lax.ppermute(value, AXES, pairs)  21 us
    pallas_call x3, Pallas kernels, finish(): pl.pallas_call(functools.partial(finish_kernel, first), in_specs=[SMEM] +...  11.8 us
    all_to_all x1, starting transfers between devices, body(): lax.all_to_all(partials, AXES, split_axis=0, concat_axis=0, tiled=True)  11.5 us
    pallas_call x1, Pallas kernels, count(): pl.pallas_call(count_kernel, grid=(RING,), in_specs=[codes, codes], out_s...  11.4 us
    unnamed x19, local copies, waits for them, and re-layouts  7.42 us
    pallas_call x2, Pallas kernels, collect(): pl.pallas_call(functools.partial(collect_kernel, blocks, first), in_specs...  7.26 us
    pallas_call x1, Pallas kernels, turn(): pl.pallas_call(turn_kernel, grid=(DIRS,), in_specs=[spec], out_specs=[spe...  2.78 us
  transfers between devices with their start and end apart: 19, of which 9 were waited for; matrix products, arithmetic and copies ran while one was open for 4% of the time, Pallas kernels for 30%

profile of v9, /device:TPU:1, one launch (start us, length us, event | category | flops | bytes accessed | tf_op | source)
XLA Modules:
  0.0 105.3 jit_solution(11929234159965178510)
XLA Ops:
  0.0 11.5 %all-to-all-start = ((f32[128,8,512]{2,1,0:T(8,128)}), f32[128,8,512]{2,1,0:T(8,128)S(1)}, u32[]{:S(2)}, u32[]{:S(2)}) async-start(f32[128,8,512]{2,1,0:T(8,128)} %bitcast.14), calls=%async_computation | async-start | bytes 4194304 | tf_op jit(solution)/shard_map/all_to_all | solution.py:269
  11.6 3.3 %collective-permute-start.4 = (s32[2,8192]{1,0:T(2,128)S(1)}, s32[2,8192]{1,0:T(2,128)S(1)}, u32[]{:S(2)}, u32[]{:S(2)}) collective-permute-start(s32[2,8192]{1,0:T(2,128)S(1)} %get-tuple-element.72), channel_id=1, source_target_pairs={{32,0},{33,1},{34,2},{35,3},{36,4},{37,5},{38,6},{39,7},{40,8},{41... | collective-permute-start | bytes 196616 | tf_op jit(solution)/shard_map/ppermute | solution.py:39
  14.9 1.5 %collective-permute-start.3 = (s32[2,8192]{1,0:T(2,128)S(1)}, s32[2,8192]{1,0:T(2,128)S(1)}, u32[]{:S(2)}, u32[]{:S(2)}) collective-permute-start(s32[2,8192]{1,0:T(2,128)S(1)} %get-tuple-element.72), channel_id=1, source_target_pairs={{64,0},{65,1},{66,2},{67,3},{68,4},{69,5},{70,6},{71,7},{72,8},{73... | collective-permute-start | bytes 196616 | tf_op jit(solution)/shard_map/ppermute | solution.py:39
  16.4 0.9 fusion.49
  18.5 3.4 %copy-done.5 = f32[8,512,512]{2,1,0:T(8,128)S(1)} copy-done((f32[8,512,512]{2,1,0:T(8,128)S(1)}, f32[8,512,512]{2,1,0:T(8,128)}, u32[]{:S(2)}) %copy-start.5) | copy-done | bytes 8388632
  21.9 2.8 %turn.1 = (bf16[8,512,512]{2,1,0:T(8,128)(2,1)S(1)}, bf16[8,512,512]{2,1,0:T(8,128)(2,1)S(1)}) custom-call(f32[8,512,512]{2,1,0:T(8,128)S(1)} %copy-done.5), custom_call_target="tpu_custom_call" | custom-call | flops 100000000 | bytes 1048576 | tf_op jit(solution)/shard_map/turn/pallas_call | solution.py:248
  24.7 1.9 %copy-done.1 = bf16[8,512,512]{2,1,0:T(8,128)(2,1)} copy-done((bf16[8,512,512]{2,1,0:T(8,128)(2,1)}, bf16[8,512,512]{2,1,0:T(8,128)(2,1)S(1)}, u32[]{:S(2)}) %copy-start.1) | copy-done | bytes 4194328
  26.7 2.0 %copy-done.3 = bf16[8,512,512]{2,1,0:T(8,128)(2,1)} copy-done((bf16[8,512,512]{2,1,0:T(8,128)(2,1)}, bf16[8,512,512]{2,1,0:T(8,128)(2,1)S(1)}, u32[]{:S(2)}) %copy-start.3) | copy-done | bytes 4194328
  28.7 1.0 collective-permute-done.4
  29.7 11.5 %collective-permute-done.5 = s32[2,8192]{1,0:T(2,128)S(1)} collective-permute-done((s32[2,8192]{1,0:T(2,128)S(1)}, s32[2,8192]{1,0:T(2,128)S(1)}, u32[]{:S(2)}, u32[]{:S(2)}) %collective-permute-start.5) | collective-permute-done | bytes 65568 | tf_op jit(solution)/shard_map/ppermute | solution.py:39
  41.3 0.9 fusion
  42.8 2.5 %collective-permute-start.1 = (f32[128,512]{1,0:T(8,128)S(1)}, f32[128,512]{1,0:T(8,128)S(1)}, u32[]{:S(2)}, u32[]{:S(2)}) collective-permute-start(f32[128,512]{1,0:T(8,128)S(1)} %fusion), channel_id=1, source_target_pairs={{8,0},{9,1},{10,2},{11,3},{12,4},{13,5},{14,6},{15,7},{0,8},{1,9},... | collective-permute-start | bytes 786440 | tf_op jit(solution)/shard_map/ppermute | solution.py:39
  45.3 0.9 collective-permute-start
  47.8 1.2 %collective-permute-done.2 = f32[128,512]{1,0:T(8,128)S(1)} collective-permute-done((f32[128,512]{1,0:T(8,128)S(1)}, f32[128,512]{1,0:T(8,128)S(1)}, u32[]{:S(2)}, u32[]{:S(2)}) %collective-permute-start.2) | collective-permute-done | bytes 262176 | tf_op jit(solution)/shard_map/ppermute | solution.py:39
  49.0 3.2 %collective-permute-done.1 = f32[128,512]{1,0:T(8,128)S(1)} collective-permute-done((f32[128,512]{1,0:T(8,128)S(1)}, f32[128,512]{1,0:T(8,128)S(1)}, u32[]{:S(2)}, u32[]{:S(2)}) %collective-permute-start.1) | collective-permute-done | bytes 262176 | tf_op jit(solution)/shard_map/ppermute | solution.py:39
  53.1 2.1 %collective-permute-start.6 = (f32[512,512]{1,0:T(8,128)S(1)}, f32[512,512]{1,0:T(8,128)S(1)}, u32[]{:S(2)}, u32[]{:S(2)}) collective-permute-start(f32[512,512]{1,0:T(8,128)S(1)} %constant_dynamic-update-slice_fusion.refs_0_), channel_id=1, source_target_pairs={{1,0},{2,1},{3,2},{0,3},{5,4},{6,5},{7,6},{4,7},{9,8},{10,9},{11,1... | collective-permute-start | bytes 3145736 | tf_op jit(solution)/shard_map/ppermute | solution.py:39
  55.3 2.7 %collective-permute-start.10 = (f32[512,512]{1,0:T(8,128)S(1)}, f32[512,512]{1,0:T(8,128)S(1)}, u32[]{:S(2)}, u32[]{:S(2)}) collective-permute-start(f32[512,512]{1,0:T(8,128)S(1)} %constant_dynamic-update-slice_fusion.refs_0_), channel_id=1, source_target_pairs={{16,0},{17,1},{18,2},{19,3},{20,4},{21,5},{22,6},{23,7},{24,8},{25... | collective-permute-start | bytes 3145736 | tf_op jit(solution)/shard_map/ppermute | solution.py:39
  58.0 11.4 %count.1 = (bf16[4,4,1024,256]{3,2,1,0:T(8,128)(2,1)S(1)}, s32[4]{0:T(128)S(1)}) custom-call(s32[32,1024]{1,0:T(8,128)S(1)} %get-tuple-element.41.row_ref, s32[32,1024]{1,0:T(8,128)S(1)} %get-tuple-element.42.col_ref), custom_call_target="tpu_custom_call" | custom-call | flops 100000000 | bytes 1048576 | tf_op jit(solution)/shard_map/count/pallas_call | solution.py:90
  69.3 1.4 %collective-permute-start.11 = (f32[512,512]{1,0:T(8,128)S(1)}, f32[512,512]{1,0:T(8,128)S(1)}, u32[]{:S(2)}, u32[]{:S(2)}) collective-permute-start(f32[512,512]{1,0:T(8,128)S(1)} %collective-permute-done.6.refs_2_), channel_id=1, source_target_pairs={{16,0},{17,1},{18,2},{19,3},{20,4},{21,5},{22,6},{23,7},{24,8},{25... | collective-permute-start | bytes 3145736 | tf_op jit(solution)/shard_map/ppermute | solution.py:39
  70.8 1.2 %collective-permute-start.9 = (f32[256,512]{1,0:T(8,128)S(1)}, f32[256,512]{1,0:T(8,128)S(1)}, u32[]{:S(2)}, u32[]{:S(2)}) collective-permute-start(f32[256,512]{1,0:T(8,128)S(1)} %slice.15), channel_id=1, source_target_pairs={{3,0},{0,1},{1,2},{2,3},{7,4},{4,5},{5,6},{6,7},{11,8},{8,9},{9,10... | collective-permute-start | bytes 1572872 | tf_op jit(solution)/shard_map/ppermute | solution.py:39
  72.0 1.6 %collective-permute-start.8 = (f32[256,512]{1,0:T(8,128)S(1)}, f32[256,512]{1,0:T(8,128)S(1)}, u32[]{:S(2)}, u32[]{:S(2)}) collective-permute-start(f32[256,512]{1,0:T(8,128)S(1)} %slice.14), channel_id=1, source_target_pairs={{1,0},{2,1},{3,2},{0,3},{5,4},{6,5},{7,6},{4,7},{9,8},{10,9},{11,1... | collective-permute-start | bytes 1572872 | tf_op jit(solution)/shard_map/ppermute | solution.py:39
  73.6 0.9 collective-permute-done.12.refs_5_
  74.5 1.9 %gather.9 = (bf16[4,256,1024]{2,1,0:T(8,128)(2,1)S(1)}, bf16[4,256,1024]{2,1,0:T(8,128)(2,1)S(1)}, bf16[4,256,1024]{2,1,0:T(8,128)(2,1)S(1)}) custom-call(s32[32,128]{1,0:T(8,128)S(1)} %broadcast_select_fusion.ids_ref, f32[512,512]{1,0:T(8,128)S(1)} %constant_dynamic-update-slice_fusion.refs_0_, f32[512,512]{1,0:T(8,128)S(1)} %collective-permute-done.10.refs_1_, ...), custom_call_target="tpu_custom_call" | custom-call | flops 4499999744 | bytes 3145728 | tf_op jit(solution)/shard_map/gather/pallas_call | solution.py:136
  76.4 3.6 %collect.2.x_ref = f32[2,1024,512]{2,1,0:T(8,128)S(1)} custom-call(bf16[4,4,1024,256]{3,2,1,0:T(8,128)(2,1)S(1)} %get-tuple-element.48.count_ref, bf16[4,256,1024]{2,1,0:T(8,128)(2,1)S(1)} %get-tuple-element.54.refs_0_.rows0, bf16[4,256,1024]{2,1,0:T(8,128)(2,1)S(1)} %get-tuple-element.55.refs_1_.rows1, bf16[4,256,1024]{2,1,0:T(8,128)(2,1)S(1)} %get-tuple-element.58.refs_2_.rows3), custom_call_target="tpu_custom_call" | custom-call | flops 3300000000 | bytes 3145728 | tf_op jit(solution)/shard_map/collect/pallas_call | solution.py:173
  80.4 1.4 %collective-permute-start.13 = (f32[256,512]{1,0:T(8,128)S(1)}, f32[256,512]{1,0:T(8,128)S(1)}, u32[]{:S(2)}, u32[]{:S(2)}) collective-permute-start(f32[256,512]{1,0:T(8,128)S(1)} %collective-permute-done.8.refs_0_), channel_id=1, source_target_pairs={{16,0},{17,1},{18,2},{19,3},{20,4},{21,5},{22,6},{23,7},{24,8},{25... | collective-permute-start | bytes 1572872 | tf_op jit(solution)/shard_map/ppermute | solution.py:39
  81.8 3.6 %collect.3.x_ref = f32[2,1024,512]{2,1,0:T(8,128)S(1)} custom-call(bf16[4,4,1024,256]{3,2,1,0:T(8,128)(2,1)S(1)} %get-tuple-element.48.count_ref, bf16[4,256,1024]{2,1,0:T(8,128)(2,1)S(1)} %get-tuple-element.54.refs_0_.rows0, bf16[4,256,1024]{2,1,0:T(8,128)(2,1)S(1)} %get-tuple-element.55.refs_1_.rows1, ...), custom_call_target="tpu_custom_call" | custom-call | flops 3300000000 | bytes 3145728 | tf_op jit(solution)/shard_map/collect/pallas_call | solution.py:173
  86.2 3.1 %finish.4 = f32[128,512]{1,0:T(8,128)S(1)} custom-call(s32[4]{0:T(128)S(1)} %get-tuple-element.45.flag_ref, f32[2,1024,512]{2,1,0:T(8,128)S(1)} %collect.2.x_ref, bf16[4,256,1024]{2,1,0:T(8,128)(2,1)S(1)} %get-tuple-element.54.refs_0_.rows0, bf16[4,256,1024]{2,1,0:T(8,128)(2,1)S(1)} %get-tuple-element.55.refs_1_.rows1, ...), custom_call_target="tpu_custom_call" | custom-call | flops 3000000000 | bytes 2097152 | tf_op jit(solution)/shard_map/finish/pallas_call | solution.py:228
  89.3 1.1 %collective-permute-start.15 = (f32[128,512]{1,0:T(8,128)S(1)}, f32[128,512]{1,0:T(8,128)S(1)}, u32[]{:S(2)}, u32[]{:S(2)}) collective-permute-start(f32[128,512]{1,0:T(8,128)S(1)} %finish.4), channel_id=1, source_target_pairs={{64,0},{65,1},{66,2},{67,3},{68,4},{69,5},{70,6},{71,7},{72,8},{73... | collective-permute-start | bytes 786440 | tf_op jit(solution)/shard_map/ppermute | solution.py:39
  90.4 5.7 %finish.5 = (f32[128,512]{1,0:T(8,128)S(1)}, f32[128,512]{1,0:T(8,128)S(1)}) custom-call(s32[4]{0:T(128)S(1)} %get-tuple-element.45.flag_ref, f32[2,1024,512]{2,1,0:T(8,128)S(1)} %collect.3.x_ref, bf16[4,256,1024]{2,1,0:T(8,128)(2,1)S(1)} %get-tuple-element.54.refs_0_.rows0, bf16[4,256,1024]{2,1,0:T(8,128)(2,1)S(1)} %get-tuple-element.55.refs_1_.rows1, ...), custom_call_target="tpu_custom_call" | custom-call | flops 6000000000 | bytes 2097152 | tf_op jit(solution)/shard_map/finish/pallas_call | solution.py:228
  96.7 2.1 %collective-permute-start.17 = (f32[128,512]{1,0:T(8,128)S(1)}, f32[128,512]{1,0:T(8,128)S(1)}, u32[]{:S(2)}, u32[]{:S(2)}) collective-permute-start(f32[128,512]{1,0:T(8,128)S(1)} %get-tuple-element.62), channel_id=1, source_target_pairs={{32,0},{33,1},{34,2},{35,3},{36,4},{37,5},{38,6},{39,7},{40,8},{41... | collective-permute-start | bytes 786440 | tf_op jit(solution)/shard_map/ppermute | solution.py:39
  98.9 3.1 %finish.3 = f32[128,512]{1,0:T(8,128)S(1)} custom-call(s32[4]{0:T(128)S(1)} %get-tuple-element.45.flag_ref, f32[2,1024,512]{2,1,0:T(8,128)S(1)} %collect.2.x_ref, bf16[4,256,1024]{2,1,0:T(8,128)(2,1)S(1)} %get-tuple-element.54.refs_0_.rows0, bf16[4,256,1024]{2,1,0:T(8,128)(2,1)S(1)} %get-tuple-element.55.refs_1_.rows1, ...), custom_call_target="tpu_custom_call" | custom-call | flops 3000000000 | bytes 2097152 | tf_op jit(solution)/shard_map/finish/pallas_call | solution.py:228
  102.0 2.5 %collective-permute-done.16 = f32[128,512]{1,0:T(8,128)S(1)} collective-permute-done((f32[128,512]{1,0:T(8,128)S(1)}, f32[128,512]{1,0:T(8,128)S(1)}, u32[]{:S(2)}, u32[]{:S(2)}) %collective-permute-start.16) | collective-permute-done | bytes 262176 | tf_op jit(solution)/shard_map/ppermute | solution.py:39
  (57 shorter events, 7.0 us)
Async XLA Ops:
  0.0 18.4 %copy-start = (s32[128,1024]{1,0:T(8,128)S(1)}, s32[128,1024]{1,0:T(8,128)}, u32[]{:S(2)}) copy-start(s32[128,1024]{1,0:T(8,128)} %param.7) | copy-start | bytes 1572868
  0.0 11.5 %copy-start.6 = (s32[1,8192]{1,0:T(1,128)S(1)}, s32[1,8192]{1,0:T(1,128)}, u32[]{:S(2)}) copy-start(s32[1,8192]{1,0:T(1,128)} %param.10) | copy-start | bytes 98308
  0.0 11.5 %copy-start.7 = (s32[1,8192]{1,0:T(1,128)S(1)}, s32[1,8192]{1,0:T(1,128)}, u32[]{:S(2)}) copy-start(s32[1,8192]{1,0:T(1,128)} %param.9) | copy-start | bytes 98308
  0.0 41.3 %all-to-all-start = ((f32[128,8,512]{2,1,0:T(8,128)}), f32[128,8,512]{2,1,0:T(8,128)S(1)}, u32[]{:S(2)}, u32[]{:S(2)}) async-start(f32[128,8,512]{2,1,0:T(8,128)} %bitcast.14), calls=%async_computation | async-start | bytes 4194304 | tf_op jit(solution)/shard_map/all_to_all | solution.py:269
  11.6 18.1 %collective-permute-start.4 = (s32[2,8192]{1,0:T(2,128)S(1)}, s32[2,8192]{1,0:T(2,128)S(1)}, u32[]{:S(2)}, u32[]{:S(2)}) collective-permute-start(s32[2,8192]{1,0:T(2,128)S(1)} %get-tuple-element.72), channel_id=1, source_target_pairs={{32,0},{33,1},{34,2},{35,3},{36,4},{37,5},{38,6},{39,7},{40,8},{41... | collective-permute-start | bytes 196616 | tf_op jit(solution)/shard_map/ppermute | solution.py:39
  14.9 26.2 %collective-permute-start.5 = (s32[2,8192]{1,0:T(2,128)S(1)}, s32[2,8192]{1,0:T(2,128)S(1)}, u32[]{:S(2)}, u32[]{:S(2)}) collective-permute-start(s32[2,8192]{1,0:T(2,128)S(1)} %get-tuple-element.72), channel_id=1, source_target_pairs={{96,0},{97,1},{98,2},{99,3},{100,4},{101,5},{102,6},{103,7},{104,8... | collective-permute-start | bytes 196616 | tf_op jit(solution)/shard_map/ppermute | solution.py:39
  14.9 26.2 %collective-permute-start.3 = (s32[2,8192]{1,0:T(2,128)S(1)}, s32[2,8192]{1,0:T(2,128)S(1)}, u32[]{:S(2)}, u32[]{:S(2)}) collective-permute-start(s32[2,8192]{1,0:T(2,128)S(1)} %get-tuple-element.72), channel_id=1, source_target_pairs={{64,0},{65,1},{66,2},{67,3},{68,4},{69,5},{70,6},{71,7},{72,8},{73... | collective-permute-start | bytes 196616 | tf_op jit(solution)/shard_map/ppermute | solution.py:39
  18.5 3.4 %copy-start.5 = (f32[8,512,512]{2,1,0:T(8,128)S(1)}, f32[8,512,512]{2,1,0:T(8,128)}, u32[]{:S(2)}) copy-start(f32[8,512,512]{2,1,0:T(8,128)} %k_ref.1) | copy-start | bytes 25165828
  24.7 2.0 %copy-start.1 = (bf16[8,512,512]{2,1,0:T(8,128)(2,1)}, bf16[8,512,512]{2,1,0:T(8,128)(2,1)S(1)}, u32[]{:S(2)}) copy-start(bf16[8,512,512]{2,1,0:T(8,128)(2,1)S(1)} %get-tuple-element.59.kh_ref.refs_3_) | copy-start | bytes 12582916
  26.7 2.0 %copy-start.3 = (bf16[8,512,512]{2,1,0:T(8,128)(2,1)}, bf16[8,512,512]{2,1,0:T(8,128)(2,1)S(1)}, u32[]{:S(2)}) copy-start(bf16[8,512,512]{2,1,0:T(8,128)(2,1)S(1)} %get-tuple-element.60.kl_ref.refs_4_) | copy-start | bytes 12582916
  42.2 6.8 %collective-permute-start.2 = (f32[128,512]{1,0:T(8,128)S(1)}, f32[128,512]{1,0:T(8,128)S(1)}, u32[]{:S(2)}, u32[]{:S(2)}) collective-permute-start(f32[128,512]{1,0:T(8,128)S(1)} %fusion), channel_id=1, source_target_pairs={{12,0},{13,1},{14,2},{15,3},{0,4},{1,5},{2,6},{3,7},{4,8},{5,9},{6... | collective-permute-start | bytes 786440 | tf_op jit(solution)/shard_map/ppermute | solution.py:39
  42.8 9.4 %collective-permute-start.1 = (f32[128,512]{1,0:T(8,128)S(1)}, f32[128,512]{1,0:T(8,128)S(1)}, u32[]{:S(2)}, u32[]{:S(2)}) collective-permute-start(f32[128,512]{1,0:T(8,128)S(1)} %fusion), channel_id=1, source_target_pairs={{8,0},{9,1},{10,2},{11,3},{12,4},{13,5},{14,6},{15,7},{0,8},{1,9},... | collective-permute-start | bytes 786440 | tf_op jit(solution)/shard_map/ppermute | solution.py:39
  45.3 7.1 %collective-permute-start = (f32[128,512]{1,0:T(8,128)S(1)}, f32[128,512]{1,0:T(8,128)S(1)}, u32[]{:S(2)}, u32[]{:S(2)}) collective-permute-start(f32[128,512]{1,0:T(8,128)S(1)} %fusion), channel_id=1, source_target_pairs={{4,0},{5,1},{6,2},{7,3},{8,4},{9,5},{10,6},{11,7},{12,8},{13,9},{1... | collective-permute-start | bytes 786440 | tf_op jit(solution)/shard_map/ppermute | solution.py:39
  52.5 16.8 %collective-permute-start.7 = (f32[512,512]{1,0:T(8,128)S(1)}, f32[512,512]{1,0:T(8,128)S(1)}, u32[]{:S(2)}, u32[]{:S(2)}) collective-permute-start(f32[512,512]{1,0:T(8,128)S(1)} %constant_dynamic-update-slice_fusion.refs_0_), channel_id=1, source_target_pairs={{3,0},{0,1},{1,2},{2,3},{7,4},{4,5},{5,6},{6,7},{11,8},{8,9},{9,10... | collective-permute-start | bytes 3145736 | tf_op jit(solution)/shard_map/ppermute | solution.py:39
  53.1 16.2 %collective-permute-start.6 = (f32[512,512]{1,0:T(8,128)S(1)}, f32[512,512]{1,0:T(8,128)S(1)}, u32[]{:S(2)}, u32[]{:S(2)}) collective-permute-start(f32[512,512]{1,0:T(8,128)S(1)} %constant_dynamic-update-slice_fusion.refs_0_), channel_id=1, source_target_pairs={{1,0},{2,1},{3,2},{0,3},{5,4},{6,5},{7,6},{4,7},{9,8},{10,9},{11,1... | collective-permute-start | bytes 3145736 | tf_op jit(solution)/shard_map/ppermute | solution.py:39
  55.3 18.3 %collective-permute-start.10 = (f32[512,512]{1,0:T(8,128)S(1)}, f32[512,512]{1,0:T(8,128)S(1)}, u32[]{:S(2)}, u32[]{:S(2)}) collective-permute-start(f32[512,512]{1,0:T(8,128)S(1)} %constant_dynamic-update-slice_fusion.refs_0_), channel_id=1, source_target_pairs={{16,0},{17,1},{18,2},{19,3},{20,4},{21,5},{22,6},{23,7},{24,8},{25... | collective-permute-start | bytes 3145736 | tf_op jit(solution)/shard_map/ppermute | solution.py:39
  69.3 4.2 %collective-permute-start.11 = (f32[512,512]{1,0:T(8,128)S(1)}, f32[512,512]{1,0:T(8,128)S(1)}, u32[]{:S(2)}, u32[]{:S(2)}) collective-permute-start(f32[512,512]{1,0:T(8,128)S(1)} %collective-permute-done.6.refs_2_), channel_id=1, source_target_pairs={{16,0},{17,1},{18,2},{19,3},{20,4},{21,5},{22,6},{23,7},{24,8},{25... | collective-permute-start | bytes 3145736 | tf_op jit(solution)/shard_map/ppermute | solution.py:39
  70.7 3.8 %collective-permute-start.12 = (f32[512,512]{1,0:T(8,128)S(1)}, f32[512,512]{1,0:T(8,128)S(1)}, u32[]{:S(2)}, u32[]{:S(2)}) collective-permute-start(f32[512,512]{1,0:T(8,128)S(1)} %collective-permute-done.7.refs_4_), channel_id=1, source_target_pairs={{16,0},{17,1},{18,2},{19,3},{20,4},{21,5},{22,6},{23,7},{24,8},{25... | collective-permute-start | bytes 3145736 | tf_op jit(solution)/shard_map/ppermute | solution.py:39
  70.8 9.6 %collective-permute-start.9 = (f32[256,512]{1,0:T(8,128)S(1)}, f32[256,512]{1,0:T(8,128)S(1)}, u32[]{:S(2)}, u32[]{:S(2)}) collective-permute-start(f32[256,512]{1,0:T(8,128)S(1)} %slice.15), channel_id=1, source_target_pairs={{3,0},{0,1},{1,2},{2,3},{7,4},{4,5},{5,6},{6,7},{11,8},{8,9},{9,10... | collective-permute-start | bytes 1572872 | tf_op jit(solution)/shard_map/ppermute | solution.py:39
  72.0 8.4 %collective-permute-start.8 = (f32[256,512]{1,0:T(8,128)S(1)}, f32[256,512]{1,0:T(8,128)S(1)}, u32[]{:S(2)}, u32[]{:S(2)}) collective-permute-start(f32[256,512]{1,0:T(8,128)S(1)} %slice.14), channel_id=1, source_target_pairs={{1,0},{2,1},{3,2},{0,3},{5,4},{6,5},{7,6},{4,7},{9,8},{10,9},{11,1... | collective-permute-start | bytes 1572872 | tf_op jit(solution)/shard_map/ppermute | solution.py:39
  76.4 5.4 %copy-start.2 = (bf16[8,512,512]{2,1,0:T(8,128)(2,1)S(1)}, bf16[8,512,512]{2,1,0:T(8,128)(2,1)}, u32[]{:S(2)}) copy-start(bf16[8,512,512]{2,1,0:T(8,128)(2,1)} %copy-done.1) | copy-start | bytes 12582916
  76.4 5.4 %copy-start.4 = (bf16[8,512,512]{2,1,0:T(8,128)(2,1)S(1)}, bf16[8,512,512]{2,1,0:T(8,128)(2,1)}, u32[]{:S(2)}) copy-start(bf16[8,512,512]{2,1,0:T(8,128)(2,1)} %copy-done.3) | copy-start | bytes 12582916
  80.4 5.0 %collective-permute-start.13 = (f32[256,512]{1,0:T(8,128)S(1)}, f32[256,512]{1,0:T(8,128)S(1)}, u32[]{:S(2)}, u32[]{:S(2)}) collective-permute-start(f32[256,512]{1,0:T(8,128)S(1)} %collective-permute-done.8.refs_0_), channel_id=1, source_target_pairs={{16,0},{17,1},{18,2},{19,3},{20,4},{21,5},{22,6},{23,7},{24,8},{25... | collective-permute-start | bytes 1572872 | tf_op jit(solution)/shard_map/ppermute | solution.py:39
  81.8 3.7 %collective-permute-start.14 = (f32[256,512]{1,0:T(8,128)S(1)}, f32[256,512]{1,0:T(8,128)S(1)}, u32[]{:S(2)}, u32[]{:S(2)}) collective-permute-start(f32[256,512]{1,0:T(8,128)S(1)} %collective-permute-done.9.refs_1_), channel_id=1, source_target_pairs={{16,0},{17,1},{18,2},{19,3},{20,4},{21,5},{22,6},{23,7},{24,8},{25... | collective-permute-start | bytes 1572872 | tf_op jit(solution)/shard_map/ppermute | solution.py:39
  89.3 12.6 %collective-permute-start.15 = (f32[128,512]{1,0:T(8,128)S(1)}, f32[128,512]{1,0:T(8,128)S(1)}, u32[]{:S(2)}, u32[]{:S(2)}) collective-permute-start(f32[128,512]{1,0:T(8,128)S(1)} %finish.4), channel_id=1, source_target_pairs={{64,0},{65,1},{66,2},{67,3},{68,4},{69,5},{70,6},{71,7},{72,8},{73... | collective-permute-start | bytes 786440 | tf_op jit(solution)/shard_map/ppermute | solution.py:39
  96.1 8.3 %collective-permute-start.16 = (f32[128,512]{1,0:T(8,128)S(1)}, f32[128,512]{1,0:T(8,128)S(1)}, u32[]{:S(2)}, u32[]{:S(2)}) collective-permute-start(f32[128,512]{1,0:T(8,128)S(1)} %get-tuple-element.61), channel_id=1, source_target_pairs={{96,0},{97,1},{98,2},{99,3},{100,4},{101,5},{102,6},{103,7},{104,8... | collective-permute-start | bytes 786440 | tf_op jit(solution)/shard_map/ppermute | solution.py:39
  96.7 7.7 %collective-permute-start.17 = (f32[128,512]{1,0:T(8,128)S(1)}, f32[128,512]{1,0:T(8,128)S(1)}, u32[]{:S(2)}, u32[]{:S(2)}) collective-permute-start(f32[128,512]{1,0:T(8,128)S(1)} %get-tuple-element.62), channel_id=1, source_target_pairs={{32,0},{33,1},{34,2},{35,3},{36,4},{37,5},{38,6},{39,7},{40,8},{41... | collective-permute-start | bytes 786440 | tf_op jit(solution)/shard_map/ppermute | solution.py:39
